TPU v7x, 128 devices: a whole 4x4x4 slice. The times are simulated.
128 devices in a mesh: grp: 4 (over z_hi, core), dev: 32 (over z_lo, y, x).
Axes of the slice: x: 4, y: 4, z: 4 (z_hi: 2, z_lo: 2; z = z_hi * 2 + z_lo), core: 2. Of those that a mesh axis runs over, the one named last changes fastest.
Arguments:
- initial_state: float32 [5, 256, 32, 128], P(None, 'dev', 'grp'), may hold values from -6 to 6
- viscosity: float32 [256, 32, 128], P('dev', 'grp'), may hold values from 0.02 to 0.12
- speeds: float32 [5, 3], replicated, may hold values from -0.3 to 0.3
- energy_weights: float32 [5], replicated, may hold values from 0.5 to 2
- block_index: int32 [2, 6], replicated, may hold values from 0 to 7
- block_offset: int32 [2], replicated, may hold values from 0 to 7
Outputs:
- final_state: float32 [5, 256, 32, 128], P(None, 'dev', 'grp')
- modes: bfloat16 [64, 2, 2, 5, 256, 32, 128], P('dev', None, None, None, None, 'grp')
- leading_energy: float32 [64], P('dev')
All inputs are finite; a program needn't handle non-finite values.
Results may differ from a plain program's by a relative error of at most 0.0075.
Values may be sent and summed in bfloat16 or wider, within the bound.
No kernel may reach another device: no remote copies, remote signals or barrier semaphores. Data moves between devices by JAX's collectives and lax.ppermute only.
A program may use at most 256 MiB of HBM per device.

v0:
```python
import functools
import math

import jax
import jax.numpy as jnp
from jax import lax
from jax.sharding import Mesh
from jax.sharding import PartitionSpec as P

FREQS = 64
BLOCKS = 2
SNAPS = 8
GRP_DEV = ("grp_0", "grp_1", "dev_0", "dev_1", "dev_2")
GRP = ("grp_0", "grp_1")
DEV = ("dev_0", "dev_1", "dev_2")


def with_halo(x, sides, width):
    edges = {}
    for axis, dim in sides:
        size, length = (lax.axis_size(axis), x.shape[dim])
        up = [(i, (i + 1) % size) for i in range(size - 1)]
        last = lax.slice_in_dim(x, length - width, length, axis=dim)
        first = lax.slice_in_dim(x, 0, width, axis=dim)
        edges[dim] = (
            lax.ppermute(last, axis, up),
            lax.ppermute(first, axis, [(b, a) for a, b in up]),
        )
    done = []
    for _, dim in sides:
        low, high = edges[dim]
        around = [(width, width) if d in done else (0, 0) for d in range(x.ndim)]
        x = jnp.concatenate([jnp.pad(low, around), x, jnp.pad(high, around)], axis=dim)
        done.append(dim)
    return x


def over_axes(x, axes):
    return functools.reduce(lax.psum, axes, x)


def flux_update(padded, visc_pad, speeds):
    center = padded[:, 1:-1, 1:-1, :]
    visc_mid = visc_pad[1:-1, 1:-1, :]
    pairs = [
        (
            padded[:, 2:, 1:-1, :],
            padded[:, :-2, 1:-1, :],
            visc_pad[2:, 1:-1, :],
            visc_pad[:-2, 1:-1, :],
        ),
        (
            padded[:, 1:-1, 2:, :],
            padded[:, 1:-1, :-2, :],
            visc_pad[1:-1, 2:, :],
            visc_pad[1:-1, :-2, :],
        ),
        (
            jnp.roll(center, -1, axis=3),
            jnp.roll(center, 1, axis=3),
            jnp.roll(visc_mid, -1, axis=2),
            jnp.roll(visc_mid, 1, axis=2),
        ),
    ]
    result = center
    for column, (forward, backward, visc_fwd, visc_back) in enumerate(pairs):
        rate = speeds[:, column].reshape(-1, 1, 1, 1)
        face_fwd = (visc_mid + visc_fwd) * 0.5
        face_back = (visc_mid + visc_back) * 0.5
        result = (
            result
            - 0.5 * rate * (forward - backward)
            + face_fwd * (forward - center)
            - face_back * (center - backward)
        )
    return result


def block_coefficients(block_index, block_offset, freqs_count, snap_count):
    frequency = jnp.arange(freqs_count)
    distance = block_index - block_offset[:, None]
    angles = (frequency[:, None, None] * distance[None]).astype(jnp.float32) * (
        math.pi / freqs_count
    )
    length = block_index.shape[1]
    window = jnp.sin(math.pi * (jnp.arange(length).astype(jnp.float32) + 0.5) / length) ** 2
    onehot = (block_index[:, :, None] == jnp.arange(snap_count)[None, None, :]).astype(jnp.float32)
    cosine_part = jnp.einsum(
        "fbj,bjt->fbt", window * jnp.cos(angles), onehot, precision=lax.Precision.HIGHEST
    )
    sine_part = -jnp.einsum(
        "fbj,bjt->fbt", window * jnp.sin(angles), onehot, precision=lax.Precision.HIGHEST
    )
    return jnp.stack([cosine_part, sine_part], axis=2)


def gram_terms(spec, energy_weights):
    shaped = spec.astype(jnp.float32).reshape(spec.shape[:4] + (-1,))
    real_zero, imag_zero = (shaped[:, 0, 0], shaped[:, 0, 1])
    real_one, imag_one = (shaped[:, 1, 0], shaped[:, 1, 1])
    high = lax.Precision.HIGHEST
    diag_zero = jnp.einsum(
        "fvc,v->f", real_zero * real_zero + imag_zero * imag_zero, energy_weights, precision=high
    )
    diag_one = jnp.einsum(
        "fvc,v->f", real_one * real_one + imag_one * imag_one, energy_weights, precision=high
    )
    cross_real = jnp.einsum(
        "fvc,v->f", real_zero * real_one + imag_zero * imag_one, energy_weights, precision=high
    )
    cross_imag = jnp.einsum(
        "fvc,v->f", real_zero * imag_one - imag_zero * real_one, energy_weights, precision=high
    )
    return jnp.stack([diag_zero, diag_one, cross_real, cross_imag], axis=1)


def leading(gram_sums):
    diag_zero, diag_one = (gram_sums[:, 0], gram_sums[:, 1])
    cross_real, cross_imag = (gram_sums[:, 2], gram_sums[:, 3])
    middle = (diag_zero + diag_one) * 0.5
    radius = jnp.sqrt(((diag_zero - diag_one) * 0.5) ** 2 + cross_real**2 + cross_imag**2)
    top_energy = middle + radius
    low_energy = middle - radius
    total_energy = diag_zero + diag_one + 1e-06
    kernel = (
        (diag_zero - low_energy) / total_energy,
        (diag_one - low_energy) / total_energy,
        cross_real / total_energy,
        cross_imag / total_energy,
    )
    return (top_energy, kernel)


def widen(vector, ndim):
    return vector.reshape(vector.shape + (1,) * (ndim - 1))


def project(spec, kernel):
    shaped = spec.astype(jnp.float32)
    real_zero, imag_zero = (shaped[:, 0, 0], shaped[:, 0, 1])
    real_one, imag_one = (shaped[:, 1, 0], shaped[:, 1, 1])
    ndim = real_zero.ndim
    keep_zero, keep_one, cross_real, cross_imag = [widen(item, ndim) for item in kernel]
    zero_real = real_zero * keep_zero + real_one * cross_real + imag_one * cross_imag
    zero_imag = imag_zero * keep_zero + imag_one * cross_real - real_one * cross_imag
    one_real = real_zero * cross_real - imag_zero * cross_imag + real_one * keep_one
    one_imag = imag_zero * cross_real + real_zero * cross_imag + imag_one * keep_one
    block_zero = jnp.stack([zero_real, zero_imag], axis=1)
    block_one = jnp.stack([one_real, one_imag], axis=1)
    return jnp.stack([block_zero, block_one], axis=1).astype(jnp.bfloat16)


def body(initial_state, viscosity, speeds, energy_weights, block_index, block_offset):
    visc_pad = with_halo(viscosity, ((GRP, 1), (DEV, 0)), 1)
    fields = initial_state
    snapshots = []
    for number in range(SNAPS):
        padded = with_halo(fields, ((GRP, 2), (DEV, 1)), 1)
        fields = flux_update(padded, visc_pad, speeds)
        snapshots.append(fields.astype(jnp.bfloat16))
    stacked = jnp.stack(snapshots)
    coeffs = block_coefficients(block_index, block_offset, FREQS, SNAPS)
    dev_count = lax.axis_size(DEV)
    own_count = FREQS // dev_count
    own_start = lax.axis_index(DEV) * own_count
    cells_total = (
        fields.shape[1] * dev_count * fields.shape[2] * lax.axis_size(GRP) * fields.shape[3]
    )
    own_coef = lax.dynamic_slice_in_dim(coeffs, own_start, own_count, 0).reshape(-1, SNAPS)
    section = lax.all_gather(stacked, DEV, axis=2, tiled=True)
    flattened = section.reshape(SNAPS, -1).astype(jnp.float32)
    product = jnp.dot(own_coef, flattened, precision=lax.Precision.HIGHEST)
    owned_spec = product.reshape((own_count, BLOCKS, 2) + section.shape[1:]).astype(jnp.bfloat16)
    flattened = stacked.reshape(SNAPS, -1).astype(jnp.float32)
    product = jnp.dot(coeffs.reshape(-1, SNAPS), flattened, precision=lax.Precision.HIGHEST)
    whole_spec = product.reshape((FREQS, BLOCKS, 2) + fields.shape).astype(jnp.bfloat16)
    every_sum = over_axes(gram_terms(whole_spec, energy_weights), GRP_DEV) / cells_total
    gram_sums = lax.dynamic_slice_in_dim(every_sum, own_start, own_count, 0)
    top_energy, kernel = leading(gram_sums)
    modes = project(owned_spec, kernel)
    return (fields, modes, top_energy)


def solution(mesh):
    torus = Mesh(mesh.devices.reshape(2, 2, 2, 4, 4), ("grp_0", "grp_1", "dev_0", "dev_1", "dev_2"))
    in_specs = (P(None, DEV, GRP, None), P(DEV, GRP, None), P(), P(), P(), P())
    out_specs = (P(None, DEV, GRP, None), P(DEV, None, None, None, None, GRP, None), P(DEV))
    return jax.shard_map(body, mesh=torus, in_specs=in_specs, out_specs=out_specs, check_vma=False)
```

profile of v0, /device:TPU:1, one launch (start us, length us, event | category | flops | bytes accessed | tf_op | source)
XLA Modules:
  0.0 612.2 jit_solution(15523027405224646616)
XLA Ops:
  8.1 6.9 %collective-permute-start.4 = (f32[8,1,128]{2,1,0:T(1,128)S(1)}, f32[8,1,128]{2,1,0:T(1,128)S(1)}, u32[]{:S(2)}, u32[]{:S(2)}) collective-permute-start(f32[8,1,128]{2,1,0:T(1,128)S(1)} %get-tuple-element.124), channel_id=1, source_target_pairs={{0,32},{32,64},{64,96},{1,33},{33,65},{65,97},{2,34},{34,66},{66,9... | collective-permute-start | bytes 12296 | tf_op jit(solution)/shard_map/ppermute | solution.py:26
  18.9 4.0 collective-permute-start.7
  23.9 5.7 collective-permute-start
  38.4 4.0 collective-permute-start.3
  46.7 4.0 collective-permute-start.11
  50.8 6.9 %collective-permute-start.8 = (f32[5,8,1,128]{3,2,1,0:T(1,128)S(1)}, f32[5,8,1,128]{3,2,1,0:T(1,128)S(1)}, u32[]{:S(2)}, u32[]{:S(2)}) collective-permute-start(f32[5,8,1,128]{3,2,1,0:T(1,128)S(1)} %get-tuple-element.102), channel_id=1, source_target_pairs={{0,32},{32,64},{64,96},{1,33},{33,65},{65,97},{2,34},{34,66},{66,9... | collective-permute-start | bytes 61448 | tf_op jit(solution)/shard_map/ppermute | solution.py:26
  59.7 4.5 collective-permute-done.9
  70.4 4.3 collective-permute-start.15
  76.2 5.5 collective-permute-start.16
  84.9 6.3 %collective-permute-start.19 = (f32[5,1,8,128]{3,2,1,0:T(8,128)S(1)}, f32[5,1,8,128]{3,2,1,0:T(8,128)S(1)}, u32[]{:S(2)}, u32[]{:S(2)}) collective-permute-start(f32[5,1,8,128]{3,2,1,0:T(8,128)S(1)} %get-tuple-element.84), channel_id=1, source_target_pairs={{0,1},{1,2},{2,3},{3,4},{4,5},{5,6},{6,7},{7,8},{8,9},{9,10},{10,1... | collective-permute-start | bytes 61448 | tf_op jit(solution)/shard_map/ppermute | solution.py:26
  92.7 6.0 collective-permute-start.20
  101.9 6.7 %collective-permute-start.23 = (f32[5,1,8,128]{3,2,1,0:T(8,128)S(1)}, f32[5,1,8,128]{3,2,1,0:T(8,128)S(1)}, u32[]{:S(2)}, u32[]{:S(2)}) collective-permute-start(f32[5,1,8,128]{3,2,1,0:T(8,128)S(1)} %get-tuple-element.76), channel_id=1, source_target_pairs={{0,1},{1,2},{2,3},{3,4},{4,5},{5,6},{6,7},{7,8},{8,9},{9,10},{10,1... | collective-permute-start | bytes 61448 | tf_op jit(solution)/shard_map/ppermute | solution.py:26
  110.1 6.0 collective-permute-start.24
  119.3 6.4 %collective-permute-start.27 = (f32[5,1,8,128]{3,2,1,0:T(8,128)S(1)}, f32[5,1,8,128]{3,2,1,0:T(8,128)S(1)}, u32[]{:S(2)}, u32[]{:S(2)}) collective-permute-start(f32[5,1,8,128]{3,2,1,0:T(8,128)S(1)} %get-tuple-element.68), channel_id=1, source_target_pairs={{0,1},{1,2},{2,3},{3,4},{4,5},{5,6},{6,7},{7,8},{8,9},{9,10},{10,1... | collective-permute-start | bytes 61448 | tf_op jit(solution)/shard_map/ppermute | solution.py:26
  127.1 6.0 collective-permute-start.28
  136.4 6.7 %collective-permute-start.31 = (f32[5,1,8,128]{3,2,1,0:T(8,128)S(1)}, f32[5,1,8,128]{3,2,1,0:T(8,128)S(1)}, u32[]{:S(2)}, u32[]{:S(2)}) collective-permute-start(f32[5,1,8,128]{3,2,1,0:T(8,128)S(1)} %get-tuple-element.60), channel_id=1, source_target_pairs={{0,1},{1,2},{2,3},{3,4},{4,5},{5,6},{6,7},{7,8},{8,9},{9,10},{10,1... | collective-permute-start | bytes 61448 | tf_op jit(solution)/shard_map/ppermute | solution.py:26
  144.5 6.0 collective-permute-start.32
  153.7 6.8 %collective-permute-start.35 = (f32[5,1,8,128]{3,2,1,0:T(8,128)S(1)}, f32[5,1,8,128]{3,2,1,0:T(8,128)S(1)}, u32[]{:S(2)}, u32[]{:S(2)}) collective-permute-start(f32[5,1,8,128]{3,2,1,0:T(8,128)S(1)} %get-tuple-element.52), channel_id=1, source_target_pairs={{0,1},{1,2},{2,3},{3,4},{4,5},{5,6},{6,7},{7,8},{8,9},{9,10},{10,1... | collective-permute-start | bytes 61448 | tf_op jit(solution)/shard_map/ppermute | solution.py:26
  166.3 20.7 %convert_convert_fusion = f32[64,2,2,5,8,8,128]{6,0,5,4,3,2,1:T(8,128)} fusion(bf16[5,8,8,128,8,1,1]{3,4,2,1,0,6,5:T(8,128)(2,1)S(1)} %bitcast.164, f32[64,2,1,8]{0,3,1,2:T(8,128)S(1)} %fusion.1, f32[64,2,1,8]{0,3,1,2:T(8,128)S(1)} %convolution_bitcast_fusion), kind=kOutput, calls=%fused_computation.4 | convolution fusion | flops 1027606528 | bytes 42606592 | tf_op jit(solution)/shard_map/dot_general | solution.py:175
  187.0 38.9 %copy.25 = f32[64,2,2,5,8,8,128]{6,5,4,0,3,2,1:T(8,128)} copy(f32[64,2,2,5,8,8,128]{6,0,5,4,3,2,1:T(8,128)} %convert_convert_fusion) | data formatting | bytes 83886080 | tf_op jit(solution)/shard_map/reshape | solution.py:98
  225.9 44.9 %reshape.332 = f32[64,2,2,5,8192]{4,0,3,2,1:T(8,128)} reshape(f32[64,2,2,5,8,8,128]{6,5,4,0,3,2,1:T(8,128)} %copy.25) | data formatting | bytes 83886080 | tf_op jit(solution)/shard_map/reshape | solution.py:98
  270.8 15.3 %add_reduce_fusion.2 = (f32[64,5]{0,1:T(8,128)S(1)}, f32[64,5]{0,1:T(8,128)S(1)}, f32[64,5]{0,1:T(8,128)S(1)}, f32[64,5]{0,1:T(8,128)S(1)}) fusion(f32[64,2,2,5,8192]{4,0,3,2,1:T(8,128)} %reshape.332), kind=kLoop, calls=%fused_computation.14 | loop fusion | flops 41941760 | bytes 41948160 | tf_op jit(solution)/shard_map/fvc,v->f/reduce_sum | solution.py:102
  286.6 6.1 psum.35
  296.6 130.4 %psum.37 = f32[64,4]{0,1:T(4,128)S(1)} all-reduce(f32[64,4]{0,1:T(4,128)S(1)} %psum.36), channel_id=1, replica_groups=mesh['grp_0'=2,'grp_1'=2,'dev_0'=2,'dev_1'=4,'dev_2'=4] {'dev_0'}, use_global_device_ids=true, to_apply=%region_6.7 | all-reduce | flops 256 | bytes 2048 | tf_op jit(solution)/shard_map/psum | solution.py:39
  427.0 6.1 psum.38
  433.0 7.5 %psum.39 = f32[64,4]{0,1:T(4,128)S(1)} all-reduce(f32[64,4]{0,1:T(4,128)S(1)} %psum.38), channel_id=1, replica_groups=mesh['grp_0'=2,'grp_1'=2,'dev_0'=2,'dev_1'=4,'dev_2'=4] {'dev_2'}, use_global_device_ids=true, to_apply=%region_8.9 | all-reduce | flops 256 | bytes 2048 | tf_op jit(solution)/shard_map/psum | solution.py:39
  441.2 22.7 %copy.44 = bf16[1,8,10240,128]{3,1,2,0:T(8,128)(2,1)} copy(bf16[1,8,10240,128]{3,2,1,0:T(8,128)(2,1)} %bitcast.162) | data formatting | bytes 41943040
  463.9 56.5 %fusion = f32[2,2,2,5,256,8,128]{6,2,5,4,3,1,0:T(2,128)} fusion(f32[2,2,2,8,1,1,1]{3,2,6,5,4,1,0:T(2,128)S(1)} %copy.29, bf16[5,256,8,128,8,1,1]{3,4,2,1,0,6,5:T(8,128)(2,1)} %bitcast.163), kind=kOutput, calls=%fused_computation.1 | convolution fusion | flops 1027604480 | bytes 62914816 | tf_op jit(solution)/shard_map/dot_general | solution.py:172
  520.3 45.3 %fusion.164 = (f32[2,1,1,5,256,8,128]{6,2,5,4,3,1,0:T(1,128)}, f32[2,1,1,5,256,8,128]{6,2,5,4,3,1,0:T(1,128)}, f32[2,1,1,5,256,8,128]{6,2,5,4,3,1,0:T(1,128)}, f32[2,1,1,5,256,8,128]{6,2,5,4,3,1,0:T(1,128)}) fusion(f32[2,2,2,5,256,8,128]{6,2,5,4,3,1,0:T(2,128)} %fusion), kind=kLoop, calls=%fused_computation.301 | loop fusion | bytes 83886080 | tf_op jit(solution)/shard_map/slice | solution.py:141
  565.7 21.9 %add_convert_fusion.2 = (bf16[2,1,5,256,8,128]{5,4,3,2,0,1:T(8,128)(2,1)}, bf16[2,1,5,256,8,128]{5,4,3,2,0,1:T(8,128)(2,1)}, bf16[2,1,5,256,8,128]{5,4,3,2,0,1:T(8,128)(2,1)}, bf16[2,1,5,256,8,128]{5,4,3,2,0,1:T(8,128)(2,1)}) fusion(f32[2,1,5,256,8,128]{5,4,3,2,0,1:T(8,128)} %bitcast.161, f32[2,1,5,256,8,128]{5,4,3,2,0,1:T(8,128)} %bitcast.158, ...), kind=kLoop, calls=%fused_computation.10 | loop fusion | flops 62914560 | bytes 62914592 | tf_op jit(solution)/shard_map/convert.7
  587.6 8.1 %maximum_bitcast_fusion = (bf16[2,1,2,5,256,8,128]{6,5,4,3,0,2,1:T(8,128)(2,1)S(1)}, bf16[2,1,2,5,256,8,128]{6,5,4,3,0,2,1:T(8,128)(2,1)S(1)}) fusion(bf16[2,1,5,256,8,128]{5,4,3,2,0,1:T(8,128)(2,1)} %get-tuple-element.48, bf16[2,1,5,256,8,128]{5,4,3,2,0,1:T(8,128)(2,1)} %get-tuple-element.47, bf16[2,1,5,256,8,128]{5,4,3,2,0,1:T(8,128)(2,1)} %get-tuple-element.50, ...), kind=kLoop, calls=%fused_computation.5 | loop fusion | flops 10485760 | bytes 41943040 | tf_op jit(solution)/shard_map/stack | solution.py:150
  597.8 7.5 %copy.28 = bf16[2,2,2,5,256,8,128]{6,5,4,3,2,1,0:T(8,128)(2,1)} copy(bf16[2,2,2,5,256,8,128]{6,5,4,3,0,2,1:T(8,128)(2,1)S(1)} %pad_maximum_fusion) | data formatting | bytes 41943040
  (139 shorter events, 62.8 us)
Async XLA Ops:
  7.2 434.0 %all-gather.2.cloned.1.call-start = ((), (), s32[]{:S(2)}) async-start(), calls=%async_computation | async-start | bytes 21626880 | tf_op jit(solution)/shard_map/all_gather | solution.py:170
  8.1 27.1 %collective-permute-start.4 = (f32[8,1,128]{2,1,0:T(1,128)S(1)}, f32[8,1,128]{2,1,0:T(1,128)S(1)}, u32[]{:S(2)}, u32[]{:S(2)}) collective-permute-start(f32[8,1,128]{2,1,0:T(1,128)S(1)} %get-tuple-element.124), channel_id=1, source_target_pairs={{0,32},{32,64},{64,96},{1,33},{33,65},{65,97},{2,34},{34,66},{66,9... | collective-permute-start | bytes 12296 | tf_op jit(solution)/shard_map/ppermute | solution.py:26
  14.9 22.2 %collective-permute-start.5 = (f32[8,1,128]{2,1,0:T(1,128)S(1)}, f32[8,1,128]{2,1,0:T(1,128)S(1)}, u32[]{:S(2)}, u32[]{:S(2)}) collective-permute-start(f32[8,1,128]{2,1,0:T(1,128)S(1)} %get-tuple-element.123), channel_id=1, source_target_pairs={{32,0},{64,32},{96,64},{33,1},{65,33},{97,65},{34,2},{66,34},{98,6... | collective-permute-start | bytes 12296 | tf_op jit(solution)/shard_map/ppermute | solution.py:27
  17.6 20.9 %collective-permute-start.6 = (f32[1,8,128]{2,1,0:T(8,128)S(1)}, f32[1,8,128]{2,1,0:T(8,128)S(1)}, u32[]{:S(2)}, u32[]{:S(2)}) collective-permute-start(f32[1,8,128]{2,1,0:T(8,128)S(1)} %get-tuple-element.121), channel_id=1, source_target_pairs={{1,0},{2,1},{3,2},{4,3},{5,4},{6,5},{7,6},{8,7},{9,8},{10,9},{11,1... | collective-permute-start | bytes 12296 | tf_op jit(solution)/shard_map/ppermute | solution.py:27
  18.9 23.6 %collective-permute-start.7 = (f32[1,8,128]{2,1,0:T(8,128)S(1)}, f32[1,8,128]{2,1,0:T(8,128)S(1)}, u32[]{:S(2)}, u32[]{:S(2)}) collective-permute-start(f32[1,8,128]{2,1,0:T(8,128)S(1)} %get-tuple-element.122), channel_id=1, source_target_pairs={{0,1},{1,2},{2,3},{3,4},{4,5},{5,6},{6,7},{7,8},{8,9},{9,10},{10,1... | collective-permute-start | bytes 12296 | tf_op jit(solution)/shard_map/ppermute | solution.py:26
  23.9 19.6 %collective-permute-start = (f32[5,8,1,128]{3,2,1,0:T(1,128)S(1)}, f32[5,8,1,128]{3,2,1,0:T(1,128)S(1)}, u32[]{:S(2)}, u32[]{:S(2)}) collective-permute-start(f32[5,8,1,128]{3,2,1,0:T(1,128)S(1)} %get-tuple-element.110), channel_id=1, source_target_pairs={{0,32},{32,64},{64,96},{1,33},{33,65},{65,97},{2,34},{34,66},{66,9... | collective-permute-start | bytes 61448 | tf_op jit(solution)/shard_map/ppermute | solution.py:26
  35.2 8.3 %collective-permute-start.1 = (f32[5,8,1,128]{3,2,1,0:T(1,128)S(1)}, f32[5,8,1,128]{3,2,1,0:T(1,128)S(1)}, u32[]{:S(2)}, u32[]{:S(2)}) collective-permute-start(f32[5,8,1,128]{3,2,1,0:T(1,128)S(1)} %get-tuple-element.109), channel_id=1, source_target_pairs={{32,0},{64,32},{96,64},{33,1},{65,33},{97,65},{34,2},{66,34},{98,6... | collective-permute-start | bytes 61448 | tf_op jit(solution)/shard_map/ppermute | solution.py:27
  45.4 14.2 %collective-permute-start.10 = (f32[5,1,8,128]{3,2,1,0:T(8,128)S(1)}, f32[5,1,8,128]{3,2,1,0:T(8,128)S(1)}, u32[]{:S(2)}, u32[]{:S(2)}) collective-permute-start(f32[5,1,8,128]{3,2,1,0:T(8,128)S(1)} %get-tuple-element.99), channel_id=1, source_target_pairs={{1,0},{2,1},{3,2},{4,3},{5,4},{6,5},{7,6},{8,7},{9,8},{10,9},{11,1... | collective-permute-start | bytes 61448 | tf_op jit(solution)/shard_map/ppermute | solution.py:27
  46.7 13.0 %collective-permute-start.11 = (f32[5,1,8,128]{3,2,1,0:T(8,128)S(1)}, f32[5,1,8,128]{3,2,1,0:T(8,128)S(1)}, u32[]{:S(2)}, u32[]{:S(2)}) collective-permute-start(f32[5,1,8,128]{3,2,1,0:T(8,128)S(1)} %get-tuple-element.100), channel_id=1, source_target_pairs={{0,1},{1,2},{2,3},{3,4},{4,5},{5,6},{6,7},{7,8},{8,9},{9,10},{10,1... | collective-permute-start | bytes 61448 | tf_op jit(solution)/shard_map/ppermute | solution.py:26
  50.8 8.9 %collective-permute-start.8 = (f32[5,8,1,128]{3,2,1,0:T(1,128)S(1)}, f32[5,8,1,128]{3,2,1,0:T(1,128)S(1)}, u32[]{:S(2)}, u32[]{:S(2)}) collective-permute-start(f32[5,8,1,128]{3,2,1,0:T(1,128)S(1)} %get-tuple-element.102), channel_id=1, source_target_pairs={{0,32},{32,64},{64,96},{1,33},{33,65},{65,97},{2,34},{34,66},{66,9... | collective-permute-start | bytes 61448 | tf_op jit(solution)/shard_map/ppermute | solution.py:26
  64.8 10.0 %collective-permute-start.12 = (f32[5,8,1,128]{3,2,1,0:T(1,128)S(1)}, f32[5,8,1,128]{3,2,1,0:T(1,128)S(1)}, u32[]{:S(2)}, u32[]{:S(2)}) collective-permute-start(f32[5,8,1,128]{3,2,1,0:T(1,128)S(1)} %get-tuple-element.94), channel_id=1, source_target_pairs={{0,32},{32,64},{64,96},{1,33},{33,65},{65,97},{2,34},{34,66},{66,9... | collective-permute-start | bytes 61448 | tf_op jit(solution)/shard_map/ppermute | solution.py:26
  66.7 8.1 %collective-permute-start.13 = (f32[5,8,1,128]{3,2,1,0:T(1,128)S(1)}, f32[5,8,1,128]{3,2,1,0:T(1,128)S(1)}, u32[]{:S(2)}, u32[]{:S(2)}) collective-permute-start(f32[5,8,1,128]{3,2,1,0:T(1,128)S(1)} %get-tuple-element.93), channel_id=1, source_target_pairs={{32,0},{64,32},{96,64},{33,1},{65,33},{97,65},{34,2},{66,34},{98,6... | collective-permute-start | bytes 61448 | tf_op jit(solution)/shard_map/ppermute | solution.py:27
  76.2 15.2 %collective-permute-start.16 = (f32[5,8,1,128]{3,2,1,0:T(1,128)S(1)}, f32[5,8,1,128]{3,2,1,0:T(1,128)S(1)}, u32[]{:S(2)}, u32[]{:S(2)}) collective-permute-start(f32[5,8,1,128]{3,2,1,0:T(1,128)S(1)} %get-tuple-element.86), channel_id=1, source_target_pairs={{0,32},{32,64},{64,96},{1,33},{33,65},{65,97},{2,34},{34,66},{66,9... | collective-permute-start | bytes 61448 | tf_op jit(solution)/shard_map/ppermute | solution.py:26
  81.7 9.7 %collective-permute-start.17 = (f32[5,8,1,128]{3,2,1,0:T(1,128)S(1)}, f32[5,8,1,128]{3,2,1,0:T(1,128)S(1)}, u32[]{:S(2)}, u32[]{:S(2)}) collective-permute-start(f32[5,8,1,128]{3,2,1,0:T(1,128)S(1)} %get-tuple-element.85), channel_id=1, source_target_pairs={{32,0},{64,32},{96,64},{33,1},{65,33},{97,65},{34,2},{66,34},{98,6... | collective-permute-start | bytes 61448 | tf_op jit(solution)/shard_map/ppermute | solution.py:27
  83.6 7.8 %collective-permute-start.18 = (f32[5,1,8,128]{3,2,1,0:T(8,128)S(1)}, f32[5,1,8,128]{3,2,1,0:T(8,128)S(1)}, u32[]{:S(2)}, u32[]{:S(2)}) collective-permute-start(f32[5,1,8,128]{3,2,1,0:T(8,128)S(1)} %get-tuple-element.83), channel_id=1, source_target_pairs={{1,0},{2,1},{3,2},{4,3},{5,4},{6,5},{7,6},{8,7},{9,8},{10,9},{11,1... | collective-permute-start | bytes 61448 | tf_op jit(solution)/shard_map/ppermute | solution.py:27
  84.9 7.2 %collective-permute-start.19 = (f32[5,1,8,128]{3,2,1,0:T(8,128)S(1)}, f32[5,1,8,128]{3,2,1,0:T(8,128)S(1)}, u32[]{:S(2)}, u32[]{:S(2)}) collective-permute-start(f32[5,1,8,128]{3,2,1,0:T(8,128)S(1)} %get-tuple-element.84), channel_id=1, source_target_pairs={{0,1},{1,2},{2,3},{3,4},{4,5},{5,6},{6,7},{7,8},{8,9},{9,10},{10,1... | collective-permute-start | bytes 61448 | tf_op jit(solution)/shard_map/ppermute | solution.py:26
  92.7 16.0 %collective-permute-start.20 = (f32[5,8,1,128]{3,2,1,0:T(1,128)S(1)}, f32[5,8,1,128]{3,2,1,0:T(1,128)S(1)}, u32[]{:S(2)}, u32[]{:S(2)}) collective-permute-start(f32[5,8,1,128]{3,2,1,0:T(1,128)S(1)} %get-tuple-element.78), channel_id=1, source_target_pairs={{0,32},{32,64},{64,96},{1,33},{33,65},{65,97},{2,34},{34,66},{66,9... | collective-permute-start | bytes 61448 | tf_op jit(solution)/shard_map/ppermute | solution.py:26
  98.7 10.0 %collective-permute-start.21 = (f32[5,8,1,128]{3,2,1,0:T(1,128)S(1)}, f32[5,8,1,128]{3,2,1,0:T(1,128)S(1)}, u32[]{:S(2)}, u32[]{:S(2)}) collective-permute-start(f32[5,8,1,128]{3,2,1,0:T(1,128)S(1)} %get-tuple-element.77), channel_id=1, source_target_pairs={{32,0},{64,32},{96,64},{33,1},{65,33},{97,65},{34,2},{66,34},{98,6... | collective-permute-start | bytes 61448 | tf_op jit(solution)/shard_map/ppermute | solution.py:27
  100.6 8.1 %collective-permute-start.22 = (f32[5,1,8,128]{3,2,1,0:T(8,128)S(1)}, f32[5,1,8,128]{3,2,1,0:T(8,128)S(1)}, u32[]{:S(2)}, u32[]{:S(2)}) collective-permute-start(f32[5,1,8,128]{3,2,1,0:T(8,128)S(1)} %get-tuple-element.75), channel_id=1, source_target_pairs={{1,0},{2,1},{3,2},{4,3},{5,4},{6,5},{7,6},{8,7},{9,8},{10,9},{11,1... | collective-permute-start | bytes 61448 | tf_op jit(solution)/shard_map/ppermute | solution.py:27
  101.9 7.6 %collective-permute-start.23 = (f32[5,1,8,128]{3,2,1,0:T(8,128)S(1)}, f32[5,1,8,128]{3,2,1,0:T(8,128)S(1)}, u32[]{:S(2)}, u32[]{:S(2)}) collective-permute-start(f32[5,1,8,128]{3,2,1,0:T(8,128)S(1)} %get-tuple-element.76), channel_id=1, source_target_pairs={{0,1},{1,2},{2,3},{3,4},{4,5},{5,6},{6,7},{7,8},{8,9},{9,10},{10,1... | collective-permute-start | bytes 61448 | tf_op jit(solution)/shard_map/ppermute | solution.py:26
  110.1 15.7 %collective-permute-start.24 = (f32[5,8,1,128]{3,2,1,0:T(1,128)S(1)}, f32[5,8,1,128]{3,2,1,0:T(1,128)S(1)}, u32[]{:S(2)}, u32[]{:S(2)}) collective-permute-start(f32[5,8,1,128]{3,2,1,0:T(1,128)S(1)} %get-tuple-element.70), channel_id=1, source_target_pairs={{0,32},{32,64},{64,96},{1,33},{33,65},{65,97},{2,34},{34,66},{66,9... | collective-permute-start | bytes 61448 | tf_op jit(solution)/shard_map/ppermute | solution.py:26
  116.1 9.7 %collective-permute-start.25 = (f32[5,8,1,128]{3,2,1,0:T(1,128)S(1)}, f32[5,8,1,128]{3,2,1,0:T(1,128)S(1)}, u32[]{:S(2)}, u32[]{:S(2)}) collective-permute-start(f32[5,8,1,128]{3,2,1,0:T(1,128)S(1)} %get-tuple-element.69), channel_id=1, source_target_pairs={{32,0},{64,32},{96,64},{33,1},{65,33},{97,65},{34,2},{66,34},{98,6... | collective-permute-start | bytes 61448 | tf_op jit(solution)/shard_map/ppermute | solution.py:27
  118.0 7.8 %collective-permute-start.26 = (f32[5,1,8,128]{3,2,1,0:T(8,128)S(1)}, f32[5,1,8,128]{3,2,1,0:T(8,128)S(1)}, u32[]{:S(2)}, u32[]{:S(2)}) collective-permute-start(f32[5,1,8,128]{3,2,1,0:T(8,128)S(1)} %get-tuple-element.67), channel_id=1, source_target_pairs={{1,0},{2,1},{3,2},{4,3},{5,4},{6,5},{7,6},{8,7},{9,8},{10,9},{11,1... | collective-permute-start | bytes 61448 | tf_op jit(solution)/shard_map/ppermute | solution.py:27
  119.3 7.3 %collective-permute-start.27 = (f32[5,1,8,128]{3,2,1,0:T(8,128)S(1)}, f32[5,1,8,128]{3,2,1,0:T(8,128)S(1)}, u32[]{:S(2)}, u32[]{:S(2)}) collective-permute-start(f32[5,1,8,128]{3,2,1,0:T(8,128)S(1)} %get-tuple-element.68), channel_id=1, source_target_pairs={{0,1},{1,2},{2,3},{3,4},{4,5},{5,6},{6,7},{7,8},{8,9},{9,10},{10,1... | collective-permute-start | bytes 61448 | tf_op jit(solution)/shard_map/ppermute | solution.py:26
  127.1 16.0 %collective-permute-start.28 = (f32[5,8,1,128]{3,2,1,0:T(1,128)S(1)}, f32[5,8,1,128]{3,2,1,0:T(1,128)S(1)}, u32[]{:S(2)}, u32[]{:S(2)}) collective-permute-start(f32[5,8,1,128]{3,2,1,0:T(1,128)S(1)} %get-tuple-element.62), channel_id=1, source_target_pairs={{0,32},{32,64},{64,96},{1,33},{33,65},{65,97},{2,34},{34,66},{66,9... | collective-permute-start | bytes 61448 | tf_op jit(solution)/shard_map/ppermute | solution.py:26
  133.1 10.0 %collective-permute-start.29 = (f32[5,8,1,128]{3,2,1,0:T(1,128)S(1)}, f32[5,8,1,128]{3,2,1,0:T(1,128)S(1)}, u32[]{:S(2)}, u32[]{:S(2)}) collective-permute-start(f32[5,8,1,128]{3,2,1,0:T(1,128)S(1)} %get-tuple-element.61), channel_id=1, source_target_pairs={{32,0},{64,32},{96,64},{33,1},{65,33},{97,65},{34,2},{66,34},{98,6... | collective-permute-start | bytes 61448 | tf_op jit(solution)/shard_map/ppermute | solution.py:27
  135.1 8.1 %collective-permute-start.30 = (f32[5,1,8,128]{3,2,1,0:T(8,128)S(1)}, f32[5,1,8,128]{3,2,1,0:T(8,128)S(1)}, u32[]{:S(2)}, u32[]{:S(2)}) collective-permute-start(f32[5,1,8,128]{3,2,1,0:T(8,128)S(1)} %get-tuple-element.59), channel_id=1, source_target_pairs={{1,0},{2,1},{3,2},{4,3},{5,4},{6,5},{7,6},{8,7},{9,8},{10,9},{11,1... | collective-permute-start | bytes 61448 | tf_op jit(solution)/shard_map/ppermute | solution.py:27
  136.4 7.6 %collective-permute-start.31 = (f32[5,1,8,128]{3,2,1,0:T(8,128)S(1)}, f32[5,1,8,128]{3,2,1,0:T(8,128)S(1)}, u32[]{:S(2)}, u32[]{:S(2)}) collective-permute-start(f32[5,1,8,128]{3,2,1,0:T(8,128)S(1)} %get-tuple-element.60), channel_id=1, source_target_pairs={{0,1},{1,2},{2,3},{3,4},{4,5},{5,6},{6,7},{7,8},{8,9},{9,10},{10,1... | collective-permute-start | bytes 61448 | tf_op jit(solution)/shard_map/ppermute | solution.py:26
  144.5 16.2 %collective-permute-start.32 = (f32[5,8,1,128]{3,2,1,0:T(1,128)S(1)}, f32[5,8,1,128]{3,2,1,0:T(1,128)S(1)}, u32[]{:S(2)}, u32[]{:S(2)}) collective-permute-start(f32[5,8,1,128]{3,2,1,0:T(1,128)S(1)} %get-tuple-element.54), channel_id=1, source_target_pairs={{0,32},{32,64},{64,96},{1,33},{33,65},{65,97},{2,34},{34,66},{66,9... | collective-permute-start | bytes 61448 | tf_op jit(solution)/shard_map/ppermute | solution.py:26
  150.5 10.2 %collective-permute-start.33 = (f32[5,8,1,128]{3,2,1,0:T(1,128)S(1)}, f32[5,8,1,128]{3,2,1,0:T(1,128)S(1)}, u32[]{:S(2)}, u32[]{:S(2)}) collective-permute-start(f32[5,8,1,128]{3,2,1,0:T(1,128)S(1)} %get-tuple-element.53), channel_id=1, source_target_pairs={{32,0},{64,32},{96,64},{33,1},{65,33},{97,65},{34,2},{66,34},{98,6... | collective-permute-start | bytes 61448 | tf_op jit(solution)/shard_map/ppermute | solution.py:27
  152.4 8.3 %collective-permute-start.34 = (f32[5,1,8,128]{3,2,1,0:T(8,128)S(1)}, f32[5,1,8,128]{3,2,1,0:T(8,128)S(1)}, u32[]{:S(2)}, u32[]{:S(2)}) collective-permute-start(f32[5,1,8,128]{3,2,1,0:T(8,128)S(1)} %get-tuple-element.51), channel_id=1, source_target_pairs={{1,0},{2,1},{3,2},{4,3},{5,4},{6,5},{7,6},{8,7},{9,8},{10,9},{11,1... | collective-permute-start | bytes 61448 | tf_op jit(solution)/shard_map/ppermute | solution.py:27
  153.7 7.6 %collective-permute-start.35 = (f32[5,1,8,128]{3,2,1,0:T(8,128)S(1)}, f32[5,1,8,128]{3,2,1,0:T(8,128)S(1)}, u32[]{:S(2)}, u32[]{:S(2)}) collective-permute-start(f32[5,1,8,128]{3,2,1,0:T(8,128)S(1)} %get-tuple-element.52), channel_id=1, source_target_pairs={{0,1},{1,2},{2,3},{3,4},{4,5},{5,6},{6,7},{7,8},{8,9},{9,10},{10,1... | collective-permute-start | bytes 61448 | tf_op jit(solution)/shard_map/ppermute | solution.py:26
  (10 other events, 552.3 us)
Sparse Core Ops, SparseCore 0:
  163.3 264.5 all-gather.1
where the time goes:
time: 619 us; the launch traced here: 612 us
  local copies, waits for them, and re-layouts  172 us (28%)
  blocking collectives  154 us (25%)
  starting transfers between devices  129 us (21%)
  matrix products  78.1 us (13%)
  other arithmetic  55.1 us (9%)
  between operations  14.9 us (2%)
  waiting for transfers between devices  8.97 us (1%)
    psum x5, blocking collectives, over_axes(): return functools.reduce(lax.psum, axes, x)  154 us
    ppermute x18, starting transfers between devices, with_halo(): lax.ppermute(last, axis, up)  100 us
    reshape x2, local copies, waits for them, and re-layouts, gram_terms(): shaped = spec.astype(jnp.float32).reshape(spec.shape[:4] + (-1,))  83.8 us
    dot_general x1, matrix products, body(): product = jnp.dot(own_coef, flattened, precision=lax.Precision.HIGHEST)  56.5 us
    slice x1, local copies, waits for them, and re-layouts, project(): real_one, imag_one = (shaped[:, 1, 0], shaped[:, 1, 1])  45.3 us
    unnamed x12, local copies, waits for them, and re-layouts  31.1 us
    ppermute x18, starting transfers between devices, with_halo(): lax.ppermute(first, axis, [(b, a) for a, b in up])  29.4 us
    another operation x1, other arithmetic  21.9 us
  transfers between devices with their start and end apart: 37, of which 7 were waited for; matrix products, arithmetic and copies ran while one was open for 22% of the time, Pallas kernels for 0%

commit v1 on v0

v1 whole, which is shorter than its diff:
```python
import math

import jax
import jax.numpy as jnp
from jax import lax
from jax.experimental import pallas as pl
from jax.experimental.pallas import tpu as pltpu
from jax.sharding import Mesh
from jax.sharding import PartitionSpec as P

VARS = 5
FREQS = 64
BLOCKS = 2
SNAPS = 8
GRP_DEV = ("grp_0", "grp_1", "dev_0", "dev_1", "dev_2")
GRP = ("grp_0", "grp_1")
DEV = ("dev_0", "dev_1", "dev_2")
CELLS = 256 * 32 * 128

TILES = 32
QP = (TILES + 2) * 8
FP = (TILES + 1) * 8
CP = TILES * 8
PLANES = 24
PAIRS = [(a, b) for a in range(SNAPS) for b in range(a, SNAPS)]


def block_coefficients(block_index, block_offset):
    frequency = jnp.arange(FREQS)
    distance = block_index - block_offset[:, None]
    angles = (frequency[:, None, None] * distance[None]).astype(jnp.float32) * (math.pi / FREQS)
    length = block_index.shape[1]
    window = jnp.sin(math.pi * (jnp.arange(length).astype(jnp.float32) + 0.5) / length) ** 2
    onehot = (block_index[:, :, None] == jnp.arange(SNAPS)[None, None, :]).astype(jnp.float32)
    cosine = jnp.sum((window * jnp.cos(angles))[..., None] * onehot[None], axis=2)
    sine = -jnp.sum((window * jnp.sin(angles))[..., None] * onehot[None], axis=2)
    return jnp.stack([cosine, sine], axis=2)


def mode_matrix(coef, corr):
    def form(a, b):
        return jnp.sum(a[:, :, None] * corr[None] * b[:, None, :], axis=(1, 2))

    a0, b0, a1, b1 = coef[:, 0, 0], coef[:, 0, 1], coef[:, 1, 0], coef[:, 1, 1]
    g00 = form(a0, a0) + form(b0, b0)
    g11 = form(a1, a1) + form(b1, b1)
    gre = form(a0, a1) + form(b0, b1)
    gim = form(a0, b1) - form(b0, a1)
    middle = (g00 + g11) * 0.5
    radius = jnp.sqrt(((g00 - g11) * 0.5) ** 2 + gre**2 + gim**2)
    low = middle - radius
    total = g00 + g11 + 1e-06
    k0, k1 = ((g00 - low) / total)[:, None], ((g11 - low) / total)[:, None]
    cr, ci = (gre / total)[:, None], (gim / total)[:, None]
    rows = [
        a0 * k0 + a1 * cr + b1 * ci,
        b0 * k0 + b1 * cr - a1 * ci,
        a0 * cr - b0 * ci + a1 * k1,
        b0 * cr + a0 * ci + b1 * k1,
    ]
    return middle + radius, jnp.stack(rows, axis=1)


def rows_at(start, stride=None):
    return pl.ds(start, 8) if stride is None else pl.ds(start, 8, stride=stride)


def edge_masks():
    lane = lax.broadcasted_iota(jnp.int32, (8, 128), 0)
    return lane == 0, lane == 7


def ghosts(first, last):
    is_first, is_last = edge_masks()
    left = jnp.where(is_first, 0.0, pltpu.roll(last, 1, axis=0))
    right = jnp.where(is_last, 0.0, pltpu.roll(first, 7, axis=0))
    return left, right


def evolve_kernel(
    ints, speeds, weights, nu_own, nu_par, nu_third, q_own, q_par, q_ta, q_tb,
    snaps_ref, final_ref, corr_ref, q, q_odd, nx, ny, nym, nz, diag, snap, tmp,
):
    var = pl.program_id(0)
    par_base, third_base, inner = ints[64], ints[65], ints[66]
    own_tile, own_s, own_j = ints[67], ints[68], ints[69]

    def load_section(src, table, base):
        def unpack(slot, carry):
            d = ints[table + slot]
            tmp[pl.ds(pl.multiple_of(d * 64, 64), 64), :] = src[slot].astype(jnp.float32)
            return carry

        lax.fori_loop(0, 32, unpack, 0)

        def place(z, carry):
            row = pl.multiple_of((base + z) * QP, 8)
            first = last = None
            for j in range(TILES):
                val = tmp[rows_at(j * 8 + z, 256), :]
                q[rows_at(row + (j + 1) * 8), :] = val
                first = val if j == 0 else first
                last = val
            left, right = ghosts(first, last)
            q[rows_at(row), :] = left
            q[rows_at(row + (TILES + 1) * 8), :] = right
            return carry

        lax.fori_loop(0, 8, place, 0)

    def load_all(own, par, third):
        load_section(own, 0, 8)
        load_section(par, 32, par_base)

        @pl.when(inner == 1)
        def _():
            third()

    @pl.when(var == 0)
    def _():
        @pl.when(inner == 0)
        def _():
            def clear(k, carry):
                zero = jnp.zeros((QP, 128), jnp.float32)
                q[pl.ds(pl.multiple_of((third_base + k) * QP, 8), QP), :] = zero
                q_odd[pl.ds(pl.multiple_of((third_base + k) * QP, 8), QP), :] = zero
                return carry

            lax.fori_loop(0, 8, clear, 0)

        load_all(nu_own, nu_par, lambda: load_section(nu_third, 0, third_base))

        def faces(z, carry):
            row = pl.multiple_of(z * QP, 8)
            frow = pl.multiple_of(z * FP, 8)
            crow = pl.multiple_of(z * CP, 8)
            left = q[rows_at(row), :]
            mid = q[rows_at(row + 8), :]
            face_left = (left + mid) * 0.5
            nx[rows_at(frow), :] = face_left
            for j in range(TILES):
                right = q[rows_at(row + (j + 2) * 8), :]
                above = q[rows_at(row + QP + (j + 1) * 8), :]
                below = q[rows_at(row - QP + (j + 1) * 8), :]
                face_right = (mid + right) * 0.5
                face_up = (mid + above) * 0.5
                face_down = (mid + below) * 0.5
                face_y = (mid + pltpu.roll(mid, 127, axis=1)) * 0.5
                face_ym = pltpu.roll(face_y, 1, axis=1)
                nx[rows_at(frow + (j + 1) * 8), :] = face_right
                nz[rows_at(crow + CP + j * 8), :] = face_up
                nz[rows_at(crow + j * 8), :] = face_down
                ny[rows_at(crow + j * 8), :] = face_y
                nym[rows_at(crow + j * 8), :] = face_ym
                diag[rows_at(crow + j * 8), :] = 1.0 - (
                    (face_left + face_right) + (face_up + face_down) + (face_y + face_ym)
                )
                mid, face_left = right, face_right
            return carry

        lax.fori_loop(1, PLANES - 1, faces, 0)
        corr_ref[...] = jnp.zeros_like(corr_ref)

    def third():
        @pl.when(var < 2)
        def _():
            load_section(q_ta, 0, third_base)

        @pl.when(var >= 2)
        def _():
            load_section(q_tb, 32, third_base)

    load_all(q_own, q_par, third)

    hx, hz, hy = (0.5 * speeds[var * 3 + d] for d in range(3))

    def plane(z, src, dst, keep):
        row = pl.multiple_of(z * QP, 8)
        frow = pl.multiple_of(z * FP, 8)
        crow = pl.multiple_of(z * CP, 8)
        qm = src[rows_at(row), :]
        qc = src[rows_at(row + 8), :]
        fm = nx[rows_at(frow), :]
        first = last = None
        for j in range(TILES):
            qp = src[rows_at(row + (j + 2) * 8), :]
            fp = nx[rows_at(frow + (j + 1) * 8), :]
            up = src[rows_at(row + QP + (j + 1) * 8), :]
            down = src[rows_at(row - QP + (j + 1) * 8), :]
            new = (
                diag[rows_at(crow + j * 8), :] * qc
                + ((fp - hx) * qp + (fm + hx) * qm)
                + (
                    (nz[rows_at(crow + CP + j * 8), :] - hz) * up
                    + (nz[rows_at(crow + j * 8), :] + hz) * down
                )
                + (
                    (ny[rows_at(crow + j * 8), :] - hy) * pltpu.roll(qc, 127, axis=1)
                    + (nym[rows_at(crow + j * 8), :] + hy) * pltpu.roll(qc, 1, axis=1)
                )
            )
            dst[rows_at(row + (j + 1) * 8), :] = new
            if keep is not None:
                snap[rows_at(keep + j * 8), :] = new
            first = new if j == 0 else first
            last = new
            qm, qc, fm = qc, qp, fp
        left, right = ghosts(first, last)
        dst[rows_at(row), :] = left
        dst[rows_at(row + (TILES + 1) * 8), :] = right

    def step(t, src, dst):
        low, high = ints[72 + t], ints[84 + t]
        below = 8 - low

        def halo(k, inner_carry):
            plane(jnp.where(k < below, low + k, 16 + k - below), src, dst, None)
            return inner_carry

        lax.fori_loop(0, below + high - 16, halo, 0)

        def own(z, inner_carry):
            keep = pl.multiple_of((t - 1) * (8 * CP) + (z - 8) * CP, 8)
            plane(z, src, dst, keep)
            return inner_carry

        lax.fori_loop(8, 16, own, 0)

    def two_steps(k, carry):
        step(2 * k + 1, q, q_odd)
        step(2 * k + 2, q_odd, q)
        return carry

    lax.fori_loop(0, SNAPS // 2, two_steps, 0)

    for i in range(8):
        final_ref[i] = snap[rows_at(7 * 8 * CP + (own_j + i) * 8 + own_s, CP), :]

    weight = weights[var]
    sums = [jnp.zeros((8, 128), jnp.float32)] * len(PAIRS)
    for z in range(8):
        vals = [
            snap[rows_at(pl.multiple_of(t * 8 * CP + z * CP + own_tile * 8, 8)), :]
            .astype(jnp.bfloat16)
            .astype(jnp.float32)
            for t in range(SNAPS)
        ]
        for n, (a, b) in enumerate(PAIRS):
            sums[n] = sums[n] + vals[a] * vals[b]
    for n in range(len(PAIRS)):
        corr_ref[n] += weight * sums[n]

    def pack(t, carry):
        base = t * (8 * CP)
        for s in range(8):
            for j in range(0, TILES, 2):
                pair = [snap[rows_at(base + (j + e) * 8 + s, CP), :] for e in range(2)]
                x = s * TILES + j
                snaps_ref[t, x * 8 : x * 8 + 16, :] = jnp.concatenate(pair).astype(jnp.bfloat16)
        return carry

    lax.fori_loop(0, SNAPS, pack, 0)


def evolve(ints, speeds, weights, own, par):
    smem = pl.BlockSpec(memory_space=pltpu.SMEM)

    def stream(index):
        return pl.BlockSpec((32, None, 64, 128), lambda v: (0, index(v), 0, 0))

    return pl.pallas_call(
        evolve_kernel,
        name="evolve",
        grid=(VARS,),
        in_specs=[
            smem, smem, smem,
            stream(lambda v: 0), stream(lambda v: 0), stream(lambda v: 6),
            stream(lambda v: v + 1), stream(lambda v: v + 1),
            stream(lambda v: jnp.minimum(v + 7, 8)), stream(lambda v: jnp.maximum(v + 4, 6)),
        ],
        out_specs=[
            pl.BlockSpec((SNAPS, None, 2048, 128), lambda v: (0, v, 0, 0)),
            pl.BlockSpec((None, 8, 8, 128), lambda v: (v, 0, 0, 0)),
            pl.BlockSpec((len(PAIRS), 8, 128), lambda v: (0, 0, 0)),
        ],
        out_shape=[
            jax.ShapeDtypeStruct((SNAPS, VARS, 2048, 128), jnp.bfloat16),
            jax.ShapeDtypeStruct((VARS, 8, 8, 128), jnp.float32),
            jax.ShapeDtypeStruct((len(PAIRS), 8, 128), jnp.float32),
        ],
        scratch_shapes=[
            pltpu.VMEM((PLANES * QP, 128), jnp.float32),
            pltpu.VMEM((PLANES * QP, 128), jnp.float32),
            pltpu.VMEM((PLANES * FP, 128), jnp.float32),
            pltpu.VMEM((PLANES * CP, 128), jnp.float32),
            pltpu.VMEM((PLANES * CP, 128), jnp.float32),
            pltpu.VMEM(((PLANES + 1) * CP, 128), jnp.float32),
            pltpu.VMEM((PLANES * CP, 128), jnp.float32),
            pltpu.VMEM((SNAPS * 8 * CP, 128), jnp.float32),
            pltpu.VMEM((2048, 128), jnp.float32),
        ],
        compiler_params=pltpu.CompilerParams(vmem_limit_bytes=66_000_000),
    )(ints, speeds, weights, own, par, own, own, par, own, par)


def project_kernel(high_ref, low_ref, snaps_ref, out_ref):
    rows = snaps_ref.shape[1]

    def group(k, carry):
        at = pl.ds(pl.multiple_of(k * 32, 32), 32)
        data = snaps_ref[:, at, :].reshape(SNAPS * 32, 128)
        value = jnp.dot(high_ref[...], data, preferred_element_type=jnp.float32)
        value += jnp.dot(low_ref[...], data, preferred_element_type=jnp.float32)
        out_ref[:, at, :] = value.astype(jnp.bfloat16).reshape(8, 32, 128)
        return carry

    lax.fori_loop(0, rows // 32, group, 0, unroll=4)


def project(matrix, snaps):
    wide = jnp.kron(matrix, jnp.eye(32, dtype=jnp.float32))
    high = wide.astype(jnp.bfloat16)
    low = (wide - high.astype(jnp.float32)).astype(jnp.bfloat16)
    size = 1024
    whole = pl.BlockSpec((256, 256), lambda v, c: (0, 0))
    tile = pl.BlockSpec((SNAPS, None, size, 128), lambda v, c: (0, v, c, 0))
    return pl.pallas_call(
        project_kernel,
        name="project",
        grid=(VARS, 2048 // size),
        in_specs=[whole, whole, tile],
        out_specs=tile,
        out_shape=jax.ShapeDtypeStruct(snaps.shape, jnp.bfloat16),
    )(high, low, snaps)


def ring_gather(block, axis_of_core, direct):
    axes = ("grp_1", "dev_1", "dev_2")

    def shift(by):
        pairs = []
        for core in range(2):
            for y in range(4):
                for x in range(4):
                    to = ((y + by) % 4, x) if axis_of_core[core] == "y" else (y, (x + by) % 4)
                    pairs.append((core * 16 + y * 4 + x, core * 16 + to[0] * 4 + to[1]))
        return pairs

    before = lax.ppermute(block, axes, shift(1))
    after = lax.ppermute(block, axes, shift(-1))
    if direct:
        across = lax.ppermute(block, axes, shift(2))
    else:
        half = block.shape[0] // 2
        across = jnp.concatenate(
            [
                lax.ppermute(before[:half], axes, shift(1)),
                lax.ppermute(after[half:], axes, shift(-1)),
            ]
        )
    return jnp.stack([block, after, across, before])


def gather_sections(initial_state, viscosity):
    state = jnp.concatenate([viscosity[None], initial_state]).astype(jnp.bfloat16)
    state = state.reshape(VARS + 1, 64, 128)
    near = lax.ppermute(state[:3], GRP, [(2, 1), (1, 2)])
    far = lax.ppermute(state[3:], GRP, [(2, 0), (1, 3)])
    block = jnp.concatenate([state, near + far])
    other = lax.ppermute(block, "dev_0", [(0, 1), (1, 0)])
    pair = jnp.stack([block, other])
    first = ring_gather(pair, ("y", "x"), True)
    own = ring_gather(first, ("x", "y"), False).reshape(32, 9, 64, 128)
    par = lax.ppermute(own, "grp_1", [(0, 1), (1, 0)])
    return own, par


def layout_ints():
    h, c, l, y, x = (lax.axis_index(axis) for axis in GRP_DEV)
    slots = jnp.arange(32)
    outer_rel, inner_rel, l_rel = slots // 8, slots // 2 % 4, slots % 2

    def owners(core):
        along_y = jnp.where(core == 0, inner_rel, outer_rel)
        along_x = jnp.where(core == 0, outer_rel, inner_rel)
        return ((l + l_rel) % 2) * 16 + ((y + along_y) % 4) * 4 + (x + along_x) % 4

    d = l * 16 + y * 4 + x
    inner = (h != c).astype(jnp.int32)
    par_base = jnp.where(c == 1, 0, 16)
    third_base = 16 - par_base
    steps = jnp.arange(12)
    low = jnp.where((inner == 0) & (c == 0), 8, steps)
    high = jnp.where((inner == 0) & (c == 1), 16, 24 - steps)
    scalars = jnp.stack([par_base, third_base, inner, d, d // 4, (d % 4) * 8, d, d])
    return jnp.concatenate([owners(c), owners(1 - c), scalars, low, high]).astype(jnp.int32)


def body(initial_state, viscosity, speeds, energy_weights, block_index, block_offset):
    own, par = gather_sections(initial_state, viscosity)
    snaps, final, corr = evolve(layout_ints(), speeds.reshape(-1), energy_weights, own, par)
    sums = jnp.sum(corr, axis=(1, 2))
    for axis in GRP_DEV:
        sums = lax.psum(sums, axis)
    sums = sums / CELLS
    order = [[PAIRS.index((min(a, b), max(a, b))) for b in range(SNAPS)] for a in range(SNAPS)]
    corr_matrix = sums[jnp.array(order)]
    coef = block_coefficients(block_index, block_offset)
    own_coef = lax.dynamic_slice_in_dim(coef, lax.axis_index(DEV) * 2, 2, 0)
    energy, matrix = mode_matrix(own_coef, corr_matrix)
    modes = project(matrix.reshape(8, SNAPS), snaps)
    return final, modes.reshape(2, BLOCKS, 2, VARS, 256, 8, 128), energy


def solution(mesh):
    torus = Mesh(mesh.devices.reshape(2, 2, 2, 4, 4), GRP_DEV)
    in_specs = (P(None, DEV, GRP, None), P(DEV, GRP, None), P(), P(), P(), P())
    out_specs = (P(None, DEV, GRP, None), P(DEV, None, None, None, None, GRP, None), P(DEV))
    return jax.shard_map(body, mesh=torus, in_specs=in_specs, out_specs=out_specs, check_vma=False)
```

time: 619 us -> 284 us (0.46)
  Pallas kernels: 0 us -> 175 us
  local copies, waits for them, and re-layouts: 172 us -> 3.03 us
  blocking collectives: 154 us -> 29.3 us
  starting transfers between devices: 129 us -> 20.7 us
  matrix products: 78.1 us -> 0 us
  other arithmetic: 55.1 us -> 8.95 us
  waiting for transfers between devices: 8.97 us -> 41.9 us
  between operations: 14.9 us -> 0.85 us
    pallas_call x0 -> x2, Pallas kernels: none -> 175 us  [the longest x1 137 us: evolve(): pl.pallas_call(evolve_kernel, name='evolve', grid=(VARS,), in_specs=[smem...]
    psum x5, blocking collectives: 154 us -> 29.3 us  [body(): sums = lax.psum(sums, axis)]
    ppermute x36 -> x11, starting transfers between devices: 129 us -> 20.7 us  [the longest x1 6.32 us: gather_sections(): far = lax.ppermute(state[3:], GRP, [(2, 0), (1, 3)])]
    reshape x2 -> x1, local copies, waits for them, and re-layouts: 83.8 us -> 0.66 us  [body(): speeds.reshape(-1)]
    dot_general x8 -> x0, matrix products: 78.1 us -> none  [the longest x1 56.5 us: body(): product = jnp.dot(own_coef, flattened, precision=lax.Precision.HIGHEST)]
    slice x37 -> x7, local copies, waits for them, and re-layouts: 54.4 us -> 0.41 us  [the longest x2 0.09 us: mode_matrix(): coef[:, 1, 0]]
    ppermute x36 -> x11, waiting for transfers between devices: 8.94 us -> 41.9 us  [the longest x2 16.4 us: ring_gather(): after = lax.ppermute(block, axes, shift(-1))]
    unnamed x12 -> x9, local copies, waits for them, and re-layouts: 31.1 us -> 0.12 us
  transfers between devices with their start and end apart: 37 -> 11, of which waited for: 7 -> 8; matrix products, arithmetic and copies ran while one was open for 22% -> 1% of each run, Pallas kernels for 0% -> 0%
where the time goes in v1:
time: 284 us; the launch traced here: 279 us
  Pallas kernels  175 us (62%)
  waiting for transfers between devices  41.9 us (15%)
  blocking collectives  29.3 us (10%)
  starting transfers between devices  20.7 us (7%)
  other arithmetic  8.95 us (3%)
  local copies, waits for them, and re-layouts  3.03 us (1%)
    pallas_call x1, Pallas kernels, evolve(): pl.pallas_call(evolve_kernel, name='evolve', grid=(VARS,), in_specs=[smem...  137 us
    pallas_call x1, Pallas kernels, project(): pl.pallas_call(project_kernel, name='project', grid=(VARS, 2048 // size),...  37.2 us
    psum x5, blocking collectives, body(): sums = lax.psum(sums, axis)  29.3 us
    ppermute x2, waiting for transfers between devices, ring_gather(): after = lax.ppermute(block, axes, shift(-1))  16.4 us
    ppermute x1, waiting for transfers between devices, ring_gather(): lax.ppermute(after[half:], axes, shift(-1))  6.7 us
    ppermute x1, starting transfers between devices, gather_sections(): far = lax.ppermute(state[3:], GRP, [(2, 0), (1, 3)])  6.32 us
  transfers between devices with their start and end apart: 11, of which 8 were waited for; matrix products, arithmetic and copies ran while one was open for 1% of the time, Pallas kernels for 0%

profile of v1, /device:TPU:1, one launch (start us, length us, event | category | flops | bytes accessed | tf_op | source)
XLA Modules:
  0.0 279.4 jit_solution(4328124730373046176)
XLA Ops:
  0.6 0.8 convert_bitcast_fusion.1
  1.4 0.9 convert.12
  2.3 6.3 %collective-permute-start.1 = (bf16[3,64,128]{2,1,0:T(8,128)(2,1)S(1)}, bf16[3,64,128]{2,1,0:T(8,128)(2,1)S(1)}, u32[]{:S(2)}, u32[]{:S(2)}) collective-permute-start(bf16[3,64,128]{2,1,0:T(8,128)(2,1)S(1)} %get-tuple-element.30), channel_id=1, source_target_pairs={{64,0},{32,96},{65,1},{33,97},{66,2},{34,98},{67,3},{35,99},{68,4}... | collective-permute-start | bytes 147464 | tf_op jit(solution)/shard_map/ppermute | solution.py:368
  8.7 2.0 collective-permute-start
  10.7 0.9 convert_bitcast_fusion.2
  11.6 4.0 %collective-permute-done = bf16[3,64,128]{2,1,0:T(8,128)(2,1)S(1)} collective-permute-done((bf16[3,64,128]{2,1,0:T(8,128)(2,1)S(1)}, bf16[3,64,128]{2,1,0:T(8,128)(2,1)S(1)}, u32[]{:S(2)}, u32[]{:S(2)}) %collective-permute-start) | collective-permute-done | bytes 49184 | tf_op jit(solution)/shard_map/ppermute | solution.py:367
  15.7 1.3 collective-permute-start.2
  17.0 2.8 collective-permute-done.2
  19.8 2.8 %collective-permute-start.4 = (bf16[2,9,64,128]{3,2,1,0:T(8,128)(2,1)S(1)}, bf16[2,9,64,128]{3,2,1,0:T(8,128)(2,1)S(1)}, u32[]{:S(2)}, u32[]{:S(2)}) collective-permute-start(bf16[2,9,64,128]{3,2,1,0:T(8,128)(2,1)S(1)} %get-tuple-element.27), channel_id=1, source_target_pairs={{0,8},{1,9},{2,10},{3,11},{4,12},{5,13},{6,14},{7,15},{8,0},{9,1},... | collective-permute-start | bytes 884744 | tf_op jit(solution)/shard_map/ppermute | solution.py:352
  22.6 0.9 collective-permute-start.3
  23.5 0.6 collective-permute-start.5
  24.1 2.9 %collective-permute-done.4 = bf16[2,9,64,128]{3,2,1,0:T(8,128)(2,1)S(1)} collective-permute-done((bf16[2,9,64,128]{3,2,1,0:T(8,128)(2,1)S(1)}, bf16[2,9,64,128]{3,2,1,0:T(8,128)(2,1)S(1)}, u32[]{:S(2)}, u32[]{:S(2)}) %collective-permute-start.4) | collective-permute-done | bytes 294944 | tf_op jit(solution)/shard_map/ppermute | solution.py:352
  27.0 3.3 %collective-permute-done.3 = bf16[2,9,64,128]{3,2,1,0:T(8,128)(2,1)S(1)} collective-permute-done((bf16[2,9,64,128]{3,2,1,0:T(8,128)(2,1)S(1)}, bf16[2,9,64,128]{3,2,1,0:T(8,128)(2,1)S(1)}, u32[]{:S(2)}, u32[]{:S(2)}) %collective-permute-start.3) | collective-permute-done | bytes 294944 | tf_op jit(solution)/shard_map/ppermute | solution.py:350
  30.5 2.8 %collective-permute-start.6 = (bf16[4,2,9,64,128]{4,3,2,1,0:T(8,128)(2,1)S(1)}, bf16[4,2,9,64,128]{4,3,2,1,0:T(8,128)(2,1)S(1)}, u32[]{:S(2)}, u32[]{:S(2)}) collective-permute-start(bf16[4,2,9,64,128]{4,3,2,1,0:T(8,128)(2,1)S(1)} %get-tuple-element.25), channel_id=1, source_target_pairs={{0,3},{1,0},{2,1},{3,2},{4,7},{5,4},{6,5},{7,6},{8,11},{9,8},{10,9... | collective-permute-start | bytes 3538952 | tf_op jit(solution)/shard_map/ppermute | solution.py:350
  33.3 13.1 %collective-permute-done.6 = bf16[4,2,9,64,128]{4,3,2,1,0:T(8,128)(2,1)S(1)} collective-permute-done((bf16[4,2,9,64,128]{4,3,2,1,0:T(8,128)(2,1)S(1)}, bf16[4,2,9,64,128]{4,3,2,1,0:T(8,128)(2,1)S(1)}, u32[]{:S(2)}, u32[]{:S(2)}) %collective-permute-start.6) | collective-permute-done | bytes 1179680 | tf_op jit(solution)/shard_map/ppermute | solution.py:350
  46.5 3.5 %collective-permute-start.9 = (bf16[2,2,9,64,128]{4,3,2,1,0:T(8,128)(2,1)S(1)}, bf16[2,2,9,64,128]{4,3,2,1,0:T(8,128)(2,1)S(1)}, u32[]{:S(2)}, u32[]{:S(2)}) collective-permute-start(bf16[2,2,9,64,128]{4,3,2,1,0:T(8,128)(2,1)S(1)} %slice.45), channel_id=1, source_target_pairs={{0,3},{1,0},{2,1},{3,2},{4,7},{5,4},{6,5},{7,6},{8,11},{9,8},{10,9... | collective-permute-start | bytes 1769480 | tf_op jit(solution)/shard_map/ppermute | solution.py:358
  50.1 6.7 %collective-permute-done.9 = bf16[2,2,9,64,128]{4,3,2,1,0:T(8,128)(2,1)S(1)} collective-permute-done((bf16[2,2,9,64,128]{4,3,2,1,0:T(8,128)(2,1)S(1)}, bf16[2,2,9,64,128]{4,3,2,1,0:T(8,128)(2,1)S(1)}, u32[]{:S(2)}, u32[]{:S(2)}) %collective-permute-start.9) | collective-permute-done | bytes 589856 | tf_op jit(solution)/shard_map/ppermute | solution.py:358
  56.8 3.5 %collective-permute-done.8 = bf16[2,2,9,64,128]{4,3,2,1,0:T(8,128)(2,1)S(1)} collective-permute-done((bf16[2,2,9,64,128]{4,3,2,1,0:T(8,128)(2,1)S(1)}, bf16[2,2,9,64,128]{4,3,2,1,0:T(8,128)(2,1)S(1)}, u32[]{:S(2)}, u32[]{:S(2)}) %collective-permute-start.8) | collective-permute-done | bytes 589856 | tf_op jit(solution)/shard_map/ppermute | solution.py:357
  60.4 2.5 pad_maximum_fusion
  63.4 0.7 reshape.519.speeds
  65.0 0.7 concatenate.20.ints
  65.7 5.5 %collective-permute-done.10.nu_par.q_par.q_tb = bf16[32,9,64,128]{3,2,1,0:T(8,128)(2,1)} collective-permute-done((bf16[32,9,64,128]{3,2,1,0:T(8,128)(2,1)}, bf16[32,9,64,128]{3,2,1,0:T(8,128)(2,1)}, u32[]{:S(2)}, u32[]{:S(2)}) %collective-permute-start.10) | collective-permute-done | bytes 4718624 | tf_op jit(solution)/shard_map/ppermute | solution.py:374
  71.2 137.4 %evolve.1 = (bf16[8,5,2048,128]{3,2,1,0:T(8,128)(2,1)}, f32[5,8,8,128]{3,2,1,0:T(8,128)}, f32[36,8,128]{2,1,0:T(8,128)}) custom-call(s32[96]{0:T(128)} %concatenate.20.ints, f32[15]{0:T(128)} %reshape.519.speeds, f32[5]{0:T(128)} %weights.1, bf16[32,9,64,128]{3,2,1,0:T(8,128)(2,1)} %bitcast.21.nu_own.nu_third.q_own.q_ta, ...), custom_call_target="tpu_custom_call" | custom-call | tf_op jit(solution)/shard_map/evolve/pallas_call | solution.py:271
  208.7 1.3 reduce_sum.101
  209.9 5.3 %psum.35 = f32[36]{0:T(128)S(1)} all-reduce(f32[36]{0:T(128)S(1)} %reduce_sum.101), channel_id=1, replica_groups=mesh['grp_0'=2,'grp_1'=2,'dev_0'=2,'dev_1'=4,'dev_2'=4] {'grp_0'}, use_global_device_ids=true, to_apply=%region_3.4 | all-reduce | flops 36 | bytes 288 | tf_op jit(solution)/shard_map/psum | solution.py:404
  215.2 6.9 %psum.36 = f32[36]{0:T(128)S(1)} all-reduce(f32[36]{0:T(128)S(1)} %psum.35), channel_id=1, replica_groups=mesh['grp_0'=2,'grp_1'=2,'dev_0'=2,'dev_1'=4,'dev_2'=4] {'grp_1'}, use_global_device_ids=true, to_apply=%region_4.5 | all-reduce | flops 36 | bytes 288 | tf_op jit(solution)/shard_map/psum | solution.py:404
  222.0 4.3 %psum.37 = f32[36]{0:T(128)S(1)} all-reduce(f32[36]{0:T(128)S(1)} %psum.36), channel_id=1, replica_groups=mesh['grp_0'=2,'grp_1'=2,'dev_0'=2,'dev_1'=4,'dev_2'=4] {'dev_0'}, use_global_device_ids=true, to_apply=%region_5.6 | all-reduce | flops 36 | bytes 288 | tf_op jit(solution)/shard_map/psum | solution.py:404
  226.3 6.9 %psum.38 = f32[36]{0:T(128)S(1)} all-reduce(f32[36]{0:T(128)S(1)} %psum.37), channel_id=1, replica_groups=mesh['grp_0'=2,'grp_1'=2,'dev_0'=2,'dev_1'=4,'dev_2'=4] {'dev_1'}, use_global_device_ids=true, to_apply=%region_6.7 | all-reduce | flops 36 | bytes 288 | tf_op jit(solution)/shard_map/psum | solution.py:404
  233.3 6.0 %psum.39 = f32[36]{0:T(128)S(1)} all-reduce(f32[36]{0:T(128)S(1)} %psum.38), channel_id=1, replica_groups=mesh['grp_0'=2,'grp_1'=2,'dev_0'=2,'dev_1'=4,'dev_2'=4] {'dev_2'}, use_global_device_ids=true, to_apply=%region_7.8 | all-reduce | flops 36 | bytes 288 | tf_op jit(solution)/shard_map/psum | solution.py:404
  239.3 0.8 gather_fusion
  241.4 0.7 subtract_convert_fusion
  242.1 37.2 %project.1 = bf16[8,5,2048,128]{3,2,1,0:T(8,128)(2,1)} custom-call(bf16[256,256]{1,0:T(8,128)(2,1)} %get-tuple-element.23.high_ref, bf16[256,256]{1,0:T(8,128)(2,1)} %get-tuple-element.22.low_ref, bf16[8,5,2048,128]{3,2,1,0:T(8,128)(2,1)} %get-tuple-element.8.snaps_ref), custom_call_target="tpu_custom_call" | custom-call | tf_op jit(solution)/shard_map/project/pallas_call | solution.py:327
  (49 shorter events, 3.3 us)
Async XLA Ops:
  2.3 9.3 %collective-permute-start.1 = (bf16[3,64,128]{2,1,0:T(8,128)(2,1)S(1)}, bf16[3,64,128]{2,1,0:T(8,128)(2,1)S(1)}, u32[]{:S(2)}, u32[]{:S(2)}) collective-permute-start(bf16[3,64,128]{2,1,0:T(8,128)(2,1)S(1)} %get-tuple-element.30), channel_id=1, source_target_pairs={{64,0},{32,96},{65,1},{33,97},{66,2},{34,98},{67,3},{35,99},{68,4}... | collective-permute-start | bytes 147464 | tf_op jit(solution)/shard_map/ppermute | solution.py:368
  8.7 7.0 %collective-permute-start = (bf16[3,64,128]{2,1,0:T(8,128)(2,1)S(1)}, bf16[3,64,128]{2,1,0:T(8,128)(2,1)S(1)}, u32[]{:S(2)}, u32[]{:S(2)}) collective-permute-start(bf16[3,64,128]{2,1,0:T(8,128)(2,1)S(1)} %get-tuple-element.31), channel_id=1, source_target_pairs={{64,32},{32,64},{65,33},{33,65},{66,34},{34,66},{67,35},{35,67},{6... | collective-permute-start | bytes 147464 | tf_op jit(solution)/shard_map/ppermute | solution.py:367
  15.7 4.1 %collective-permute-start.2 = (bf16[9,64,128]{2,1,0:T(8,128)(2,1)S(1)}, bf16[9,64,128]{2,1,0:T(8,128)(2,1)S(1)}, u32[]{:S(2)}, u32[]{:S(2)}) collective-permute-start(bf16[9,64,128]{2,1,0:T(8,128)(2,1)S(1)} %get-tuple-element.29), channel_id=1, source_target_pairs={{0,16},{16,0},{1,17},{17,1},{2,18},{18,2},{3,19},{19,3},{4,20},{20... | collective-permute-start | bytes 442376 | tf_op jit(solution)/shard_map/ppermute | solution.py:370
  19.8 7.2 %collective-permute-start.4 = (bf16[2,9,64,128]{3,2,1,0:T(8,128)(2,1)S(1)}, bf16[2,9,64,128]{3,2,1,0:T(8,128)(2,1)S(1)}, u32[]{:S(2)}, u32[]{:S(2)}) collective-permute-start(bf16[2,9,64,128]{3,2,1,0:T(8,128)(2,1)S(1)} %get-tuple-element.27), channel_id=1, source_target_pairs={{0,8},{1,9},{2,10},{3,11},{4,12},{5,13},{6,14},{7,15},{8,0},{9,1},... | collective-permute-start | bytes 884744 | tf_op jit(solution)/shard_map/ppermute | solution.py:352
  22.6 7.6 %collective-permute-start.3 = (bf16[2,9,64,128]{3,2,1,0:T(8,128)(2,1)S(1)}, bf16[2,9,64,128]{3,2,1,0:T(8,128)(2,1)S(1)}, u32[]{:S(2)}, u32[]{:S(2)}) collective-permute-start(bf16[2,9,64,128]{3,2,1,0:T(8,128)(2,1)S(1)} %get-tuple-element.27), channel_id=1, source_target_pairs={{0,12},{1,13},{2,14},{3,15},{4,0},{5,1},{6,2},{7,3},{8,4},{9,5},{1... | collective-permute-start | bytes 884744 | tf_op jit(solution)/shard_map/ppermute | solution.py:350
  23.5 6.8 %collective-permute-start.5 = (bf16[2,9,64,128]{3,2,1,0:T(8,128)(2,1)S(1)}, bf16[2,9,64,128]{3,2,1,0:T(8,128)(2,1)S(1)}, u32[]{:S(2)}, u32[]{:S(2)}) collective-permute-start(bf16[2,9,64,128]{3,2,1,0:T(8,128)(2,1)S(1)} %get-tuple-element.27), channel_id=1, source_target_pairs={{0,4},{1,5},{2,6},{3,7},{4,8},{5,9},{6,10},{7,11},{8,12},{9,13},{1... | collective-permute-start | bytes 884744 | tf_op jit(solution)/shard_map/ppermute | solution.py:349
  30.5 16.0 %collective-permute-start.6 = (bf16[4,2,9,64,128]{4,3,2,1,0:T(8,128)(2,1)S(1)}, bf16[4,2,9,64,128]{4,3,2,1,0:T(8,128)(2,1)S(1)}, u32[]{:S(2)}, u32[]{:S(2)}) collective-permute-start(bf16[4,2,9,64,128]{4,3,2,1,0:T(8,128)(2,1)S(1)} %get-tuple-element.25), channel_id=1, source_target_pairs={{0,3},{1,0},{2,1},{3,2},{4,7},{5,4},{6,5},{7,6},{8,11},{9,8},{10,9... | collective-permute-start | bytes 3538952 | tf_op jit(solution)/shard_map/ppermute | solution.py:350
  33.3 16.7 %collective-permute-start.7 = (bf16[4,2,9,64,128]{4,3,2,1,0:T(8,128)(2,1)S(1)}, bf16[4,2,9,64,128]{4,3,2,1,0:T(8,128)(2,1)S(1)}, u32[]{:S(2)}, u32[]{:S(2)}) collective-permute-start(bf16[4,2,9,64,128]{4,3,2,1,0:T(8,128)(2,1)S(1)} %get-tuple-element.25), channel_id=1, source_target_pairs={{0,1},{1,2},{2,3},{3,0},{4,5},{5,6},{6,7},{7,4},{8,9},{9,10},{10,1... | collective-permute-start | bytes 3538952 | tf_op jit(solution)/shard_map/ppermute | solution.py:349
  46.5 10.3 %collective-permute-start.9 = (bf16[2,2,9,64,128]{4,3,2,1,0:T(8,128)(2,1)S(1)}, bf16[2,2,9,64,128]{4,3,2,1,0:T(8,128)(2,1)S(1)}, u32[]{:S(2)}, u32[]{:S(2)}) collective-permute-start(bf16[2,2,9,64,128]{4,3,2,1,0:T(8,128)(2,1)S(1)} %slice.45), channel_id=1, source_target_pairs={{0,3},{1,0},{2,1},{3,2},{4,7},{5,4},{6,5},{7,6},{8,11},{9,8},{10,9... | collective-permute-start | bytes 1769480 | tf_op jit(solution)/shard_map/ppermute | solution.py:358
  50.0 10.3 %collective-permute-start.8 = (bf16[2,2,9,64,128]{4,3,2,1,0:T(8,128)(2,1)S(1)}, bf16[2,2,9,64,128]{4,3,2,1,0:T(8,128)(2,1)S(1)}, u32[]{:S(2)}, u32[]{:S(2)}) collective-permute-start(bf16[2,2,9,64,128]{4,3,2,1,0:T(8,128)(2,1)S(1)} %slice.44), channel_id=1, source_target_pairs={{0,1},{1,2},{2,3},{3,0},{4,5},{5,6},{6,7},{7,4},{8,9},{9,10},{10,1... | collective-permute-start | bytes 1769480 | tf_op jit(solution)/shard_map/ppermute | solution.py:357
  60.4 2.9 %copy-start.1 = (f32[5,3]{0,1:T(4,128)S(1)}, f32[5,3]{0,1:T(4,128)}, u32[]{:S(2)}) copy-start(f32[5,3]{0,1:T(4,128)} %param.9) | copy-start | bytes 184
  60.4 3.7 %copy-start = (s32[2,6]{1,0:T(2,128)S(1)}, s32[2,6]{1,0:T(2,128)}, u32[]{:S(2)}) copy-start(s32[2,6]{1,0:T(2,128)} %param.11) | copy-start | bytes 148
  60.4 3.7 %copy-start.2 = (s32[2]{0:T(128)S(1)}, s32[2]{0:T(128)}, u32[]{:S(2)}) copy-start(s32[2]{0:T(128)} %param.12) | copy-start | bytes 28
  60.4 5.2 %copy-start.3 = (s32[64]{0:T(128)S(1)}, s32[64]{0:T(128)}, u32[]{:S(2)}) copy-start(s32[64]{0:T(128)} %constant.157) | copy-start | bytes 772
  62.9 8.3 %collective-permute-start.10 = (bf16[32,9,64,128]{3,2,1,0:T(8,128)(2,1)}, bf16[32,9,64,128]{3,2,1,0:T(8,128)(2,1)}, u32[]{:S(2)}, u32[]{:S(2)}) collective-permute-start(bf16[32,9,64,128]{3,2,1,0:T(8,128)(2,1)} %bitcast.21.nu_own.nu_third.q_own.q_ta), channel_id=1, source_target_pairs={{0,32},{32,0},{1,33},{33,1},{2,34},{34,2},{3,35},{35,3},{4,36},{36... | collective-permute-start | bytes 14155784 | tf_op jit(solution)/shard_map/ppermute | solution.py:374

commit v2 on v1

v2 whole, which is shorter than its diff:
```python
import math

import jax
import jax.numpy as jnp
from jax import lax
from jax.experimental import pallas as pl
from jax.experimental.pallas import tpu as pltpu
from jax.sharding import Mesh
from jax.sharding import PartitionSpec as P

VARS = 5
FREQS = 64
BLOCKS = 2
SNAPS = 8
GRP_DEV = ("grp_0", "grp_1", "dev_0", "dev_1", "dev_2")
GRP = ("grp_0", "grp_1")
DEV = ("dev_0", "dev_1", "dev_2")
CELLS = 256 * 32 * 128

TILES = 16
PLANES = 26
LOW, OWN, HIGH = 1, 9, 17
PAIRS = [(a, b) for a in range(SNAPS) for b in range(a, SNAPS)]
BF = jnp.bfloat16


def block_coefficients(block_index, block_offset):
    frequency = jnp.arange(FREQS)
    distance = block_index - block_offset[:, None]
    angles = (frequency[:, None, None] * distance[None]).astype(jnp.float32) * (math.pi / FREQS)
    length = block_index.shape[1]
    window = jnp.sin(math.pi * (jnp.arange(length).astype(jnp.float32) + 0.5) / length) ** 2
    onehot = (block_index[:, :, None] == jnp.arange(SNAPS)[None, None, :]).astype(jnp.float32)
    cosine = jnp.sum((window * jnp.cos(angles))[..., None] * onehot[None], axis=2)
    sine = -jnp.sum((window * jnp.sin(angles))[..., None] * onehot[None], axis=2)
    return jnp.stack([cosine, sine], axis=2)


def mode_matrix(coef, corr):
    def form(a, b):
        return jnp.sum(a[:, :, None] * corr[None] * b[:, None, :], axis=(1, 2))

    a0, b0, a1, b1 = coef[:, 0, 0], coef[:, 0, 1], coef[:, 1, 0], coef[:, 1, 1]
    g00 = form(a0, a0) + form(b0, b0)
    g11 = form(a1, a1) + form(b1, b1)
    gre = form(a0, a1) + form(b0, b1)
    gim = form(a0, b1) - form(b0, a1)
    middle = (g00 + g11) * 0.5
    radius = jnp.sqrt(((g00 - g11) * 0.5) ** 2 + gre**2 + gim**2)
    low = middle - radius
    total = g00 + g11 + 1e-06
    k0, k1 = ((g00 - low) / total)[:, None], ((g11 - low) / total)[:, None]
    cr, ci = (gre / total)[:, None], (gim / total)[:, None]
    rows = [
        a0 * k0 + a1 * cr + b1 * ci,
        b0 * k0 + b1 * cr - a1 * ci,
        a0 * cr - b0 * ci + a1 * k1,
        b0 * cr + a0 * ci + b1 * k1,
    ]
    return middle + radius, jnp.stack(rows, axis=1)


def by_half(fn, *values):
    parts = [fn(*[v[:, half * 128 : half * 128 + 128] for v in values]) for half in range(2)]
    return jnp.concatenate(parts, axis=1)


def ghosts(first, last):
    place = lax.broadcasted_iota(jnp.int32, (8, 128), 0)
    low, high = (pltpu.roll(last[:, k : k + 128], 1, axis=0) for k in (0, 128))
    left = jnp.concatenate(
        [jnp.where(place == 0, 0.0, low), jnp.where(place == 0, low, high)], axis=1
    )
    low, high = (pltpu.roll(first[:, k : k + 128], 7, axis=0) for k in (0, 128))
    right = jnp.concatenate(
        [jnp.where(place == 7, high, low), jnp.where(place == 7, 0.0, high)], axis=1
    )
    return left.astype(BF), right.astype(BF)


def y_next(value):
    return by_half(lambda part: pltpu.roll(part, 127, axis=1), value)


def y_last(value):
    return by_half(lambda part: pltpu.roll(part, 1, axis=1), value)


def evolve_kernel(
    ints, speeds, matrix_ref, nu_own, nu_par, nu_third, q_own, q_par, q_ta, q_tb,
    out_ref, wide, snaps_ref, full, full_odd, even, odd, nx, ny, nym, nz, axp, axm, ayp, aym, azp, azm,
):
    var = pl.program_id(0)
    par_base, third_base, inner = ints[64], ints[65], ints[66]

    def load_section(src, table, base):
        for dl in range(2):
            def pair(ip, carry):
                rows = pl.ds(pl.multiple_of(ip * 16, 16), 16)
                halves = []
                for half in range(2):
                    blocks = [
                        src[ints[table + (half * 8 + s) * 2 + dl], rows, :].astype(jnp.float32)
                        for s in range(8)
                    ]
                    grid = jnp.stack(blocks).reshape(8, 2, 8, 128)
                    halves.append([jnp.swapaxes(grid[:, i], 0, 1) for i in range(2)])
                for i in range(2):
                    slot = dl * 8 + ip * 2 + i
                    for z in range(8):
                        val = jnp.concatenate([halves[0][i][z], halves[1][i][z]], axis=1)
                        full[base + z, slot] = val
                        even[base + z, slot + 1] = val.astype(BF)
                return carry

            lax.fori_loop(0, 4, pair, 0)

        def edge(z, carry):
            left, right = ghosts(full[base + z, 0], full[base + z, TILES - 1])
            even[base + z, 0] = left
            even[base + z, TILES + 1] = right
            return carry

        lax.fori_loop(0, 8, edge, 0)

    def load_all(own, par, third):
        load_section(own, 0, OWN)
        load_section(par, 32, par_base)

        @pl.when(inner == 1)
        def _():
            third()

    @pl.when(var == 0)
    def _():
        @pl.when(inner == 0)
        def _():
            def clear(k, carry):
                even[third_base + k] = jnp.zeros((TILES + 2, 8, 256), BF)
                odd[third_base + k] = jnp.zeros((TILES + 2, 8, 256), BF)
                full[third_base + k] = jnp.zeros((TILES, 8, 256), jnp.float32)
                return carry

            lax.fori_loop(0, 8, clear, 0)

        load_all(nu_own, nu_par, lambda: load_section(nu_third, 0, third_base))

        def faces(z, carry):
            def nu(plane, slot):
                return even[plane, slot].astype(jnp.float32)

            mid = full[z, 0]
            nx[z, 0] = ((nu(z, 0) + mid) * 0.5).astype(BF)
            for j in range(TILES):
                right = nu(z, j + 2)
                face_y = (mid + y_next(mid)) * 0.5
                nx[z, j + 1] = ((mid + right) * 0.5).astype(BF)
                nz[z + 1, j] = ((mid + full[z + 1, j]) * 0.5).astype(BF)
                nz[z, j] = ((mid + full[z - 1, j]) * 0.5).astype(BF)
                ny[z, j] = face_y.astype(BF)
                nym[z, j] = y_last(face_y).astype(BF)
                mid = right
            return carry

        lax.fori_loop(2, PLANES - 2, faces, 0)

    def third():
        @pl.when(var < 2)
        def _():
            load_section(q_ta, 0, third_base)

        @pl.when(var >= 2)
        def _():
            load_section(q_tb, 32, third_base)

    load_all(q_own, q_par, third)

    hx, hz, hy = ((0.5 * speeds[var * 3 + d]).astype(BF) for d in range(3))

    def coefs(z, carry):
        for j in range(TILES):
            axp[z, j] = nx[z, j + 1] - hx
            axm[z, j] = nx[z, j] + hx
            azp[z, j] = nz[z + 1, j] - hz
            azm[z, j] = nz[z, j] + hz
            ayp[z, j] = ny[z, j] - hy
            aym[z, j] = nym[z, j] + hy
        return carry

    lax.fori_loop(2, PLANES - 2, coefs, 0)

    def planes(groups, src, dst, old_ref, new_ref, keep):
        state = []
        for z, count in groups:
            mid = [src[z + k, 1] for k in range(count)]
            state.append((mid, [mid[k] - src[z + k, 0] for k in range(count)]))
        first, last = {}, {}
        for j in range(TILES):
            for g, (z, count) in enumerate(groups):
                mid, before = state[g]
                right = [src[z + k, j + 2] for k in range(count)]
                after = [right[k] - mid[k] for k in range(count)]
                column = [src[z - 1, j + 1]] + mid + [src[z + count, j + 1]]
                steps = [column[k + 1] - column[k] for k in range(count + 1)]
                for k in range(count):
                    at = z + k
                    old = old_ref[at, j]
                    change_x = axp[at, j] * after[k] - axm[at, j] * before[k]
                    change_z = azp[at, j] * steps[k + 1] - azm[at, j] * steps[k]
                    change_y = ayp[at, j] * (y_next(old) - old).astype(BF) + aym[at, j] * (
                        y_last(old) - old
                    ).astype(BF)
                    change = (change_x + change_z) + change_y
                    new = old + change.astype(jnp.float32)
                    new_ref[at, j] = new
                    short = new.astype(BF)
                    dst[at, j + 1] = short
                    if keep is not None:
                        snaps_ref[keep[0], keep[1] + k, j] = short
                    if j == 0:
                        first[g, k] = new
                    last[g, k] = new
                state[g] = (right, after)
        for g, (z, count) in enumerate(groups):
            for k in range(count):
                left, right = ghosts(first[g, k], last[g, k])
                dst[z + k, 0] = left
                dst[z + k, TILES + 1] = right

    def step(t, src, dst, old_ref, new_ref):
        pairs = (9 - t) // 2

        @pl.when(inner == 1)
        def _():
            def both(k, carry):
                planes(
                    [(OWN - 2 - 2 * k, 2), (HIGH + 2 * k, 2)], src, dst, old_ref, new_ref, None
                )
                return carry

            lax.fori_loop(0, pairs, both, 0)

        @pl.when(inner == 0)
        def _():
            def one(k, carry):
                base = jnp.where(par_base == LOW, OWN - 2 - 2 * k, HIGH + 2 * k)
                planes([(base, 2)], src, dst, old_ref, new_ref, None)
                return carry

            lax.fori_loop(0, pairs, one, 0)

        def own(k, carry):
            planes([(OWN + 4 * k, 4)], src, dst, old_ref, new_ref, (t - 1, 4 * k))
            return carry

        lax.fori_loop(0, 2, own, 0)

    def two_steps(k, carry):
        step(2 * k + 1, even, odd, full, full_odd)
        step(2 * k + 2, odd, even, full_odd, full)
        return carry

    lax.fori_loop(0, SNAPS // 2, two_steps, 0)

    def project(jp, carry):
        for e in range(2):
            for part in range(2):
                data = snaps_ref[:, 4 * part : 4 * part + 4, jp * 2 + e]
                value = jnp.dot(
                    matrix_ref[...], data.reshape(256, 256), preferred_element_type=jnp.float32
                )
                wide[e, :, 4 * part : 4 * part + 4] = value.reshape(8, 4, 8, 256)
        rows = pl.ds(pl.multiple_of(jp * 16, 16), 16)
        for o in range(8):
            for half in range(2):
                parts = [
                    jnp.swapaxes(wide[e, o, :, :, half * 128 : half * 128 + 128], 0, 1)
                    for e in range(2)
                ]
                out_ref[o, half * 8 : half * 8 + 8, rows, :] = (
                    jnp.concatenate(parts, axis=1).astype(BF)
                )
        return carry

    lax.fori_loop(0, TILES // 2, project, 0)


def evolve(ints, speeds, matrix, own, par):
    smem = pl.BlockSpec(memory_space=pltpu.SMEM)

    def stream(index):
        return pl.BlockSpec((32, None, 64, 128), lambda v: (0, index(v), 0, 0))

    def coef_array(planes=PLANES, tiles=TILES):
        return pltpu.VMEM((planes, tiles, 8, 256), BF)

    wide = jnp.kron(matrix, jnp.eye(32, dtype=jnp.float32)).astype(BF)
    return pl.pallas_call(
        evolve_kernel,
        name="evolve",
        grid=(VARS,),
        in_specs=[
            smem, smem, pl.BlockSpec((256, 256), lambda v: (0, 0)),
            stream(lambda v: 0), stream(lambda v: 0), stream(lambda v: 6),
            stream(lambda v: v + 1), stream(lambda v: v + 1),
            stream(lambda v: jnp.minimum(v + 7, 8)), stream(lambda v: jnp.maximum(v + 4, 6)),
        ],
        out_specs=pl.BlockSpec((8, None, 16, 128, 128), lambda v: (0, v, 0, 0, 0)),
        out_shape=jax.ShapeDtypeStruct((8, VARS, 16, 128, 128), BF),
        scratch_shapes=[
            pltpu.VMEM((2, 8, 8, 8, 256), jnp.float32),
            pltpu.VMEM((SNAPS, 8, TILES, 8, 256), BF),
            pltpu.VMEM((PLANES, TILES, 8, 256), jnp.float32),
            pltpu.VMEM((PLANES, TILES, 8, 256), jnp.float32),
            coef_array(tiles=TILES + 2), coef_array(tiles=TILES + 2), coef_array(tiles=TILES + 1),
            coef_array(), coef_array(), coef_array(PLANES + 1),
            coef_array(), coef_array(), coef_array(),
            coef_array(), coef_array(), coef_array(),
        ],
        compiler_params=pltpu.CompilerParams(vmem_limit_bytes=66_000_000),
        cost_estimate=pl.CostEstimate(
            flops=400_000_000_000, bytes_accessed=40_000_000, transcendentals=0
        ),
    )(ints, speeds, wide, own, par, own, own, par, own, par)


def ring_shift(axis_of_core, by):
    pairs = []
    for core in range(2):
        for y in range(4):
            for x in range(4):
                to = ((y + by) % 4, x) if axis_of_core[core] == "y" else (y, (x + by) % 4)
                pairs.append((core * 16 + y * 4 + x, core * 16 + to[0] * 4 + to[1]))
    return lambda value: lax.ppermute(value, ("grp_1", "dev_1", "dev_2"), pairs)


def swap_cores(value):
    return lax.ppermute(value, "grp_1", [(0, 1), (1, 0)])


SIDE = 24


def local_kernel(
    ints, speeds, weights, fields, final_ref, corr_ref,
    qa, qb, nx, nzp, nzm, nyp, nym, diag, snap,
):
    low, high = ints[0], ints[1]
    row = lax.broadcasted_iota(jnp.int32, (SIDE, 128), 0)
    mask = ((row >= ints[2]) & (row < ints[3])).astype(jnp.float32)
    rates = [[0.5 * speeds[v * 3 + d] for d in range(3)] for v in range(VARS)]

    def up(value):
        return pltpu.roll(value, SIDE - 1, axis=0)

    def down(value):
        return pltpu.roll(value, 1, axis=0)

    def faces(x, carry):
        mid = fields[0, x]
        right = (mid + fields[0, x + 1]) * 0.5
        left = (mid + fields[0, x - 1]) * 0.5
        above = (mid + up(mid)) * 0.5
        below = (mid + down(mid)) * 0.5
        ahead = (mid + pltpu.roll(mid, 127, axis=1)) * 0.5
        behind = (mid + pltpu.roll(mid, 1, axis=1)) * 0.5
        nx[x + 1] = right
        nx[x] = left
        nzp[x], nzm[x], nyp[x], nym[x] = above, below, ahead, behind
        diag[x] = 1.0 - ((right + left) + (above + below) + (ahead + behind))
        return carry

    lax.fori_loop(1, SIDE - 1, faces, 0)
    for v in range(VARS):
        qa[v] = fields[v + 1]
        qb[v] = fields[v + 1]

    def step(t, src, dst):
        def one(x, carry):
            for v in range(VARS):
                hx, hz, hy = rates[v]
                mid = src[v, x]
                new = (
                    diag[x] * mid
                    + ((nx[x + 1] - hx) * src[v, x + 1] + (nx[x] + hx) * src[v, x - 1])
                    + ((nzp[x] - hz) * up(mid) + (nzm[x] + hz) * down(mid))
                    + (
                        (nyp[x] - hy) * pltpu.roll(mid, 127, axis=1)
                        + (nym[x] + hy) * pltpu.roll(mid, 1, axis=1)
                    )
                )
                dst[v, x] = new * mask
            return carry

        lax.fori_loop(jnp.maximum(t, low), jnp.minimum(SIDE - t, high), one, 0)
        for v in range(VARS):
            for x in range(8):
                snap[t - 1, v, x] = dst[v, 8 + x, 8:16, :].astype(BF).astype(jnp.float32)

    def two_steps(k, carry):
        step(2 * k + 1, qa, qb)
        step(2 * k + 2, qb, qa)
        return carry

    lax.fori_loop(0, SNAPS // 2, two_steps, 0)
    for v in range(VARS):
        for x in range(8):
            final_ref[v, x] = qa[v, 8 + x, 8:16, :]

    corr_ref[...] = jnp.zeros_like(corr_ref)

    def correlate(v, carry):
        weight = weights[v]
        sums = [jnp.zeros((8, 128), jnp.float32)] * len(PAIRS)
        for x in range(8):
            vals = [snap[t, v, x] for t in range(SNAPS)]
            for n, (a, b) in enumerate(PAIRS):
                sums[n] = sums[n] + vals[a] * vals[b]
        for n in range(len(PAIRS)):
            corr_ref[n] += weight * sums[n]
        return carry

    lax.fori_loop(0, VARS, correlate, 0)


def local_steps(ints, speeds, weights, fields):
    smem = pl.BlockSpec(memory_space=pltpu.SMEM)
    vmem = pl.BlockSpec(memory_space=pltpu.VMEM)
    cube = pltpu.VMEM((SIDE, SIDE, 128), jnp.float32)
    cubes = pltpu.VMEM((VARS, SIDE, SIDE, 128), jnp.float32)
    return pl.pallas_call(
        local_kernel,
        name="local",
        in_specs=[smem, smem, smem, vmem],
        out_specs=[vmem, vmem],
        out_shape=[
            jax.ShapeDtypeStruct((VARS, 8, 8, 128), jnp.float32),
            jax.ShapeDtypeStruct((len(PAIRS), 8, 128), jnp.float32),
        ],
        scratch_shapes=[
            cubes, cubes, pltpu.VMEM((SIDE + 1, SIDE, 128), jnp.float32),
            cube, cube, cube, cube, cube,
            pltpu.VMEM((SNAPS, VARS, 8, 8, 128), jnp.float32),
        ],
        compiler_params=pltpu.CompilerParams(vmem_limit_bytes=24_000_000),
        cost_estimate=pl.CostEstimate(
            flops=4_000_000_000, bytes_accessed=6_000_000, transcendentals=0
        ),
    )(ints, speeds, weights, fields)


def local_ints():
    own = lax.axis_index(DEV)
    grp = lax.axis_index(GRP)
    bounds = [
        jnp.where(own == 0, 8, 0),
        jnp.where(own == 31, 16, SIDE),
        jnp.where(grp == 0, 8, 0),
        jnp.where(grp == 3, 16, SIDE),
    ]
    return jnp.stack(bounds).astype(jnp.int32)


def ring_sum(value, axes):
    one, two, three = (
        lax.ppermute(value, axes, [(i, (i + by) % 4) for i in range(4)]) for by in (1, 2, 3)
    )
    return (value + two) + (one + three)


def communicate(initial_state, viscosity, speeds, energy_weights):
    fields = jnp.concatenate([viscosity[None], initial_state])
    state = fields.astype(BF).reshape(VARS + 1, 64, 128)
    near = lax.ppermute(state[:3], GRP, [(2, 1), (1, 2)])
    far = lax.ppermute(state[3:], GRP, [(2, 0), (1, 3)])
    third = lax.ppermute(fields, GRP, [(1, 2), (2, 1)])
    par = swap_cores(fields)
    block = jnp.concatenate([state, near + far])
    other = lax.ppermute(block, "dev_0", [(0, 1), (1, 0)])

    odd = lax.axis_index("grp_1") == 1
    column = jnp.concatenate(
        [jnp.where(odd, par, third), fields, jnp.where(odd, third, par)], axis=2
    )
    up = [(i, i + 1) for i in range(31)]
    before_x = lax.ppermute(column, DEV, up)
    after_x = lax.ppermute(column, DEV, [(b, a) for a, b in up])
    cube = jnp.concatenate([before_x, column, after_x], axis=1)

    pair = jnp.stack([block, other])
    near_axis = [ring_shift(("y", "x"), by) for by in (-1, 2, 1)]
    first = jnp.stack([pair] + [shift(pair) for shift in near_axis])
    first, cube = lax.optimization_barrier((first, cube))
    forward, back = ring_shift(("x", "y"), 1), ring_shift(("x", "y"), -1)
    before, after = forward(first), back(first)
    final, corr = local_steps(local_ints(), speeds, energy_weights, cube)
    sums = jnp.sum(corr, axis=(1, 2)) / CELLS
    before, after, sums = lax.optimization_barrier((before, after, sums))
    half_before, half_after = forward(before[:2]), back(after[2:])
    sums = ring_sum(ring_sum(sums, "dev_2"), "dev_1")
    half_before, half_after, sums = lax.optimization_barrier((half_before, half_after, sums))
    across = jnp.concatenate([half_before, half_after])
    own = jnp.stack([first, after, across, before]).reshape(32, 9, 64, 128)
    partner = swap_cores(own)
    sums = ring_sum(sums, ("grp_0", "dev_0"))
    sums = sums + swap_cores(sums)
    return own, partner, final, sums


def layout_ints():
    h, c, l, y, x = (lax.axis_index(axis) for axis in GRP_DEV)
    d = jnp.arange(32)
    to_l, to_y, to_x = (d // 16 + l) % 2, (d // 4 - y) % 4, (d - x) % 4

    def slots(core):
        outer = jnp.where(core == 0, to_x, to_y)
        return outer * 8 + jnp.where(core == 0, to_y, to_x) * 2 + to_l

    inner = (h != c).astype(jnp.int32)
    par_base = jnp.where(c == 1, LOW, HIGH)
    scalars = [par_base, LOW + HIGH - par_base, inner]
    return jnp.concatenate([slots(c), slots(1 - c), jnp.stack(scalars)]).astype(jnp.int32)


def body(initial_state, viscosity, speeds, energy_weights, block_index, block_offset):
    speeds = speeds.reshape(-1)
    own, par, final, sums = communicate(initial_state, viscosity, speeds, energy_weights)
    order = [[PAIRS.index((min(a, b), max(a, b))) for b in range(SNAPS)] for a in range(SNAPS)]
    corr_matrix = sums[jnp.array(order)]
    coef = block_coefficients(block_index, block_offset)
    own_coef = lax.dynamic_slice_in_dim(coef, lax.axis_index(DEV) * 2, 2, 0)
    energy, matrix = mode_matrix(own_coef, corr_matrix)
    modes = evolve(layout_ints(), speeds, matrix.reshape(8, SNAPS), own, par)
    return final, modes.reshape(2, BLOCKS, 2, VARS, 256, 8, 128), energy


def solution(mesh):
    torus = Mesh(mesh.devices.reshape(2, 2, 2, 4, 4), GRP_DEV)
    in_specs = (P(None, DEV, GRP, None), P(DEV, GRP, None), P(), P(), P(), P())
    out_specs = (P(None, DEV, GRP, None), P(DEV, None, None, None, None, GRP, None), P(DEV))
    return jax.shard_map(body, mesh=torus, in_specs=in_specs, out_specs=out_specs, check_vma=False)
```

time: 284 us -> 203 us (0.71); the launches traced: 279 us -> 203 us
  Pallas kernels: 175 us -> 109 us
  blocking collectives: 29.3 us -> 0 us
  starting transfers between devices: 20.7 us -> 45 us
  waiting for transfers between devices: 41.9 us -> 31.5 us
    pallas_call x1, Pallas kernels: 137 us -> 96.1 us  [evolve(): pl.pallas_call(evolve_kernel, name='evolve', grid=(VARS,), in_specs=[smem...]
    psum x5 -> x0, blocking collectives: 29.3 us -> none  [body(): sums = lax.psum(sums, axis)]
    ppermute x11 -> x25, starting transfers between devices: 20.7 us -> 45 us  [the longest x7 12.9 us: ring_shift(): return lambda value: lax.ppermute(value, ('grp_1', 'dev_1', 'dev_2'), pairs)]
    pallas_call x1, Pallas kernels: 37.2 us -> 13.1 us  [local_steps(): pl.pallas_call(local_kernel, name='local', in_specs=[smem, smem, smem, vm...]
    ppermute x11 -> x25, waiting for transfers between devices: 41.9 us -> 31.5 us  [the longest x7 18.8 us: ring_shift(): return lambda value: lax.ppermute(value, ('grp_1', 'dev_1', 'dev_2'), pairs)]
  transfers between devices with their start and end apart: 11 -> 25, of which waited for: 8 -> 12; matrix products, arithmetic and copies ran while one was open for 1% -> 4% of each run, Pallas kernels for 0% -> 6%
where the time goes in v2:
time: 203 us
  Pallas kernels  109 us (54%)
  starting transfers between devices  45 us (22%)
  waiting for transfers between devices  31.5 us (16%)
  other arithmetic  11 us (5%)
  local copies, waits for them, and re-layouts  5.24 us (3%)
    pallas_call x1, Pallas kernels, evolve(): pl.pallas_call(evolve_kernel, name='evolve', grid=(VARS,), in_specs=[smem...  96.1 us
    ppermute x7, waiting for transfers between devices, ring_shift(): return lambda value: lax.ppermute(value, ('grp_1', 'dev_1', 'dev_2'), pairs)  18.8 us
    pallas_call x1, Pallas kernels, local_steps(): pl.pallas_call(local_kernel, name='local', in_specs=[smem, smem, smem, vm...  13.1 us
    ppermute x7, starting transfers between devices, ring_shift(): return lambda value: lax.ppermute(value, ('grp_1', 'dev_1', 'dev_2'), pairs)  12.9 us
    ppermute x9, starting transfers between devices, ring_sum(): lax.ppermute(value, axes, [(i, (i + by) % 4) for i in range(4)])  11.9 us
    ppermute x9, waiting for transfers between devices, ring_sum(): lax.ppermute(value, axes, [(i, (i + by) % 4) for i in range(4)])  9.16 us
    ppermute x1, starting transfers between devices, communicate(): third = lax.ppermute(fields, GRP, [(1, 2), (2, 1)])  5.52 us
    ppermute x3, starting transfers between devices, swap_cores(): return lax.ppermute(value, 'grp_1', [(0, 1), (1, 0)])  4.98 us
  transfers between devices with their start and end apart: 25, of which 12 were waited for; matrix products, arithmetic and copies ran while one was open for 4% of the time, Pallas kernels for 6%

profile of v2, /device:TPU:1, one launch (start us, length us, event | category | flops | bytes accessed | tf_op | source)
XLA Modules:
  0.0 202.8 jit_solution(7102394213083681486)
XLA Ops:
  1.6 1.5 collective-permute-start.6
  3.1 5.5 %collective-permute-start.7 = (f32[6,8,8,128]{3,2,1,0:T(8,128)S(1)}, f32[6,8,8,128]{3,2,1,0:T(8,128)S(1)}, u32[]{:S(2)}, u32[]{:S(2)}) collective-permute-start(f32[6,8,8,128]{3,2,1,0:T(8,128)S(1)} %pad_maximum_fusion.5), channel_id=1, source_target_pairs={{32,64},{64,32},{33,65},{65,33},{34,66},{66,34},{35,67},{67,35},{3... | collective-permute-start | bytes 589832 | tf_op jit(solution)/shard_map/ppermute | solution.py:476
  9.6 1.3 collective-permute-start.1
  10.9 1.9 collective-permute-start
  14.5 3.3 %collective-permute-done = bf16[3,64,128]{2,1,0:T(8,128)(2,1)S(1)} collective-permute-done((bf16[3,64,128]{2,1,0:T(8,128)(2,1)S(1)}, bf16[3,64,128]{2,1,0:T(8,128)(2,1)S(1)}, u32[]{:S(2)}, u32[]{:S(2)}) %collective-permute-start) | collective-permute-done | bytes 49184 | tf_op jit(solution)/shard_map/ppermute | solution.py:474
  17.9 1.3 collective-permute-start.2
  19.3 1.3 collective-permute-start.9
  20.6 4.0 %collective-permute-start.8 = (f32[6,8,24,128]{3,2,1,0:T(8,128)S(1)}, f32[6,8,24,128]{3,2,1,0:T(8,128)S(1)}, u32[]{:S(2)}, u32[]{:S(2)}) collective-permute-start(f32[6,8,24,128]{3,2,1,0:T(8,128)S(1)} %pad_maximum_fusion.3), channel_id=1, source_target_pairs={{0,1},{1,2},{2,3},{3,4},{4,5},{5,6},{6,7},{7,8},{8,9},{9,10},{10,1... | collective-permute-start | bytes 1769480 | tf_op jit(solution)/shard_map/ppermute | solution.py:486
  24.7 2.8 %collective-permute-start.4 = (bf16[2,9,64,128]{3,2,1,0:T(8,128)(2,1)S(1)}, bf16[2,9,64,128]{3,2,1,0:T(8,128)(2,1)S(1)}, u32[]{:S(2)}, u32[]{:S(2)}) collective-permute-start(bf16[2,9,64,128]{3,2,1,0:T(8,128)(2,1)S(1)} %get-tuple-element.39), channel_id=1, source_target_pairs={{0,8},{1,9},{2,10},{3,11},{4,12},{5,13},{6,14},{7,15},{8,0},{9,1},... | collective-permute-start | bytes 884744 | tf_op jit(solution)/shard_map/ppermute | solution.py:334
  27.5 1.9 collective-permute-start.3
  29.9 10.9 %collective-permute-done.4 = bf16[2,9,64,128]{3,2,1,0:T(8,128)(2,1)S(1)} collective-permute-done((bf16[2,9,64,128]{3,2,1,0:T(8,128)(2,1)S(1)}, bf16[2,9,64,128]{3,2,1,0:T(8,128)(2,1)S(1)}, u32[]{:S(2)}, u32[]{:S(2)}) %collective-permute-start.4) | collective-permute-done | bytes 294944 | tf_op jit(solution)/shard_map/ppermute | solution.py:334
  40.8 4.9 %collective-permute-done.5 = bf16[2,9,64,128]{3,2,1,0:T(8,128)(2,1)S(1)} collective-permute-done((bf16[2,9,64,128]{3,2,1,0:T(8,128)(2,1)S(1)}, bf16[2,9,64,128]{3,2,1,0:T(8,128)(2,1)S(1)}, u32[]{:S(2)}, u32[]{:S(2)}) %collective-permute-start.5) | collective-permute-done | bytes 294944 | tf_op jit(solution)/shard_map/ppermute | solution.py:334
  45.8 1.2 pad_maximum_fusion.2
  47.1 4.9 %collective-permute-start.11 = (bf16[4,2,9,64,128]{4,3,2,1,0:T(8,128)(2,1)}, bf16[4,2,9,64,128]{4,3,2,1,0:T(8,128)(2,1)}, u32[]{:S(2)}, u32[]{:S(2)}) collective-permute-start(bf16[4,2,9,64,128]{4,3,2,1,0:T(8,128)(2,1)} %pad_maximum_fusion.2), channel_id=1, source_target_pairs={{0,3},{1,0},{2,1},{3,2},{4,7},{5,4},{6,5},{7,6},{8,11},{9,8},{10,9... | collective-permute-start | bytes 3538952 | tf_op jit(solution)/shard_map/ppermute | solution.py:334
  52.3 13.1 %local.1 = (f32[5,8,8,128]{3,2,1,0:T(8,128)}, f32[36,8,128]{2,1,0:T(8,128)S(1)}) custom-call(s32[4]{0:T(128)S(1)} %pad_add_fusion.ints, f32[15]{0:T(128)S(1)} %reshape.520.speeds, f32[5]{0:T(128)S(1)} %copy-done.1, f32[6,24,24,128]{3,2,1,0:T(8,128)S(1)} %pad_maximum_fusion.1.fields), custom_call_target="tpu_custom_call" | custom-call | flops 4000000000 | bytes 6000000 | tf_op jit(solution)/shard_map/local/pallas_call | solution.py:431
  65.7 2.9 %collective-permute-done.10 = bf16[4,2,9,64,128]{4,3,2,1,0:T(8,128)(2,1)} collective-permute-done((bf16[4,2,9,64,128]{4,3,2,1,0:T(8,128)(2,1)}, bf16[4,2,9,64,128]{4,3,2,1,0:T(8,128)(2,1)}, u32[]{:S(2)}, u32[]{:S(2)}) %collective-permute-start.10) | collective-permute-done | bytes 1179680 | tf_op jit(solution)/shard_map/ppermute | solution.py:334
  69.7 1.1 slice.36
  70.8 2.7 %collective-permute-start.13 = (bf16[2,2,9,64,128]{4,3,2,1,0:T(8,128)(2,1)S(1)}, bf16[2,2,9,64,128]{4,3,2,1,0:T(8,128)(2,1)S(1)}, u32[]{:S(2)}, u32[]{:S(2)}) collective-permute-start(bf16[2,2,9,64,128]{4,3,2,1,0:T(8,128)(2,1)S(1)} %slice.36), channel_id=1, source_target_pairs={{0,3},{1,0},{2,1},{3,2},{4,7},{5,4},{6,5},{7,6},{8,11},{9,8},{10,9... | collective-permute-start | bytes 1769480 | tf_op jit(solution)/shard_map/ppermute | solution.py:334
  73.6 1.5 collective-permute-start.15
  75.0 1.2 collective-permute-done.16
  76.3 1.2 collective-permute-done.15
  77.5 1.5 collective-permute-done.14
  78.9 2.7 %collective-permute-start.19 = (f32[36]{0:T(128)S(1)}, f32[36]{0:T(128)S(1)}, u32[]{:S(2)}, u32[]{:S(2)}) collective-permute-start(f32[36]{0:T(128)S(1)} %add_add_fusion.2), channel_id=1, source_target_pairs={{0,12},{4,0},{8,4},{12,8},{1,13},{5,1},{9,5},{13,9},{2,14},{6,2},{... | collective-permute-start | bytes 440 | tf_op jit(solution)/shard_map/ppermute | solution.py:466
  81.6 1.3 collective-permute-start.17
  82.9 2.4 %collective-permute-done.18 = f32[36]{0:T(128)S(1)} collective-permute-done((f32[36]{0:T(128)S(1)}, f32[36]{0:T(128)S(1)}, u32[]{:S(2)}, u32[]{:S(2)}) %collective-permute-start.18) | collective-permute-done | bytes 176 | tf_op jit(solution)/shard_map/ppermute | solution.py:466
  85.7 3.9 %pad_maximum_fusion = bf16[4,4,2,9,64,128]{5,4,3,2,1,0:T(8,128)(2,1)} fusion(bf16[1,4,2,9,64,128]{5,4,3,2,1,0:T(8,128)(2,1)} %bitcast.34, bf16[1,4,2,9,64,128]{5,4,3,2,1,0:T(8,128)(2,1)S(1)} %maximum_bitcast_fusion, bf16[1,4,2,9,64,128]{5,4,3,2,1,0:T(8,128)(2,1)} %bitcast.32, bf16[1,4,2,9,64,128]{5,4,3,2,1,0:T(8,128)(2,1)} %bitcast.31), kind=kLoop, calls=%fused_computation.1 | loop fusion | flops 7077888 | bytes 9437184 | tf_op jit(solution)/shard_map/stack | solution.py:503
  89.6 2.1 %collective-permute-start.24 = (bf16[32,9,64,128]{3,2,1,0:T(8,128)(2,1)}, bf16[32,9,64,128]{3,2,1,0:T(8,128)(2,1)}, u32[]{:S(2)}, u32[]{:S(2)}) collective-permute-start(bf16[32,9,64,128]{3,2,1,0:T(8,128)(2,1)} %bitcast.35.nu_own.nu_third.q_own.q_ta), channel_id=1, source_target_pairs={{0,32},{32,0},{1,33},{33,1},{2,34},{34,2},{3,35},{35,3},{4,36},{36... | collective-permute-start | bytes 14155784 | tf_op jit(solution)/shard_map/ppermute | solution.py:338
  92.6 5.1 %collective-permute-start.22 = (f32[36]{0:T(128)S(1)}, f32[36]{0:T(128)S(1)}, u32[]{:S(2)}, u32[]{:S(2)}) collective-permute-start(f32[36]{0:T(128)S(1)} %add_add_fusion.1), channel_id=1, source_target_pairs={{0,80},{16,0},{64,16},{80,64},{1,81},{17,1},{65,17},{81,65},{2,82}... | collective-permute-start | bytes 440 | tf_op jit(solution)/shard_map/ppermute | solution.py:466
  97.7 1.4 collective-permute-start.20
  99.0 2.3 %collective-permute-done.21 = f32[36]{0:T(128)S(1)} collective-permute-done((f32[36]{0:T(128)S(1)}, f32[36]{0:T(128)S(1)}, u32[]{:S(2)}, u32[]{:S(2)}) %collective-permute-start.21) | collective-permute-done | bytes 176 | tf_op jit(solution)/shard_map/ppermute | solution.py:466
  101.6 1.4 collective-permute-start.23
  106.7 96.1 %evolve.1 = bf16[8,5,16,128,128]{4,3,2,1,0:T(8,128)(2,1)} custom-call(s32[67]{0:T(128)} %concatenate.31.ints, f32[15]{0:T(128)} %copy-done, bf16[256,256]{1,0:T(8,128)(2,1)} %convert_element_type.49.matrix_ref, bf16[32,9,64,128]{3,2,1,0:T(8,128)(2,1)} %bitcast.35.nu_own.nu_third.q_own.q_ta, ...), custom_call_target="tpu_custom_call" | custom-call | flops 399999991808 | bytes 40000000 | tf_op jit(solution)/shard_map/evolve/pallas_call | solution.py:298
  (87 shorter events, 11.4 us)
Async XLA Ops:
  0.6 18.6 %copy-start.2 = (f32[5,8,8,128]{3,2,1,0:T(8,128)S(1)}, f32[5,8,8,128]{3,2,1,0:T(8,128)}, u32[]{:S(2)}) copy-start(f32[5,8,8,128]{3,2,1,0:T(8,128)} %param.7) | copy-start | bytes 491524
  0.6 18.6 %copy-start.3 = (f32[8,8,128]{2,1,0:T(8,128)S(1)}, f32[8,8,128]{2,1,0:T(8,128)}, u32[]{:S(2)}) copy-start(f32[8,8,128]{2,1,0:T(8,128)} %param.8) | copy-start | bytes 98308
  1.6 17.6 %collective-permute-start.6 = (f32[6,8,8,128]{3,2,1,0:T(8,128)S(1)}, f32[6,8,8,128]{3,2,1,0:T(8,128)S(1)}, u32[]{:S(2)}, u32[]{:S(2)}) collective-permute-start(f32[6,8,8,128]{3,2,1,0:T(8,128)S(1)} %pad_maximum_fusion.5), channel_id=1, source_target_pairs={{0,32},{32,0},{1,33},{33,1},{2,34},{34,2},{3,35},{35,3},{4,36},{36... | collective-permute-start | bytes 589832 | tf_op jit(solution)/shard_map/ppermute | solution.py:338
  3.1 16.1 %collective-permute-start.7 = (f32[6,8,8,128]{3,2,1,0:T(8,128)S(1)}, f32[6,8,8,128]{3,2,1,0:T(8,128)S(1)}, u32[]{:S(2)}, u32[]{:S(2)}) collective-permute-start(f32[6,8,8,128]{3,2,1,0:T(8,128)S(1)} %pad_maximum_fusion.5), channel_id=1, source_target_pairs={{32,64},{64,32},{33,65},{65,33},{34,66},{66,34},{35,67},{67,35},{3... | collective-permute-start | bytes 589832 | tf_op jit(solution)/shard_map/ppermute | solution.py:476
  9.6 4.9 %collective-permute-start.1 = (bf16[3,64,128]{2,1,0:T(8,128)(2,1)S(1)}, bf16[3,64,128]{2,1,0:T(8,128)(2,1)S(1)}, u32[]{:S(2)}, u32[]{:S(2)}) collective-permute-start(bf16[3,64,128]{2,1,0:T(8,128)(2,1)S(1)} %get-tuple-element.42), channel_id=1, source_target_pairs={{64,0},{32,96},{65,1},{33,97},{66,2},{34,98},{67,3},{35,99},{68,4}... | collective-permute-start | bytes 147464 | tf_op jit(solution)/shard_map/ppermute | solution.py:475
  10.9 7.0 %collective-permute-start = (bf16[3,64,128]{2,1,0:T(8,128)(2,1)S(1)}, bf16[3,64,128]{2,1,0:T(8,128)(2,1)S(1)}, u32[]{:S(2)}, u32[]{:S(2)}) collective-permute-start(bf16[3,64,128]{2,1,0:T(8,128)(2,1)S(1)} %get-tuple-element.43), channel_id=1, source_target_pairs={{64,32},{32,64},{65,33},{33,65},{66,34},{34,66},{67,35},{35,67},{6... | collective-permute-start | bytes 147464 | tf_op jit(solution)/shard_map/ppermute | solution.py:474
  17.9 6.7 %collective-permute-start.2 = (bf16[9,64,128]{2,1,0:T(8,128)(2,1)S(1)}, bf16[9,64,128]{2,1,0:T(8,128)(2,1)S(1)}, u32[]{:S(2)}, u32[]{:S(2)}) collective-permute-start(bf16[9,64,128]{2,1,0:T(8,128)(2,1)S(1)} %get-tuple-element.41), channel_id=1, source_target_pairs={{0,16},{16,0},{1,17},{17,1},{2,18},{18,2},{3,19},{19,3},{4,20},{20... | collective-permute-start | bytes 442376 | tf_op jit(solution)/shard_map/ppermute | solution.py:479
  19.3 27.6 %collective-permute-start.9 = (f32[6,8,24,128]{3,2,1,0:T(8,128)S(1)}, f32[6,8,24,128]{3,2,1,0:T(8,128)S(1)}, u32[]{:S(2)}, u32[]{:S(2)}) collective-permute-start(f32[6,8,24,128]{3,2,1,0:T(8,128)S(1)} %pad_maximum_fusion.3), channel_id=1, source_target_pairs={{1,0},{2,1},{3,2},{4,3},{5,4},{6,5},{7,6},{8,7},{9,8},{10,9},{11,1... | collective-permute-start | bytes 1769480 | tf_op jit(solution)/shard_map/ppermute | solution.py:487
  20.6 26.4 %collective-permute-start.8 = (f32[6,8,24,128]{3,2,1,0:T(8,128)S(1)}, f32[6,8,24,128]{3,2,1,0:T(8,128)S(1)}, u32[]{:S(2)}, u32[]{:S(2)}) collective-permute-start(f32[6,8,24,128]{3,2,1,0:T(8,128)S(1)} %pad_maximum_fusion.3), channel_id=1, source_target_pairs={{0,1},{1,2},{2,3},{3,4},{4,5},{5,6},{6,7},{7,8},{8,9},{9,10},{10,1... | collective-permute-start | bytes 1769480 | tf_op jit(solution)/shard_map/ppermute | solution.py:486
  24.7 16.1 %collective-permute-start.4 = (bf16[2,9,64,128]{3,2,1,0:T(8,128)(2,1)S(1)}, bf16[2,9,64,128]{3,2,1,0:T(8,128)(2,1)S(1)}, u32[]{:S(2)}, u32[]{:S(2)}) collective-permute-start(bf16[2,9,64,128]{3,2,1,0:T(8,128)(2,1)S(1)} %get-tuple-element.39), channel_id=1, source_target_pairs={{0,8},{1,9},{2,10},{3,11},{4,12},{5,13},{6,14},{7,15},{8,0},{9,1},... | collective-permute-start | bytes 884744 | tf_op jit(solution)/shard_map/ppermute | solution.py:334
  27.5 13.4 %collective-permute-start.3 = (bf16[2,9,64,128]{3,2,1,0:T(8,128)(2,1)S(1)}, bf16[2,9,64,128]{3,2,1,0:T(8,128)(2,1)S(1)}, u32[]{:S(2)}, u32[]{:S(2)}) collective-permute-start(bf16[2,9,64,128]{3,2,1,0:T(8,128)(2,1)S(1)} %get-tuple-element.39), channel_id=1, source_target_pairs={{0,12},{1,13},{2,14},{3,15},{4,0},{5,1},{6,2},{7,3},{8,4},{9,5},{1... | collective-permute-start | bytes 884744 | tf_op jit(solution)/shard_map/ppermute | solution.py:334
  29.4 16.4 %collective-permute-start.5 = (bf16[2,9,64,128]{3,2,1,0:T(8,128)(2,1)S(1)}, bf16[2,9,64,128]{3,2,1,0:T(8,128)(2,1)S(1)}, u32[]{:S(2)}, u32[]{:S(2)}) collective-permute-start(bf16[2,9,64,128]{3,2,1,0:T(8,128)(2,1)S(1)} %get-tuple-element.39), channel_id=1, source_target_pairs={{0,4},{1,5},{2,6},{3,7},{4,8},{5,9},{6,10},{7,11},{8,12},{9,13},{1... | collective-permute-start | bytes 884744 | tf_op jit(solution)/shard_map/ppermute | solution.py:334
  46.9 5.3 %copy-start.1 = (f32[5]{0:T(128)S(1)}, f32[5]{0:T(128)}, u32[]{:S(2)}) copy-start(f32[5]{0:T(128)} %weights.1) | copy-start | bytes 64
  47.1 18.6 %collective-permute-start.11 = (bf16[4,2,9,64,128]{4,3,2,1,0:T(8,128)(2,1)}, bf16[4,2,9,64,128]{4,3,2,1,0:T(8,128)(2,1)}, u32[]{:S(2)}, u32[]{:S(2)}) collective-permute-start(bf16[4,2,9,64,128]{4,3,2,1,0:T(8,128)(2,1)} %pad_maximum_fusion.2), channel_id=1, source_target_pairs={{0,3},{1,0},{2,1},{3,2},{4,7},{5,4},{6,5},{7,6},{8,11},{9,8},{10,9... | collective-permute-start | bytes 3538952 | tf_op jit(solution)/shard_map/ppermute | solution.py:334
  52.0 16.6 %collective-permute-start.10 = (bf16[4,2,9,64,128]{4,3,2,1,0:T(8,128)(2,1)}, bf16[4,2,9,64,128]{4,3,2,1,0:T(8,128)(2,1)}, u32[]{:S(2)}, u32[]{:S(2)}) collective-permute-start(bf16[4,2,9,64,128]{4,3,2,1,0:T(8,128)(2,1)} %pad_maximum_fusion.2), channel_id=1, source_target_pairs={{0,1},{1,2},{2,3},{3,0},{4,5},{5,6},{6,7},{7,4},{8,9},{9,10},{10,1... | collective-permute-start | bytes 3538952 | tf_op jit(solution)/shard_map/ppermute | solution.py:334
  52.2 13.2 %copy-start = (f32[15]{0:T(128)}, f32[15]{0:T(128)S(1)}, u32[]{:S(2)}) copy-start(f32[15]{0:T(128)S(1)} %reshape.520.speeds) | copy-start | bytes 184
  70.8 14.8 %collective-permute-start.13 = (bf16[2,2,9,64,128]{4,3,2,1,0:T(8,128)(2,1)S(1)}, bf16[2,2,9,64,128]{4,3,2,1,0:T(8,128)(2,1)S(1)}, u32[]{:S(2)}, u32[]{:S(2)}) collective-permute-start(bf16[2,2,9,64,128]{4,3,2,1,0:T(8,128)(2,1)S(1)} %slice.36), channel_id=1, source_target_pairs={{0,3},{1,0},{2,1},{3,2},{4,7},{5,4},{6,5},{7,6},{8,11},{9,8},{10,9... | collective-permute-start | bytes 1769480 | tf_op jit(solution)/shard_map/ppermute | solution.py:334
  73.5 12.0 %collective-permute-start.12 = (bf16[2,2,9,64,128]{4,3,2,1,0:T(8,128)(2,1)S(1)}, bf16[2,2,9,64,128]{4,3,2,1,0:T(8,128)(2,1)S(1)}, u32[]{:S(2)}, u32[]{:S(2)}) collective-permute-start(bf16[2,2,9,64,128]{4,3,2,1,0:T(8,128)(2,1)S(1)} %slice.35), channel_id=1, source_target_pairs={{0,1},{1,2},{2,3},{3,0},{4,5},{5,6},{6,7},{7,4},{8,9},{9,10},{10,1... | collective-permute-start | bytes 1769480 | tf_op jit(solution)/shard_map/ppermute | solution.py:334
  73.5 2.7 %collective-permute-start.16 = (f32[36]{0:T(128)S(1)}, f32[36]{0:T(128)S(1)}, u32[]{:S(2)}, u32[]{:S(2)}) collective-permute-start(f32[36]{0:T(128)S(1)} %broadcast_multiply_fusion), channel_id=1, source_target_pairs={{0,3},{1,0},{2,1},{3,2},{4,7},{5,4},{6,5},{7,6},{8,11},{9,8},{10,9... | collective-permute-start | bytes 440 | tf_op jit(solution)/shard_map/ppermute | solution.py:466
  73.6 3.9 %collective-permute-start.15 = (f32[36]{0:T(128)S(1)}, f32[36]{0:T(128)S(1)}, u32[]{:S(2)}, u32[]{:S(2)}) collective-permute-start(f32[36]{0:T(128)S(1)} %broadcast_multiply_fusion), channel_id=1, source_target_pairs={{0,1},{1,2},{2,3},{3,0},{4,5},{5,6},{6,7},{7,4},{8,9},{9,10},{10,1... | collective-permute-start | bytes 440 | tf_op jit(solution)/shard_map/ppermute | solution.py:466
  75.0 3.9 %collective-permute-start.14 = (f32[36]{0:T(128)S(1)}, f32[36]{0:T(128)S(1)}, u32[]{:S(2)}, u32[]{:S(2)}) collective-permute-start(f32[36]{0:T(128)S(1)} %broadcast_multiply_fusion), channel_id=1, source_target_pairs={{0,2},{1,3},{2,0},{3,1},{4,6},{5,7},{6,4},{7,5},{8,10},{9,11},{10,... | collective-permute-start | bytes 440 | tf_op jit(solution)/shard_map/ppermute | solution.py:466
  78.9 3.9 %collective-permute-start.19 = (f32[36]{0:T(128)S(1)}, f32[36]{0:T(128)S(1)}, u32[]{:S(2)}, u32[]{:S(2)}) collective-permute-start(f32[36]{0:T(128)S(1)} %add_add_fusion.2), channel_id=1, source_target_pairs={{0,12},{4,0},{8,4},{12,8},{1,13},{5,1},{9,5},{13,9},{2,14},{6,2},{... | collective-permute-start | bytes 440 | tf_op jit(solution)/shard_map/ppermute | solution.py:466
  81.6 3.6 %collective-permute-start.18 = (f32[36]{0:T(128)S(1)}, f32[36]{0:T(128)S(1)}, u32[]{:S(2)}, u32[]{:S(2)}) collective-permute-start(f32[36]{0:T(128)S(1)} %add_add_fusion.2), channel_id=1, source_target_pairs={{0,4},{4,8},{8,12},{12,0},{1,5},{5,9},{9,13},{13,1},{2,6},{6,10},{... | collective-permute-start | bytes 440 | tf_op jit(solution)/shard_map/ppermute | solution.py:466
  81.6 3.9 %collective-permute-start.17 = (f32[36]{0:T(128)S(1)}, f32[36]{0:T(128)S(1)}, u32[]{:S(2)}, u32[]{:S(2)}) collective-permute-start(f32[36]{0:T(128)S(1)} %add_add_fusion.2), channel_id=1, source_target_pairs={{0,8},{4,12},{8,0},{12,4},{1,9},{5,13},{9,1},{13,5},{2,10},{6,14},... | collective-permute-start | bytes 440 | tf_op jit(solution)/shard_map/ppermute | solution.py:466
  85.7 6.0 %copy-start.4 = (s32[2,6]{1,0:T(2,128)S(1)}, s32[2,6]{1,0:T(2,128)}, u32[]{:S(2)}) copy-start(s32[2,6]{1,0:T(2,128)} %param.11) | copy-start | bytes 148
  85.7 6.0 %copy-start.6 = (s32[2]{0:T(128)S(1)}, s32[2]{0:T(128)}, u32[]{:S(2)}) copy-start(s32[2]{0:T(128)} %param.12) | copy-start | bytes 28
  85.7 6.8 %copy-start.7 = (s32[64]{0:T(128)S(1)}, s32[64]{0:T(128)}, u32[]{:S(2)}) copy-start(s32[64]{0:T(128)} %constant.124) | copy-start | bytes 772
  89.6 17.2 %collective-permute-start.24 = (bf16[32,9,64,128]{3,2,1,0:T(8,128)(2,1)}, bf16[32,9,64,128]{3,2,1,0:T(8,128)(2,1)}, u32[]{:S(2)}, u32[]{:S(2)}) collective-permute-start(bf16[32,9,64,128]{3,2,1,0:T(8,128)(2,1)} %bitcast.35.nu_own.nu_third.q_own.q_ta), channel_id=1, source_target_pairs={{0,32},{32,0},{1,33},{33,1},{2,34},{34,2},{3,35},{35,3},{4,36},{36... | collective-permute-start | bytes 14155784 | tf_op jit(solution)/shard_map/ppermute | solution.py:338
  92.6 6.5 %collective-permute-start.22 = (f32[36]{0:T(128)S(1)}, f32[36]{0:T(128)S(1)}, u32[]{:S(2)}, u32[]{:S(2)}) collective-permute-start(f32[36]{0:T(128)S(1)} %add_add_fusion.1), channel_id=1, source_target_pairs={{0,80},{16,0},{64,16},{80,64},{1,81},{17,1},{65,17},{81,65},{2,82}... | collective-permute-start | bytes 440 | tf_op jit(solution)/shard_map/ppermute | solution.py:466
  97.7 3.6 %collective-permute-start.21 = (f32[36]{0:T(128)S(1)}, f32[36]{0:T(128)S(1)}, u32[]{:S(2)}, u32[]{:S(2)}) collective-permute-start(f32[36]{0:T(128)S(1)} %add_add_fusion.1), channel_id=1, source_target_pairs={{0,16},{16,64},{64,80},{80,0},{1,17},{17,65},{65,81},{81,1},{2,18}... | collective-permute-start | bytes 440 | tf_op jit(solution)/shard_map/ppermute | solution.py:466
  97.7 3.9 %collective-permute-start.20 = (f32[36]{0:T(128)S(1)}, f32[36]{0:T(128)S(1)}, u32[]{:S(2)}, u32[]{:S(2)}) collective-permute-start(f32[36]{0:T(128)S(1)} %add_add_fusion.1), channel_id=1, source_target_pairs={{0,64},{16,80},{64,0},{80,16},{1,65},{17,81},{65,1},{81,17},{2,66}... | collective-permute-start | bytes 440 | tf_op jit(solution)/shard_map/ppermute | solution.py:466
  101.6 2.3 %collective-permute-start.23 = (f32[36]{0:T(128)S(1)}, f32[36]{0:T(128)S(1)}, u32[]{:S(2)}, u32[]{:S(2)}) collective-permute-start(f32[36]{0:T(128)S(1)} %add_add_fusion), channel_id=1, source_target_pairs={{0,32},{32,0},{1,33},{33,1},{2,34},{34,2},{3,35},{35,3},{4,36},{36... | collective-permute-start | bytes 440 | tf_op jit(solution)/shard_map/ppermute | solution.py:338
  (1 other events, 5.1 us)

commit v3 on v2

--- a/solution.py
+++ b/solution.py
@@ -2,6 +2,7 @@
 
 import jax
 import jax.numpy as jnp
+import numpy as np
 from jax import lax
 from jax.experimental import pallas as pl
 from jax.experimental.pallas import tpu as pltpu
@@ -20,6 +21,7 @@
 TILES = 16
 PLANES = 26
 LOW, OWN, HIGH = 1, 9, 17
+OWN_STEP = 8
 PAIRS = [(a, b) for a in range(SNAPS) for b in range(a, SNAPS)]
 BF = jnp.bfloat16
 
@@ -87,8 +89,8 @@
 
 
 def evolve_kernel(
-    ints, speeds, matrix_ref, nu_own, nu_par, nu_third, q_own, q_par, q_ta, q_tb,
-    out_ref, wide, snaps_ref, full, full_odd, even, odd, nx, ny, nym, nz, axp, axm, ayp, aym, azp, azm,
+    ints, speeds, matrix_ref, shift_ref, nu_own, nu_par, nu_third, q_own, q_par, q_ta, q_tb,
+    out_ref, wide, slopes, snaps_ref, full, full_odd, even, odd, nx, ny, nym, nz, axp, axm, ayp, aym, azp, azm,
 ):
     var = pl.program_id(0)
     par_base, third_base, inner = ints[64], ints[65], ints[66]
@@ -191,6 +193,18 @@
 
     def planes(groups, src, dst, old_ref, new_ref, keep):
         state = []
+        total = sum(count for _, count in groups)
+        cells = [
+            src[z : z + count, 1 : TILES + 1] if isinstance(z, int)
+            else src[pl.ds(z, count), 1 : TILES + 1]
+            for z, count in groups
+        ]
+        value = jnp.dot(
+            jnp.concatenate(cells).reshape(total * TILES * 8, 256),
+            shift_ref[...],
+            preferred_element_type=jnp.float32,
+        )
+        slopes[0:total] = value.astype(BF).reshape(total, TILES, 8, 512)
         for z, count in groups:
             mid = [src[z + k, 1] for k in range(count)]
             state.append((mid, [mid[k] - src[z + k, 0] for k in range(count)]))
@@ -207,9 +221,11 @@
                     old = old_ref[at, j]
                     change_x = axp[at, j] * after[k] - axm[at, j] * before[k]
                     change_z = azp[at, j] * steps[k + 1] - azm[at, j] * steps[k]
-                    change_y = ayp[at, j] * (y_next(old) - old).astype(BF) + aym[at, j] * (
-                        y_last(old) - old
-                    ).astype(BF)
+                    place = sum(size for _, size in groups[:g]) + k
+                    change_y = (
+                        ayp[at, j] * slopes[place, j, :, :256]
+                        + aym[at, j] * slopes[place, j, :, 256:]
+                    )
                     change = (change_x + change_z) + change_y
                     new = old + change.astype(jnp.float32)
                     new_ref[at, j] = new
@@ -250,10 +266,10 @@
             lax.fori_loop(0, pairs, one, 0)
 
         def own(k, carry):
-            planes([(OWN + 4 * k, 4)], src, dst, old_ref, new_ref, (t - 1, 4 * k))
+            planes([(OWN + OWN_STEP * k, OWN_STEP)], src, dst, old_ref, new_ref, (t - 1, OWN_STEP * k))
             return carry
 
-        lax.fori_loop(0, 2, own, 0)
+        lax.fori_loop(0, 8 // OWN_STEP, own, 0)
 
     def two_steps(k, carry):
         step(2 * k + 1, even, odd, full, full_odd)
@@ -285,6 +301,12 @@
     lax.fori_loop(0, TILES // 2, project, 0)
 
 
+def y_slopes():
+    here = np.eye(128, dtype=np.float32)
+    both = [np.kron(np.eye(2), np.roll(here, by, axis=1) - here) for by in (-1, 1)]
+    return jnp.asarray(np.concatenate(both, axis=1), BF)
+
+
 def evolve(ints, speeds, matrix, own, par):
     smem = pl.BlockSpec(memory_space=pltpu.SMEM)
 
@@ -301,6 +323,7 @@
         grid=(VARS,),
         in_specs=[
             smem, smem, pl.BlockSpec((256, 256), lambda v: (0, 0)),
+            pl.BlockSpec((256, 512), lambda v: (0, 0)),
             stream(lambda v: 0), stream(lambda v: 0), stream(lambda v: 6),
             stream(lambda v: v + 1), stream(lambda v: v + 1),
             stream(lambda v: jnp.minimum(v + 7, 8)), stream(lambda v: jnp.maximum(v + 4, 6)),
@@ -309,6 +332,7 @@
         out_shape=jax.ShapeDtypeStruct((8, VARS, 16, 128, 128), BF),
         scratch_shapes=[
             pltpu.VMEM((2, 8, 8, 8, 256), jnp.float32),
+            pltpu.VMEM((8, TILES, 8, 512), BF),
             pltpu.VMEM((SNAPS, 8, TILES, 8, 256), BF),
             pltpu.VMEM((PLANES, TILES, 8, 256), jnp.float32),
             pltpu.VMEM((PLANES, TILES, 8, 256), jnp.float32),
@@ -321,7 +345,7 @@
         cost_estimate=pl.CostEstimate(
             flops=400_000_000_000, bytes_accessed=40_000_000, transcendentals=0
         ),
-    )(ints, speeds, wide, own, par, own, own, par, own, par)
+    )(ints, speeds, wide, y_slopes(), own, par, own, own, par, own, par)
 
 
 def ring_shift(axis_of_core, by):

time: 203 us -> 192 us (0.946)
  Pallas kernels: 109 us -> 97.9 us
    pallas_call x1, Pallas kernels: 96.1 us -> 84.9 us  [evolve(): pl.pallas_call(evolve_kernel, name='evolve', grid=(VARS,), in_specs=[smem...]
  transfers between devices with their start and end apart: 25 -> 25, of which waited for: 12 -> 12; matrix products, arithmetic and copies ran while one was open for 4% -> 5% of each run, Pallas kernels for 6% -> 7%
where the time goes in v3:
time: 192 us
  Pallas kernels  97.9 us (51%)
  starting transfers between devices  45 us (23%)
  waiting for transfers between devices  31.5 us (16%)
  other arithmetic  11 us (6%)
  local copies, waits for them, and re-layouts  5.24 us (3%)
    pallas_call x1, Pallas kernels, evolve(): pl.pallas_call(evolve_kernel, name='evolve', grid=(VARS,), in_specs=[smem...  84.9 us
    ppermute x7, waiting for transfers between devices, ring_shift(): return lambda value: lax.ppermute(value, ('grp_1', 'dev_1', 'dev_2'), pairs)  18.8 us
    pallas_call x1, Pallas kernels, local_steps(): pl.pallas_call(local_kernel, name='local', in_specs=[smem, smem, smem, vm...  13.1 us
    ppermute x7, starting transfers between devices, ring_shift(): return lambda value: lax.ppermute(value, ('grp_1', 'dev_1', 'dev_2'), pairs)  12.9 us
    ppermute x9, starting transfers between devices, ring_sum(): lax.ppermute(value, axes, [(i, (i + by) % 4) for i in range(4)])  11.9 us
    ppermute x9, waiting for transfers between devices, ring_sum(): lax.ppermute(value, axes, [(i, (i + by) % 4) for i in range(4)])  9.16 us
    ppermute x1, starting transfers between devices, communicate(): third = lax.ppermute(fields, GRP, [(1, 2), (2, 1)])  5.52 us
    ppermute x3, starting transfers between devices, swap_cores(): return lax.ppermute(value, 'grp_1', [(0, 1), (1, 0)])  4.98 us
  transfers between devices with their start and end apart: 25, of which 12 were waited for; matrix products, arithmetic and copies ran while one was open for 5% of the time, Pallas kernels for 7%

profile of v3, /device:TPU:1, one launch (start us, length us, event | category | flops | bytes accessed | tf_op | source)
XLA Modules:
  0.0 191.6 jit_solution(15838256864102144014)
XLA Ops:
  1.6 1.5 collective-permute-start.6
  3.1 5.5 %collective-permute-start.7 = (f32[6,8,8,128]{3,2,1,0:T(8,128)S(1)}, f32[6,8,8,128]{3,2,1,0:T(8,128)S(1)}, u32[]{:S(2)}, u32[]{:S(2)}) collective-permute-start(f32[6,8,8,128]{3,2,1,0:T(8,128)S(1)} %pad_maximum_fusion.5), channel_id=1, source_target_pairs={{32,64},{64,32},{33,65},{65,33},{34,66},{66,34},{35,67},{67,35},{3... | collective-permute-start | bytes 589832 | tf_op jit(solution)/shard_map/ppermute | solution.py:500
  9.6 1.3 collective-permute-start.1
  10.9 1.9 %collective-permute-start = (bf16[3,64,128]{2,1,0:T(8,128)(2,1)S(1)}, bf16[3,64,128]{2,1,0:T(8,128)(2,1)S(1)}, u32[]{:S(2)}, u32[]{:S(2)}) collective-permute-start(bf16[3,64,128]{2,1,0:T(8,128)(2,1)S(1)} %get-tuple-element.43), channel_id=1, source_target_pairs={{64,32},{32,64},{65,33},{33,65},{66,34},{34,66},{67,35},{35,67},{6... | collective-permute-start | bytes 147464 | tf_op jit(solution)/shard_map/ppermute | solution.py:498
  14.5 3.3 %collective-permute-done = bf16[3,64,128]{2,1,0:T(8,128)(2,1)S(1)} collective-permute-done((bf16[3,64,128]{2,1,0:T(8,128)(2,1)S(1)}, bf16[3,64,128]{2,1,0:T(8,128)(2,1)S(1)}, u32[]{:S(2)}, u32[]{:S(2)}) %collective-permute-start) | collective-permute-done | bytes 49184 | tf_op jit(solution)/shard_map/ppermute | solution.py:498
  17.9 1.3 collective-permute-start.2
  19.3 1.3 collective-permute-start.9
  20.6 4.0 %collective-permute-start.8 = (f32[6,8,24,128]{3,2,1,0:T(8,128)S(1)}, f32[6,8,24,128]{3,2,1,0:T(8,128)S(1)}, u32[]{:S(2)}, u32[]{:S(2)}) collective-permute-start(f32[6,8,24,128]{3,2,1,0:T(8,128)S(1)} %pad_maximum_fusion.3), channel_id=1, source_target_pairs={{0,1},{1,2},{2,3},{3,4},{4,5},{5,6},{6,7},{7,8},{8,9},{9,10},{10,1... | collective-permute-start | bytes 1769480 | tf_op jit(solution)/shard_map/ppermute | solution.py:510
  24.7 2.8 %collective-permute-start.4 = (bf16[2,9,64,128]{3,2,1,0:T(8,128)(2,1)S(1)}, bf16[2,9,64,128]{3,2,1,0:T(8,128)(2,1)S(1)}, u32[]{:S(2)}, u32[]{:S(2)}) collective-permute-start(bf16[2,9,64,128]{3,2,1,0:T(8,128)(2,1)S(1)} %get-tuple-element.39), channel_id=1, source_target_pairs={{0,8},{1,9},{2,10},{3,11},{4,12},{5,13},{6,14},{7,15},{8,0},{9,1},... | collective-permute-start | bytes 884744 | tf_op jit(solution)/shard_map/ppermute | solution.py:358
  27.5 1.9 %collective-permute-start.3 = (bf16[2,9,64,128]{3,2,1,0:T(8,128)(2,1)S(1)}, bf16[2,9,64,128]{3,2,1,0:T(8,128)(2,1)S(1)}, u32[]{:S(2)}, u32[]{:S(2)}) collective-permute-start(bf16[2,9,64,128]{3,2,1,0:T(8,128)(2,1)S(1)} %get-tuple-element.39), channel_id=1, source_target_pairs={{0,12},{1,13},{2,14},{3,15},{4,0},{5,1},{6,2},{7,3},{8,4},{9,5},{1... | collective-permute-start | bytes 884744 | tf_op jit(solution)/shard_map/ppermute | solution.py:358
  29.9 10.9 %collective-permute-done.4 = bf16[2,9,64,128]{3,2,1,0:T(8,128)(2,1)S(1)} collective-permute-done((bf16[2,9,64,128]{3,2,1,0:T(8,128)(2,1)S(1)}, bf16[2,9,64,128]{3,2,1,0:T(8,128)(2,1)S(1)}, u32[]{:S(2)}, u32[]{:S(2)}) %collective-permute-start.4) | collective-permute-done | bytes 294944 | tf_op jit(solution)/shard_map/ppermute | solution.py:358
  40.8 4.9 %collective-permute-done.5 = bf16[2,9,64,128]{3,2,1,0:T(8,128)(2,1)S(1)} collective-permute-done((bf16[2,9,64,128]{3,2,1,0:T(8,128)(2,1)S(1)}, bf16[2,9,64,128]{3,2,1,0:T(8,128)(2,1)S(1)}, u32[]{:S(2)}, u32[]{:S(2)}) %collective-permute-start.5) | collective-permute-done | bytes 294944 | tf_op jit(solution)/shard_map/ppermute | solution.py:358
  45.8 1.2 pad_maximum_fusion.2
  47.1 4.9 %collective-permute-start.11 = (bf16[4,2,9,64,128]{4,3,2,1,0:T(8,128)(2,1)}, bf16[4,2,9,64,128]{4,3,2,1,0:T(8,128)(2,1)}, u32[]{:S(2)}, u32[]{:S(2)}) collective-permute-start(bf16[4,2,9,64,128]{4,3,2,1,0:T(8,128)(2,1)} %pad_maximum_fusion.2), channel_id=1, source_target_pairs={{0,3},{1,0},{2,1},{3,2},{4,7},{5,4},{6,5},{7,6},{8,11},{9,8},{10,9... | collective-permute-start | bytes 3538952 | tf_op jit(solution)/shard_map/ppermute | solution.py:358
  52.3 13.1 %local.1 = (f32[5,8,8,128]{3,2,1,0:T(8,128)}, f32[36,8,128]{2,1,0:T(8,128)S(1)}) custom-call(s32[4]{0:T(128)S(1)} %pad_add_fusion.ints, f32[15]{0:T(128)S(1)} %reshape.520.speeds, f32[5]{0:T(128)S(1)} %copy-done.1, f32[6,24,24,128]{3,2,1,0:T(8,128)S(1)} %pad_maximum_fusion.1.fields), custom_call_target="tpu_custom_call" | custom-call | flops 4000000000 | bytes 6000000 | tf_op jit(solution)/shard_map/local/pallas_call | solution.py:455
  65.7 2.9 %collective-permute-done.10 = bf16[4,2,9,64,128]{4,3,2,1,0:T(8,128)(2,1)} collective-permute-done((bf16[4,2,9,64,128]{4,3,2,1,0:T(8,128)(2,1)}, bf16[4,2,9,64,128]{4,3,2,1,0:T(8,128)(2,1)}, u32[]{:S(2)}, u32[]{:S(2)}) %collective-permute-start.10) | collective-permute-done | bytes 1179680 | tf_op jit(solution)/shard_map/ppermute | solution.py:358
  69.7 1.1 slice.36
  70.8 2.7 %collective-permute-start.13 = (bf16[2,2,9,64,128]{4,3,2,1,0:T(8,128)(2,1)S(1)}, bf16[2,2,9,64,128]{4,3,2,1,0:T(8,128)(2,1)S(1)}, u32[]{:S(2)}, u32[]{:S(2)}) collective-permute-start(bf16[2,2,9,64,128]{4,3,2,1,0:T(8,128)(2,1)S(1)} %slice.36), channel_id=1, source_target_pairs={{0,3},{1,0},{2,1},{3,2},{4,7},{5,4},{6,5},{7,6},{8,11},{9,8},{10,9... | collective-permute-start | bytes 1769480 | tf_op jit(solution)/shard_map/ppermute | solution.py:358
  73.6 1.5 collective-permute-start.15
  75.0 1.2 collective-permute-done.16
  76.3 1.2 collective-permute-done.15
  77.5 1.5 collective-permute-done.14
  78.9 2.7 %collective-permute-start.19 = (f32[36]{0:T(128)S(1)}, f32[36]{0:T(128)S(1)}, u32[]{:S(2)}, u32[]{:S(2)}) collective-permute-start(f32[36]{0:T(128)S(1)} %add_add_fusion.2), channel_id=1, source_target_pairs={{0,12},{4,0},{8,4},{12,8},{1,13},{5,1},{9,5},{13,9},{2,14},{6,2},{... | collective-permute-start | bytes 440 | tf_op jit(solution)/shard_map/ppermute | solution.py:490
  81.6 1.3 collective-permute-start.17
  82.9 2.4 %collective-permute-done.18 = f32[36]{0:T(128)S(1)} collective-permute-done((f32[36]{0:T(128)S(1)}, f32[36]{0:T(128)S(1)}, u32[]{:S(2)}, u32[]{:S(2)}) %collective-permute-start.18) | collective-permute-done | bytes 176 | tf_op jit(solution)/shard_map/ppermute | solution.py:490
  85.7 3.9 %pad_maximum_fusion = bf16[4,4,2,9,64,128]{5,4,3,2,1,0:T(8,128)(2,1)} fusion(bf16[1,4,2,9,64,128]{5,4,3,2,1,0:T(8,128)(2,1)} %bitcast.34, bf16[1,4,2,9,64,128]{5,4,3,2,1,0:T(8,128)(2,1)S(1)} %maximum_bitcast_fusion, bf16[1,4,2,9,64,128]{5,4,3,2,1,0:T(8,128)(2,1)} %bitcast.32, bf16[1,4,2,9,64,128]{5,4,3,2,1,0:T(8,128)(2,1)} %bitcast.31), kind=kLoop, calls=%fused_computation.1 | loop fusion | flops 7077888 | bytes 9437184 | tf_op jit(solution)/shard_map/stack | solution.py:527
  89.6 2.1 %collective-permute-start.24 = (bf16[32,9,64,128]{3,2,1,0:T(8,128)(2,1)}, bf16[32,9,64,128]{3,2,1,0:T(8,128)(2,1)}, u32[]{:S(2)}, u32[]{:S(2)}) collective-permute-start(bf16[32,9,64,128]{3,2,1,0:T(8,128)(2,1)} %bitcast.35.nu_own.nu_third.q_own.q_ta), channel_id=1, source_target_pairs={{0,32},{32,0},{1,33},{33,1},{2,34},{34,2},{3,35},{35,3},{4,36},{36... | collective-permute-start | bytes 14155784 | tf_op jit(solution)/shard_map/ppermute | solution.py:362
  92.6 5.1 %collective-permute-start.22 = (f32[36]{0:T(128)S(1)}, f32[36]{0:T(128)S(1)}, u32[]{:S(2)}, u32[]{:S(2)}) collective-permute-start(f32[36]{0:T(128)S(1)} %add_add_fusion.1), channel_id=1, source_target_pairs={{0,80},{16,0},{64,16},{80,64},{1,81},{17,1},{65,17},{81,65},{2,82}... | collective-permute-start | bytes 440 | tf_op jit(solution)/shard_map/ppermute | solution.py:490
  97.7 1.4 collective-permute-start.20
  99.0 2.3 %collective-permute-done.21 = f32[36]{0:T(128)S(1)} collective-permute-done((f32[36]{0:T(128)S(1)}, f32[36]{0:T(128)S(1)}, u32[]{:S(2)}, u32[]{:S(2)}) %collective-permute-start.21) | collective-permute-done | bytes 176 | tf_op jit(solution)/shard_map/ppermute | solution.py:490
  101.6 1.4 collective-permute-start.23
  106.7 84.9 %evolve.1 = bf16[8,5,16,128,128]{4,3,2,1,0:T(8,128)(2,1)} custom-call(s32[67]{0:T(128)} %concatenate.31.ints, f32[15]{0:T(128)} %copy-done, bf16[256,256]{1,0:T(8,128)(2,1)} %convert_element_type.49.matrix_ref, bf16[256,512]{1,0:T(8,128)(2,1)} %constant.120.clone.shift_ref, bf16[32,9,64,128]{3,2,1,0:T(8,128)(2,1)} %bitcast.35.nu_own.nu_third.q_own.q_ta, ...), custom_call_target="tpu_custom_call" | custom-call | flops 399999991808 | bytes 40000000 | tf_op jit(solution)/shard_map/evolve/pallas_call | solution.py:320
  (87 shorter events, 11.4 us)
Async XLA Ops:
  0.6 18.6 %copy-start.2 = (f32[5,8,8,128]{3,2,1,0:T(8,128)S(1)}, f32[5,8,8,128]{3,2,1,0:T(8,128)}, u32[]{:S(2)}) copy-start(f32[5,8,8,128]{3,2,1,0:T(8,128)} %param.8) | copy-start | bytes 491524
  0.6 18.6 %copy-start.3 = (f32[8,8,128]{2,1,0:T(8,128)S(1)}, f32[8,8,128]{2,1,0:T(8,128)}, u32[]{:S(2)}) copy-start(f32[8,8,128]{2,1,0:T(8,128)} %param.9) | copy-start | bytes 98308
  1.6 17.6 %collective-permute-start.6 = (f32[6,8,8,128]{3,2,1,0:T(8,128)S(1)}, f32[6,8,8,128]{3,2,1,0:T(8,128)S(1)}, u32[]{:S(2)}, u32[]{:S(2)}) collective-permute-start(f32[6,8,8,128]{3,2,1,0:T(8,128)S(1)} %pad_maximum_fusion.5), channel_id=1, source_target_pairs={{0,32},{32,0},{1,33},{33,1},{2,34},{34,2},{3,35},{35,3},{4,36},{36... | collective-permute-start | bytes 589832 | tf_op jit(solution)/shard_map/ppermute | solution.py:362
  3.1 16.1 %collective-permute-start.7 = (f32[6,8,8,128]{3,2,1,0:T(8,128)S(1)}, f32[6,8,8,128]{3,2,1,0:T(8,128)S(1)}, u32[]{:S(2)}, u32[]{:S(2)}) collective-permute-start(f32[6,8,8,128]{3,2,1,0:T(8,128)S(1)} %pad_maximum_fusion.5), channel_id=1, source_target_pairs={{32,64},{64,32},{33,65},{65,33},{34,66},{66,34},{35,67},{67,35},{3... | collective-permute-start | bytes 589832 | tf_op jit(solution)/shard_map/ppermute | solution.py:500
  9.6 4.9 %collective-permute-start.1 = (bf16[3,64,128]{2,1,0:T(8,128)(2,1)S(1)}, bf16[3,64,128]{2,1,0:T(8,128)(2,1)S(1)}, u32[]{:S(2)}, u32[]{:S(2)}) collective-permute-start(bf16[3,64,128]{2,1,0:T(8,128)(2,1)S(1)} %get-tuple-element.42), channel_id=1, source_target_pairs={{64,0},{32,96},{65,1},{33,97},{66,2},{34,98},{67,3},{35,99},{68,4}... | collective-permute-start | bytes 147464 | tf_op jit(solution)/shard_map/ppermute | solution.py:499
  10.9 7.0 %collective-permute-start = (bf16[3,64,128]{2,1,0:T(8,128)(2,1)S(1)}, bf16[3,64,128]{2,1,0:T(8,128)(2,1)S(1)}, u32[]{:S(2)}, u32[]{:S(2)}) collective-permute-start(bf16[3,64,128]{2,1,0:T(8,128)(2,1)S(1)} %get-tuple-element.43), channel_id=1, source_target_pairs={{64,32},{32,64},{65,33},{33,65},{66,34},{34,66},{67,35},{35,67},{6... | collective-permute-start | bytes 147464 | tf_op jit(solution)/shard_map/ppermute | solution.py:498
  17.9 6.7 %collective-permute-start.2 = (bf16[9,64,128]{2,1,0:T(8,128)(2,1)S(1)}, bf16[9,64,128]{2,1,0:T(8,128)(2,1)S(1)}, u32[]{:S(2)}, u32[]{:S(2)}) collective-permute-start(bf16[9,64,128]{2,1,0:T(8,128)(2,1)S(1)} %get-tuple-element.41), channel_id=1, source_target_pairs={{0,16},{16,0},{1,17},{17,1},{2,18},{18,2},{3,19},{19,3},{4,20},{20... | collective-permute-start | bytes 442376 | tf_op jit(solution)/shard_map/ppermute | solution.py:503
  19.3 27.6 %collective-permute-start.9 = (f32[6,8,24,128]{3,2,1,0:T(8,128)S(1)}, f32[6,8,24,128]{3,2,1,0:T(8,128)S(1)}, u32[]{:S(2)}, u32[]{:S(2)}) collective-permute-start(f32[6,8,24,128]{3,2,1,0:T(8,128)S(1)} %pad_maximum_fusion.3), channel_id=1, source_target_pairs={{1,0},{2,1},{3,2},{4,3},{5,4},{6,5},{7,6},{8,7},{9,8},{10,9},{11,1... | collective-permute-start | bytes 1769480 | tf_op jit(solution)/shard_map/ppermute | solution.py:511
  20.6 26.4 %collective-permute-start.8 = (f32[6,8,24,128]{3,2,1,0:T(8,128)S(1)}, f32[6,8,24,128]{3,2,1,0:T(8,128)S(1)}, u32[]{:S(2)}, u32[]{:S(2)}) collective-permute-start(f32[6,8,24,128]{3,2,1,0:T(8,128)S(1)} %pad_maximum_fusion.3), channel_id=1, source_target_pairs={{0,1},{1,2},{2,3},{3,4},{4,5},{5,6},{6,7},{7,8},{8,9},{9,10},{10,1... | collective-permute-start | bytes 1769480 | tf_op jit(solution)/shard_map/ppermute | solution.py:510
  24.7 16.1 %collective-permute-start.4 = (bf16[2,9,64,128]{3,2,1,0:T(8,128)(2,1)S(1)}, bf16[2,9,64,128]{3,2,1,0:T(8,128)(2,1)S(1)}, u32[]{:S(2)}, u32[]{:S(2)}) collective-permute-start(bf16[2,9,64,128]{3,2,1,0:T(8,128)(2,1)S(1)} %get-tuple-element.39), channel_id=1, source_target_pairs={{0,8},{1,9},{2,10},{3,11},{4,12},{5,13},{6,14},{7,15},{8,0},{9,1},... | collective-permute-start | bytes 884744 | tf_op jit(solution)/shard_map/ppermute | solution.py:358
  27.5 13.4 %collective-permute-start.3 = (bf16[2,9,64,128]{3,2,1,0:T(8,128)(2,1)S(1)}, bf16[2,9,64,128]{3,2,1,0:T(8,128)(2,1)S(1)}, u32[]{:S(2)}, u32[]{:S(2)}) collective-permute-start(bf16[2,9,64,128]{3,2,1,0:T(8,128)(2,1)S(1)} %get-tuple-element.39), channel_id=1, source_target_pairs={{0,12},{1,13},{2,14},{3,15},{4,0},{5,1},{6,2},{7,3},{8,4},{9,5},{1... | collective-permute-start | bytes 884744 | tf_op jit(solution)/shard_map/ppermute | solution.py:358
  29.4 16.4 %collective-permute-start.5 = (bf16[2,9,64,128]{3,2,1,0:T(8,128)(2,1)S(1)}, bf16[2,9,64,128]{3,2,1,0:T(8,128)(2,1)S(1)}, u32[]{:S(2)}, u32[]{:S(2)}) collective-permute-start(bf16[2,9,64,128]{3,2,1,0:T(8,128)(2,1)S(1)} %get-tuple-element.39), channel_id=1, source_target_pairs={{0,4},{1,5},{2,6},{3,7},{4,8},{5,9},{6,10},{7,11},{8,12},{9,13},{1... | collective-permute-start | bytes 884744 | tf_op jit(solution)/shard_map/ppermute | solution.py:358
  46.9 5.3 %copy-start.1 = (f32[5]{0:T(128)S(1)}, f32[5]{0:T(128)}, u32[]{:S(2)}) copy-start(f32[5]{0:T(128)} %weights.1) | copy-start | bytes 64
  47.1 18.6 %collective-permute-start.11 = (bf16[4,2,9,64,128]{4,3,2,1,0:T(8,128)(2,1)}, bf16[4,2,9,64,128]{4,3,2,1,0:T(8,128)(2,1)}, u32[]{:S(2)}, u32[]{:S(2)}) collective-permute-start(bf16[4,2,9,64,128]{4,3,2,1,0:T(8,128)(2,1)} %pad_maximum_fusion.2), channel_id=1, source_target_pairs={{0,3},{1,0},{2,1},{3,2},{4,7},{5,4},{6,5},{7,6},{8,11},{9,8},{10,9... | collective-permute-start | bytes 3538952 | tf_op jit(solution)/shard_map/ppermute | solution.py:358
  52.0 16.6 %collective-permute-start.10 = (bf16[4,2,9,64,128]{4,3,2,1,0:T(8,128)(2,1)}, bf16[4,2,9,64,128]{4,3,2,1,0:T(8,128)(2,1)}, u32[]{:S(2)}, u32[]{:S(2)}) collective-permute-start(bf16[4,2,9,64,128]{4,3,2,1,0:T(8,128)(2,1)} %pad_maximum_fusion.2), channel_id=1, source_target_pairs={{0,1},{1,2},{2,3},{3,0},{4,5},{5,6},{6,7},{7,4},{8,9},{9,10},{10,1... | collective-permute-start | bytes 3538952 | tf_op jit(solution)/shard_map/ppermute | solution.py:358
  52.2 13.2 %copy-start = (f32[15]{0:T(128)}, f32[15]{0:T(128)S(1)}, u32[]{:S(2)}) copy-start(f32[15]{0:T(128)S(1)} %reshape.520.speeds) | copy-start | bytes 184
  70.8 14.8 %collective-permute-start.13 = (bf16[2,2,9,64,128]{4,3,2,1,0:T(8,128)(2,1)S(1)}, bf16[2,2,9,64,128]{4,3,2,1,0:T(8,128)(2,1)S(1)}, u32[]{:S(2)}, u32[]{:S(2)}) collective-permute-start(bf16[2,2,9,64,128]{4,3,2,1,0:T(8,128)(2,1)S(1)} %slice.36), channel_id=1, source_target_pairs={{0,3},{1,0},{2,1},{3,2},{4,7},{5,4},{6,5},{7,6},{8,11},{9,8},{10,9... | collective-permute-start | bytes 1769480 | tf_op jit(solution)/shard_map/ppermute | solution.py:358
  73.5 12.0 %collective-permute-start.12 = (bf16[2,2,9,64,128]{4,3,2,1,0:T(8,128)(2,1)S(1)}, bf16[2,2,9,64,128]{4,3,2,1,0:T(8,128)(2,1)S(1)}, u32[]{:S(2)}, u32[]{:S(2)}) collective-permute-start(bf16[2,2,9,64,128]{4,3,2,1,0:T(8,128)(2,1)S(1)} %slice.35), channel_id=1, source_target_pairs={{0,1},{1,2},{2,3},{3,0},{4,5},{5,6},{6,7},{7,4},{8,9},{9,10},{10,1... | collective-permute-start | bytes 1769480 | tf_op jit(solution)/shard_map/ppermute | solution.py:358
  73.5 2.7 %collective-permute-start.16 = (f32[36]{0:T(128)S(1)}, f32[36]{0:T(128)S(1)}, u32[]{:S(2)}, u32[]{:S(2)}) collective-permute-start(f32[36]{0:T(128)S(1)} %broadcast_multiply_fusion), channel_id=1, source_target_pairs={{0,3},{1,0},{2,1},{3,2},{4,7},{5,4},{6,5},{7,6},{8,11},{9,8},{10,9... | collective-permute-start | bytes 440 | tf_op jit(solution)/shard_map/ppermute | solution.py:490
  73.6 3.9 %collective-permute-start.15 = (f32[36]{0:T(128)S(1)}, f32[36]{0:T(128)S(1)}, u32[]{:S(2)}, u32[]{:S(2)}) collective-permute-start(f32[36]{0:T(128)S(1)} %broadcast_multiply_fusion), channel_id=1, source_target_pairs={{0,1},{1,2},{2,3},{3,0},{4,5},{5,6},{6,7},{7,4},{8,9},{9,10},{10,1... | collective-permute-start | bytes 440 | tf_op jit(solution)/shard_map/ppermute | solution.py:490
  75.0 3.9 %collective-permute-start.14 = (f32[36]{0:T(128)S(1)}, f32[36]{0:T(128)S(1)}, u32[]{:S(2)}, u32[]{:S(2)}) collective-permute-start(f32[36]{0:T(128)S(1)} %broadcast_multiply_fusion), channel_id=1, source_target_pairs={{0,2},{1,3},{2,0},{3,1},{4,6},{5,7},{6,4},{7,5},{8,10},{9,11},{10,... | collective-permute-start | bytes 440 | tf_op jit(solution)/shard_map/ppermute | solution.py:490
  78.9 3.9 %collective-permute-start.19 = (f32[36]{0:T(128)S(1)}, f32[36]{0:T(128)S(1)}, u32[]{:S(2)}, u32[]{:S(2)}) collective-permute-start(f32[36]{0:T(128)S(1)} %add_add_fusion.2), channel_id=1, source_target_pairs={{0,12},{4,0},{8,4},{12,8},{1,13},{5,1},{9,5},{13,9},{2,14},{6,2},{... | collective-permute-start | bytes 440 | tf_op jit(solution)/shard_map/ppermute | solution.py:490
  81.6 3.6 %collective-permute-start.18 = (f32[36]{0:T(128)S(1)}, f32[36]{0:T(128)S(1)}, u32[]{:S(2)}, u32[]{:S(2)}) collective-permute-start(f32[36]{0:T(128)S(1)} %add_add_fusion.2), channel_id=1, source_target_pairs={{0,4},{4,8},{8,12},{12,0},{1,5},{5,9},{9,13},{13,1},{2,6},{6,10},{... | collective-permute-start | bytes 440 | tf_op jit(solution)/shard_map/ppermute | solution.py:490
  81.6 3.9 %collective-permute-start.17 = (f32[36]{0:T(128)S(1)}, f32[36]{0:T(128)S(1)}, u32[]{:S(2)}, u32[]{:S(2)}) collective-permute-start(f32[36]{0:T(128)S(1)} %add_add_fusion.2), channel_id=1, source_target_pairs={{0,8},{4,12},{8,0},{12,4},{1,9},{5,13},{9,1},{13,5},{2,10},{6,14},... | collective-permute-start | bytes 440 | tf_op jit(solution)/shard_map/ppermute | solution.py:490
  85.7 6.0 %copy-start.4 = (s32[2,6]{1,0:T(2,128)S(1)}, s32[2,6]{1,0:T(2,128)}, u32[]{:S(2)}) copy-start(s32[2,6]{1,0:T(2,128)} %param.12) | copy-start | bytes 148
  85.7 6.0 %copy-start.6 = (s32[2]{0:T(128)S(1)}, s32[2]{0:T(128)}, u32[]{:S(2)}) copy-start(s32[2]{0:T(128)} %param.13) | copy-start | bytes 28
  85.7 6.8 %copy-start.7 = (s32[64]{0:T(128)S(1)}, s32[64]{0:T(128)}, u32[]{:S(2)}) copy-start(s32[64]{0:T(128)} %constant.127) | copy-start | bytes 772
  89.6 17.2 %collective-permute-start.24 = (bf16[32,9,64,128]{3,2,1,0:T(8,128)(2,1)}, bf16[32,9,64,128]{3,2,1,0:T(8,128)(2,1)}, u32[]{:S(2)}, u32[]{:S(2)}) collective-permute-start(bf16[32,9,64,128]{3,2,1,0:T(8,128)(2,1)} %bitcast.35.nu_own.nu_third.q_own.q_ta), channel_id=1, source_target_pairs={{0,32},{32,0},{1,33},{33,1},{2,34},{34,2},{3,35},{35,3},{4,36},{36... | collective-permute-start | bytes 14155784 | tf_op jit(solution)/shard_map/ppermute | solution.py:362
  92.6 6.5 %collective-permute-start.22 = (f32[36]{0:T(128)S(1)}, f32[36]{0:T(128)S(1)}, u32[]{:S(2)}, u32[]{:S(2)}) collective-permute-start(f32[36]{0:T(128)S(1)} %add_add_fusion.1), channel_id=1, source_target_pairs={{0,80},{16,0},{64,16},{80,64},{1,81},{17,1},{65,17},{81,65},{2,82}... | collective-permute-start | bytes 440 | tf_op jit(solution)/shard_map/ppermute | solution.py:490
  97.7 3.6 %collective-permute-start.21 = (f32[36]{0:T(128)S(1)}, f32[36]{0:T(128)S(1)}, u32[]{:S(2)}, u32[]{:S(2)}) collective-permute-start(f32[36]{0:T(128)S(1)} %add_add_fusion.1), channel_id=1, source_target_pairs={{0,16},{16,64},{64,80},{80,0},{1,17},{17,65},{65,81},{81,1},{2,18}... | collective-permute-start | bytes 440 | tf_op jit(solution)/shard_map/ppermute | solution.py:490
  97.7 3.9 %collective-permute-start.20 = (f32[36]{0:T(128)S(1)}, f32[36]{0:T(128)S(1)}, u32[]{:S(2)}, u32[]{:S(2)}) collective-permute-start(f32[36]{0:T(128)S(1)} %add_add_fusion.1), channel_id=1, source_target_pairs={{0,64},{16,80},{64,0},{80,16},{1,65},{17,81},{65,1},{81,17},{2,66}... | collective-permute-start | bytes 440 | tf_op jit(solution)/shard_map/ppermute | solution.py:490
  101.6 2.3 %collective-permute-start.23 = (f32[36]{0:T(128)S(1)}, f32[36]{0:T(128)S(1)}, u32[]{:S(2)}, u32[]{:S(2)}) collective-permute-start(f32[36]{0:T(128)S(1)} %add_add_fusion), channel_id=1, source_target_pairs={{0,32},{32,0},{1,33},{33,1},{2,34},{34,2},{3,35},{35,3},{4,36},{36... | collective-permute-start | bytes 440 | tf_op jit(solution)/shard_map/ppermute | solution.py:362
  (1 other events, 5.1 us)

commit v4 on v3

--- a/solution.py
+++ b/solution.py
@@ -21,7 +21,6 @@
 TILES = 16
 PLANES = 26
 LOW, OWN, HIGH = 1, 9, 17
-OWN_STEP = 8
 PAIRS = [(a, b) for a in range(SNAPS) for b in range(a, SNAPS)]
 BF = jnp.bfloat16
 
@@ -141,9 +140,17 @@
                 even[third_base + k] = jnp.zeros((TILES + 2, 8, 256), BF)
                 odd[third_base + k] = jnp.zeros((TILES + 2, 8, 256), BF)
                 full[third_base + k] = jnp.zeros((TILES, 8, 256), jnp.float32)
+                full_odd[third_base + k] = jnp.zeros((TILES, 8, 256), jnp.float32)
                 return carry
 
             lax.fori_loop(0, 8, clear, 0)
+
+            def still(k, carry):
+                for coef in (axp, axm, ayp, aym, azp, azm):
+                    coef[third_base + k] = jnp.zeros((TILES, 8, 256), BF)
+                return carry
+
+            lax.fori_loop(0, 8, still, 0)
 
         load_all(nu_own, nu_par, lambda: load_section(nu_third, 0, third_base))
 
@@ -189,7 +196,13 @@
             aym[z, j] = nym[z, j] + hy
         return carry
 
-    lax.fori_loop(2, PLANES - 2, coefs, 0)
+    outer = inner == 0
+    lax.fori_loop(
+        jnp.where(outer & (third_base == LOW), OWN, 2),
+        jnp.where(outer & (third_base == HIGH), HIGH, PLANES - 2),
+        coefs,
+        0,
+    )
 
     def planes(groups, src, dst, old_ref, new_ref, keep):
         state = []
@@ -243,40 +256,12 @@
                 dst[z + k, 0] = left
                 dst[z + k, TILES + 1] = right
 
-    def step(t, src, dst, old_ref, new_ref):
-        pairs = (9 - t) // 2
-
-        @pl.when(inner == 1)
-        def _():
-            def both(k, carry):
-                planes(
-                    [(OWN - 2 - 2 * k, 2), (HIGH + 2 * k, 2)], src, dst, old_ref, new_ref, None
-                )
-                return carry
-
-            lax.fori_loop(0, pairs, both, 0)
-
-        @pl.when(inner == 0)
-        def _():
-            def one(k, carry):
-                base = jnp.where(par_base == LOW, OWN - 2 - 2 * k, HIGH + 2 * k)
-                planes([(base, 2)], src, dst, old_ref, new_ref, None)
-                return carry
-
-            lax.fori_loop(0, pairs, one, 0)
-
-        def own(k, carry):
-            planes([(OWN + OWN_STEP * k, OWN_STEP)], src, dst, old_ref, new_ref, (t - 1, OWN_STEP * k))
-            return carry
-
-        lax.fori_loop(0, 8 // OWN_STEP, own, 0)
-
-    def two_steps(k, carry):
-        step(2 * k + 1, even, odd, full, full_odd)
-        step(2 * k + 2, odd, even, full_odd, full)
-        return carry
-
-    lax.fori_loop(0, SNAPS // 2, two_steps, 0)
+    for t in range(1, SNAPS + 1):
+        refs = (even, odd, full, full_odd) if t % 2 else (odd, even, full_odd, full)
+        deep = 8 - t
+        if deep:
+            planes([(OWN - deep, deep), (HIGH, deep)], *refs, None)
+        planes([(OWN, 8)], *refs, (t - 1, 0))
 
     def project(jp, carry):
         for e in range(2):
@@ -332,7 +317,7 @@
         out_shape=jax.ShapeDtypeStruct((8, VARS, 16, 128, 128), BF),
         scratch_shapes=[
             pltpu.VMEM((2, 8, 8, 8, 256), jnp.float32),
-            pltpu.VMEM((8, TILES, 8, 512), BF),
+            pltpu.VMEM((14, TILES, 8, 512), BF),
             pltpu.VMEM((SNAPS, 8, TILES, 8, 256), BF),
             pltpu.VMEM((PLANES, TILES, 8, 256), jnp.float32),
             pltpu.VMEM((PLANES, TILES, 8, 256), jnp.float32),
@@ -497,26 +482,28 @@
     state = fields.astype(BF).reshape(VARS + 1, 64, 128)
     near = lax.ppermute(state[:3], GRP, [(2, 1), (1, 2)])
     far = lax.ppermute(state[3:], GRP, [(2, 0), (1, 3)])
+    block = jnp.concatenate([state, near + far])
+    block, fields = lax.optimization_barrier((block, fields))
+    other = lax.ppermute(block, "dev_0", [(0, 1), (1, 0)])
     third = lax.ppermute(fields, GRP, [(1, 2), (2, 1)])
     par = swap_cores(fields)
-    block = jnp.concatenate([state, near + far])
-    other = lax.ppermute(block, "dev_0", [(0, 1), (1, 0)])
 
     odd = lax.axis_index("grp_1") == 1
     column = jnp.concatenate(
         [jnp.where(odd, par, third), fields, jnp.where(odd, third, par)], axis=2
     )
+    pair = jnp.stack([block, other])
+    column, _ = lax.optimization_barrier((column, pair))
+    near_axis = [ring_shift(("y", "x"), by) for by in (-1, 2, 1)]
+    first = jnp.stack([pair] + [shift(pair) for shift in near_axis])
     up = [(i, i + 1) for i in range(31)]
     before_x = lax.ppermute(column, DEV, up)
     after_x = lax.ppermute(column, DEV, [(b, a) for a, b in up])
     cube = jnp.concatenate([before_x, column, after_x], axis=1)
 
-    pair = jnp.stack([block, other])
-    near_axis = [ring_shift(("y", "x"), by) for by in (-1, 2, 1)]
-    first = jnp.stack([pair] + [shift(pair) for shift in near_axis])
-    first, cube = lax.optimization_barrier((first, cube))
     forward, back = ring_shift(("x", "y"), 1), ring_shift(("x", "y"), -1)
     before, after = forward(first), back(first)
+    cube, _ = lax.optimization_barrier((cube, first))
     final, corr = local_steps(local_ints(), speeds, energy_weights, cube)
     sums = jnp.sum(corr, axis=(1, 2)) / CELLS
     before, after, sums = lax.optimization_barrier((before, after, sums))

time: 192 us -> 175 us (0.911)
  Pallas kernels: 97.9 us -> 81 us
  waiting for transfers between devices: 31.5 us -> 25.6 us
  starting transfers between devices: 45 us -> 50.8 us
    pallas_call x1, Pallas kernels: 84.9 us -> 68 us  [evolve(): pl.pallas_call(evolve_kernel, name='evolve', grid=(VARS,), in_specs=[smem...]
    ppermute x7, waiting for transfers between devices: 18.8 us -> 6.65 us  [ring_shift(): return lambda value: lax.ppermute(value, ('grp_1', 'dev_1', 'dev_2'), pairs)]
    ppermute x1, waiting for transfers between devices: 0.01 us -> 7.5 us  [communicate(): after_x = lax.ppermute(column, DEV, [(b, a) for a, b in up])]
    ppermute x1, starting transfers between devices: 1.29 us -> 6.32 us  [communicate(): far = lax.ppermute(state[3:], GRP, [(2, 0), (1, 3)])]
    ppermute x3, starting transfers between devices: 4.98 us -> 8.5 us  [swap_cores(): return lax.ppermute(value, 'grp_1', [(0, 1), (1, 0)])]
    ppermute x1, starting transfers between devices: 5.52 us -> 3.37 us  [communicate(): third = lax.ppermute(fields, GRP, [(1, 2), (2, 1)])]
    another operation x2 -> x3, other arithmetic: 3.97 us -> 4.82 us  [communicate(): own = jnp.stack([first, after, across, before]).reshape(32, 9, 64, 128)]
  transfers between devices with their start and end apart: 25 -> 25, of which waited for: 12 -> 12; matrix products, arithmetic and copies ran while one was open for 5% -> 6% of each run, Pallas kernels for 7% -> 8%
where the time goes in v4:
time: 175 us; the launch traced here: 174 us
  Pallas kernels  81 us (46%)
  starting transfers between devices  50.8 us (29%)
  waiting for transfers between devices  25.6 us (15%)
  other arithmetic  11.8 us (7%)
  local copies, waits for them, and re-layouts  4.16 us (2%)
    pallas_call x1, Pallas kernels, evolve(): pl.pallas_call(evolve_kernel, name='evolve', grid=(VARS,), in_specs=[smem...  68 us
    pallas_call x1, Pallas kernels, local_steps(): pl.pallas_call(local_kernel, name='local', in_specs=[smem, smem, smem, vm...  13.1 us
    ppermute x7, starting transfers between devices, ring_shift(): return lambda value: lax.ppermute(value, ('grp_1', 'dev_1', 'dev_2'), pairs)  11.7 us
    ppermute x9, starting transfers between devices, ring_sum(): lax.ppermute(value, axes, [(i, (i + by) % 4) for i in range(4)])  11.5 us
    ppermute x3, starting transfers between devices, swap_cores(): return lax.ppermute(value, 'grp_1', [(0, 1), (1, 0)])  8.5 us
    ppermute x9, waiting for transfers between devices, ring_sum(): lax.ppermute(value, axes, [(i, (i + by) % 4) for i in range(4)])  7.95 us
    ppermute x1, waiting for transfers between devices, communicate(): after_x = lax.ppermute(column, DEV, [(b, a) for a, b in up])  7.5 us
    ppermute x7, waiting for transfers between devices, ring_shift(): return lambda value: lax.ppermute(value, ('grp_1', 'dev_1', 'dev_2'), pairs)  6.65 us
  transfers between devices with their start and end apart: 25, of which 12 were waited for; matrix products, arithmetic and copies ran while one was open for 6% of the time, Pallas kernels for 8%

profile of v4, /device:TPU:1, one launch (start us, length us, event | category | flops | bytes accessed | tf_op | source)
XLA Modules:
  0.0 174.3 jit_solution(15290939445763589102)
XLA Ops:
  0.6 0.9 fusion.29
  1.6 6.3 %collective-permute-start.1 = (bf16[3,64,128]{2,1,0:T(8,128)(2,1)S(1)}, bf16[3,64,128]{2,1,0:T(8,128)(2,1)S(1)}, u32[]{:S(2)}, u32[]{:S(2)}) collective-permute-start(bf16[3,64,128]{2,1,0:T(8,128)(2,1)S(1)} %get-tuple-element.46), channel_id=1, source_target_pairs={{64,0},{32,96},{65,1},{33,97},{66,2},{34,98},{67,3},{35,99},{68,4}... | collective-permute-start | bytes 147464 | tf_op jit(solution)/shard_map/ppermute | solution.py:484
  7.9 2.0 %collective-permute-start = (bf16[3,64,128]{2,1,0:T(8,128)(2,1)S(1)}, bf16[3,64,128]{2,1,0:T(8,128)(2,1)S(1)}, u32[]{:S(2)}, u32[]{:S(2)}) collective-permute-start(bf16[3,64,128]{2,1,0:T(8,128)(2,1)S(1)} %get-tuple-element.47), channel_id=1, source_target_pairs={{64,32},{32,64},{65,33},{33,65},{66,34},{34,66},{67,35},{35,67},{6... | collective-permute-start | bytes 147464 | tf_op jit(solution)/shard_map/ppermute | solution.py:483
  12.6 2.3 %collective-permute-done = bf16[3,64,128]{2,1,0:T(8,128)(2,1)S(1)} collective-permute-done((bf16[3,64,128]{2,1,0:T(8,128)(2,1)S(1)}, bf16[3,64,128]{2,1,0:T(8,128)(2,1)S(1)}, u32[]{:S(2)}, u32[]{:S(2)}) %collective-permute-start) | collective-permute-done | bytes 49184 | tf_op jit(solution)/shard_map/ppermute | solution.py:483
  14.9 1.3 collective-permute-start.4
  16.2 3.4 %collective-permute-start.3 = (f32[6,8,8,128]{3,2,1,0:T(8,128)S(1)}, f32[6,8,8,128]{3,2,1,0:T(8,128)S(1)}, u32[]{:S(2)}, u32[]{:S(2)}) collective-permute-start(f32[6,8,8,128]{3,2,1,0:T(8,128)S(1)} %pad_maximum_fusion.5), channel_id=1, source_target_pairs={{32,64},{64,32},{33,65},{65,33},{34,66},{66,34},{35,67},{67,35},{3... | collective-permute-start | bytes 589832 | tf_op jit(solution)/shard_map/ppermute | solution.py:488
  19.8 2.8 %collective-permute-start.8 = (bf16[2,9,64,128]{3,2,1,0:T(8,128)(2,1)S(1)}, bf16[2,9,64,128]{3,2,1,0:T(8,128)(2,1)S(1)}, u32[]{:S(2)}, u32[]{:S(2)}) collective-permute-start(bf16[2,9,64,128]{3,2,1,0:T(8,128)(2,1)S(1)} %get-tuple-element.45), channel_id=1, source_target_pairs={{0,8},{1,9},{2,10},{3,11},{4,12},{5,13},{6,14},{7,15},{8,0},{9,1},... | collective-permute-start | bytes 884744 | tf_op jit(solution)/shard_map/ppermute | solution.py:343
  24.0 0.9 collective-permute-done.3
  25.1 1.3 collective-permute-start.6
  26.4 4.8 %collective-permute-start.5 = (f32[6,8,24,128]{3,2,1,0:T(8,128)S(1)}, f32[6,8,24,128]{3,2,1,0:T(8,128)}, u32[]{:S(2)}, u32[]{:S(2)}) collective-permute-start(f32[6,8,24,128]{3,2,1,0:T(8,128)S(1)} %pad_maximum_fusion.3), channel_id=1, source_target_pairs={{0,1},{1,2},{2,3},{3,4},{4,5},{5,6},{6,7},{7,8},{8,9},{9,10},{10,1... | collective-permute-start | bytes 1769480 | tf_op jit(solution)/shard_map/ppermute | solution.py:500
  31.2 1.2 fusion.31
  32.4 2.9 %collective-permute-start.11 = (bf16[4,2,9,64,128]{4,3,2,1,0:T(8,128)(2,1)}, bf16[4,2,9,64,128]{4,3,2,1,0:T(8,128)(2,1)S(1)}, u32[]{:S(2)}, u32[]{:S(2)}) collective-permute-start(bf16[4,2,9,64,128]{4,3,2,1,0:T(8,128)(2,1)} %get-tuple-element.41), channel_id=1, source_target_pairs={{0,3},{1,0},{2,1},{3,2},{4,7},{5,4},{6,5},{7,6},{8,11},{9,8},{10,9... | collective-permute-start | bytes 3538952 | tf_op jit(solution)/shard_map/ppermute | solution.py:343
  35.5 7.5 %collective-permute-done.6 = f32[6,8,24,128]{3,2,1,0:T(8,128)} collective-permute-done((f32[6,8,24,128]{3,2,1,0:T(8,128)S(1)}, f32[6,8,24,128]{3,2,1,0:T(8,128)}, u32[]{:S(2)}, u32[]{:S(2)}) %collective-permute-start.6) | collective-permute-done | bytes 589856 | tf_op jit(solution)/shard_map/ppermute | solution.py:501
  43.0 1.4 pad_maximum_fusion.1.fields
  44.4 13.1 %local.1 = (f32[5,8,8,128]{3,2,1,0:T(8,128)}, f32[36,8,128]{2,1,0:T(8,128)S(1)}) custom-call(s32[4]{0:T(128)S(1)} %pad_add_fusion.ints, f32[15]{0:T(128)S(1)} %reshape.520.speeds, f32[5]{0:T(128)S(1)} %copy-done.1, f32[6,24,24,128]{3,2,1,0:T(8,128)S(1)} %pad_maximum_fusion.1.fields), custom_call_target="tpu_custom_call" | custom-call | flops 4000000000 | bytes 6000000 | tf_op jit(solution)/shard_map/local/pallas_call | solution.py:440
  57.9 6.6 %collective-permute-done.10 = bf16[4,2,9,64,128]{4,3,2,1,0:T(8,128)(2,1)} collective-permute-done((bf16[4,2,9,64,128]{4,3,2,1,0:T(8,128)(2,1)}, bf16[4,2,9,64,128]{4,3,2,1,0:T(8,128)(2,1)}, u32[]{:S(2)}, u32[]{:S(2)}) %collective-permute-start.10) | collective-permute-done | bytes 1179680 | tf_op jit(solution)/shard_map/ppermute | solution.py:343
  64.5 1.1 slice.35
  65.7 4.6 %collective-permute-start.13 = (bf16[2,2,9,64,128]{4,3,2,1,0:T(8,128)(2,1)S(1)}, bf16[2,2,9,64,128]{4,3,2,1,0:T(8,128)(2,1)S(1)}, u32[]{:S(2)}, u32[]{:S(2)}) collective-permute-start(bf16[2,2,9,64,128]{4,3,2,1,0:T(8,128)(2,1)S(1)} %slice.36), channel_id=1, source_target_pairs={{0,3},{1,0},{2,1},{3,2},{4,7},{5,4},{6,5},{7,6},{8,11},{9,8},{10,9... | collective-permute-start | bytes 1769480 | tf_op jit(solution)/shard_map/ppermute | solution.py:343
  70.2 1.1 collective-permute-start.16
  72.9 2.4 %collective-permute-done.15 = f32[36]{0:T(128)S(1)} collective-permute-done((f32[36]{0:T(128)S(1)}, f32[36]{0:T(128)S(1)}, u32[]{:S(2)}, u32[]{:S(2)}) %collective-permute-start.15) | collective-permute-done | bytes 176 | tf_op jit(solution)/shard_map/ppermute | solution.py:475
  75.6 2.7 %collective-permute-start.19 = (f32[36]{0:T(128)S(1)}, f32[36]{0:T(128)S(1)}, u32[]{:S(2)}, u32[]{:S(2)}) collective-permute-start(f32[36]{0:T(128)S(1)} %add_add_fusion.2), channel_id=1, source_target_pairs={{0,12},{4,0},{8,4},{12,8},{1,13},{5,1},{9,5},{13,9},{2,14},{6,2},{... | collective-permute-start | bytes 440 | tf_op jit(solution)/shard_map/ppermute | solution.py:475
  78.3 1.3 collective-permute-start.17
  79.6 2.4 %collective-permute-done.18 = f32[36]{0:T(128)S(1)} collective-permute-done((f32[36]{0:T(128)S(1)}, f32[36]{0:T(128)S(1)}, u32[]{:S(2)}, u32[]{:S(2)}) %collective-permute-start.18) | collective-permute-done | bytes 176 | tf_op jit(solution)/shard_map/ppermute | solution.py:475
  82.4 3.5 %pad_maximum_fusion = bf16[4,4,2,9,64,128]{5,4,3,2,1,0:T(8,128)(2,1)} fusion(bf16[1,4,2,9,64,128]{5,4,3,2,1,0:T(8,128)(2,1)} %bitcast.34, bf16[1,4,2,9,64,128]{5,4,3,2,1,0:T(8,128)(2,1)S(1)} %maximum_bitcast_fusion, bf16[1,4,2,9,64,128]{5,4,3,2,1,0:T(8,128)(2,1)S(1)} %bitcast.93, bf16[1,4,2,9,64,128]{5,4,3,2,1,0:T(8,128)(2,1)S(1)} %get-tuple-element.40), kind=kLoop, calls=%fused_computation.1 | loop fusion | flops 7077888 | bytes 9437184 | tf_op jit(solution)/shard_map/stack | solution.py:514
  85.9 7.0 %collective-permute-start.24 = (bf16[32,9,64,128]{3,2,1,0:T(8,128)(2,1)}, bf16[32,9,64,128]{3,2,1,0:T(8,128)(2,1)}, u32[]{:S(2)}, u32[]{:S(2)}) collective-permute-start(bf16[32,9,64,128]{3,2,1,0:T(8,128)(2,1)} %bitcast.35.nu_own.nu_third.q_own.q_ta), channel_id=1, source_target_pairs={{0,32},{32,0},{1,33},{33,1},{2,34},{34,2},{3,35},{35,3},{4,36},{36... | collective-permute-start | bytes 14155784 | tf_op jit(solution)/shard_map/ppermute | solution.py:347
  93.8 2.7 %collective-permute-start.22 = (f32[36]{0:T(128)S(1)}, f32[36]{0:T(128)S(1)}, u32[]{:S(2)}, u32[]{:S(2)}) collective-permute-start(f32[36]{0:T(128)S(1)} %add_add_fusion.1), channel_id=1, source_target_pairs={{0,80},{16,0},{64,16},{80,64},{1,81},{17,1},{65,17},{81,65},{2,82}... | collective-permute-start | bytes 440 | tf_op jit(solution)/shard_map/ppermute | solution.py:475
  97.3 1.7 collective-permute-start.20
  99.0 1.2 collective-permute-done.21
  100.2 1.1 collective-permute-done.20
  101.2 1.4 collective-permute-start.23
  105.3 1.0 convert_element_type.49.matrix_ref
  106.3 68.0 %evolve.1 = bf16[8,5,16,128,128]{4,3,2,1,0:T(8,128)(2,1)} custom-call(s32[67]{0:T(128)} %concatenate.31.ints, f32[15]{0:T(128)} %copy-done, bf16[256,256]{1,0:T(8,128)(2,1)} %convert_element_type.49.matrix_ref, bf16[256,512]{1,0:T(8,128)(2,1)} %constant.120.clone.shift_ref, bf16[32,9,64,128]{3,2,1,0:T(8,128)(2,1)} %bitcast.35.nu_own.nu_third.q_own.q_ta, ...), custom_call_target="tpu_custom_call" | custom-call | flops 399999991808 | bytes 40000000 | tf_op jit(solution)/shard_map/evolve/pallas_call | solution.py:305
  (83 shorter events, 11.6 us)
Async XLA Ops:
  1.6 11.0 %collective-permute-start.1 = (bf16[3,64,128]{2,1,0:T(8,128)(2,1)S(1)}, bf16[3,64,128]{2,1,0:T(8,128)(2,1)S(1)}, u32[]{:S(2)}, u32[]{:S(2)}) collective-permute-start(bf16[3,64,128]{2,1,0:T(8,128)(2,1)S(1)} %get-tuple-element.46), channel_id=1, source_target_pairs={{64,0},{32,96},{65,1},{33,97},{66,2},{34,98},{67,3},{35,99},{68,4}... | collective-permute-start | bytes 147464 | tf_op jit(solution)/shard_map/ppermute | solution.py:484
  7.9 7.0 %collective-permute-start = (bf16[3,64,128]{2,1,0:T(8,128)(2,1)S(1)}, bf16[3,64,128]{2,1,0:T(8,128)(2,1)S(1)}, u32[]{:S(2)}, u32[]{:S(2)}) collective-permute-start(bf16[3,64,128]{2,1,0:T(8,128)(2,1)S(1)} %get-tuple-element.47), channel_id=1, source_target_pairs={{64,32},{32,64},{65,33},{33,65},{66,34},{34,66},{67,35},{35,67},{6... | collective-permute-start | bytes 147464 | tf_op jit(solution)/shard_map/ppermute | solution.py:483
  14.9 4.8 %collective-permute-start.4 = (bf16[9,64,128]{2,1,0:T(8,128)(2,1)S(1)}, bf16[9,64,128]{2,1,0:T(8,128)(2,1)S(1)}, u32[]{:S(2)}, u32[]{:S(2)}) collective-permute-start(bf16[9,64,128]{2,1,0:T(8,128)(2,1)S(1)} %pad_maximum_fusion.6), channel_id=1, source_target_pairs={{0,16},{16,0},{1,17},{17,1},{2,18},{18,2},{3,19},{19,3},{4,20},{20... | collective-permute-start | bytes 442376 | tf_op jit(solution)/shard_map/ppermute | solution.py:487
  16.2 8.8 %collective-permute-start.3 = (f32[6,8,8,128]{3,2,1,0:T(8,128)S(1)}, f32[6,8,8,128]{3,2,1,0:T(8,128)S(1)}, u32[]{:S(2)}, u32[]{:S(2)}) collective-permute-start(f32[6,8,8,128]{3,2,1,0:T(8,128)S(1)} %pad_maximum_fusion.5), channel_id=1, source_target_pairs={{32,64},{64,32},{33,65},{65,33},{34,66},{66,34},{35,67},{67,35},{3... | collective-permute-start | bytes 589832 | tf_op jit(solution)/shard_map/ppermute | solution.py:488
  19.6 5.4 %collective-permute-start.2 = (f32[6,8,8,128]{3,2,1,0:T(8,128)S(1)}, f32[6,8,8,128]{3,2,1,0:T(8,128)S(1)}, u32[]{:S(2)}, u32[]{:S(2)}) collective-permute-start(f32[6,8,8,128]{3,2,1,0:T(8,128)S(1)} %pad_maximum_fusion.5), channel_id=1, source_target_pairs={{0,32},{32,0},{1,33},{33,1},{2,34},{34,2},{3,35},{35,3},{4,36},{36... | collective-permute-start | bytes 589832 | tf_op jit(solution)/shard_map/ppermute | solution.py:347
  19.8 11.4 %collective-permute-start.8 = (bf16[2,9,64,128]{3,2,1,0:T(8,128)(2,1)S(1)}, bf16[2,9,64,128]{3,2,1,0:T(8,128)(2,1)S(1)}, u32[]{:S(2)}, u32[]{:S(2)}) collective-permute-start(bf16[2,9,64,128]{3,2,1,0:T(8,128)(2,1)S(1)} %get-tuple-element.45), channel_id=1, source_target_pairs={{0,8},{1,9},{2,10},{3,11},{4,12},{5,13},{6,14},{7,15},{8,0},{9,1},... | collective-permute-start | bytes 884744 | tf_op jit(solution)/shard_map/ppermute | solution.py:343
  22.6 8.6 %collective-permute-start.7 = (bf16[2,9,64,128]{3,2,1,0:T(8,128)(2,1)S(1)}, bf16[2,9,64,128]{3,2,1,0:T(8,128)(2,1)S(1)}, u32[]{:S(2)}, u32[]{:S(2)}) collective-permute-start(bf16[2,9,64,128]{3,2,1,0:T(8,128)(2,1)S(1)} %get-tuple-element.45), channel_id=1, source_target_pairs={{0,12},{1,13},{2,14},{3,15},{4,0},{5,1},{6,2},{7,3},{8,4},{9,5},{1... | collective-permute-start | bytes 884744 | tf_op jit(solution)/shard_map/ppermute | solution.py:343
  23.4 7.8 %collective-permute-start.9 = (bf16[2,9,64,128]{3,2,1,0:T(8,128)(2,1)S(1)}, bf16[2,9,64,128]{3,2,1,0:T(8,128)(2,1)S(1)}, u32[]{:S(2)}, u32[]{:S(2)}) collective-permute-start(bf16[2,9,64,128]{3,2,1,0:T(8,128)(2,1)S(1)} %get-tuple-element.45), channel_id=1, source_target_pairs={{0,4},{1,5},{2,6},{3,7},{4,8},{5,9},{6,10},{7,11},{8,12},{9,13},{1... | collective-permute-start | bytes 884744 | tf_op jit(solution)/shard_map/ppermute | solution.py:343
  25.1 18.0 %collective-permute-start.6 = (f32[6,8,24,128]{3,2,1,0:T(8,128)S(1)}, f32[6,8,24,128]{3,2,1,0:T(8,128)}, u32[]{:S(2)}, u32[]{:S(2)}) collective-permute-start(f32[6,8,24,128]{3,2,1,0:T(8,128)S(1)} %pad_maximum_fusion.3), channel_id=1, source_target_pairs={{1,0},{2,1},{3,2},{4,3},{5,4},{6,5},{7,6},{8,7},{9,8},{10,9},{11,1... | collective-permute-start | bytes 1769480 | tf_op jit(solution)/shard_map/ppermute | solution.py:501
  26.4 16.7 %collective-permute-start.5 = (f32[6,8,24,128]{3,2,1,0:T(8,128)S(1)}, f32[6,8,24,128]{3,2,1,0:T(8,128)}, u32[]{:S(2)}, u32[]{:S(2)}) collective-permute-start(f32[6,8,24,128]{3,2,1,0:T(8,128)S(1)} %pad_maximum_fusion.3), channel_id=1, source_target_pairs={{0,1},{1,2},{2,3},{3,4},{4,5},{5,6},{6,7},{7,8},{8,9},{9,10},{10,1... | collective-permute-start | bytes 1769480 | tf_op jit(solution)/shard_map/ppermute | solution.py:500
  31.2 4.1 %copy-start.3 = (f32[5,3]{0,1:T(4,128)S(1)}, f32[5,3]{0,1:T(4,128)}, u32[]{:S(2)}) copy-start(f32[5,3]{0,1:T(4,128)} %param.10) | copy-start | bytes 184
  32.4 25.4 %collective-permute-start.11 = (bf16[4,2,9,64,128]{4,3,2,1,0:T(8,128)(2,1)}, bf16[4,2,9,64,128]{4,3,2,1,0:T(8,128)(2,1)S(1)}, u32[]{:S(2)}, u32[]{:S(2)}) collective-permute-start(bf16[4,2,9,64,128]{4,3,2,1,0:T(8,128)(2,1)} %get-tuple-element.41), channel_id=1, source_target_pairs={{0,3},{1,0},{2,1},{3,2},{4,7},{5,4},{6,5},{7,6},{8,11},{9,8},{10,9... | collective-permute-start | bytes 3538952 | tf_op jit(solution)/shard_map/ppermute | solution.py:343
  35.3 29.2 %collective-permute-start.10 = (bf16[4,2,9,64,128]{4,3,2,1,0:T(8,128)(2,1)}, bf16[4,2,9,64,128]{4,3,2,1,0:T(8,128)(2,1)}, u32[]{:S(2)}, u32[]{:S(2)}) collective-permute-start(bf16[4,2,9,64,128]{4,3,2,1,0:T(8,128)(2,1)} %get-tuple-element.41), channel_id=1, source_target_pairs={{0,1},{1,2},{2,3},{3,0},{4,5},{5,6},{6,7},{7,4},{8,9},{9,10},{10,1... | collective-permute-start | bytes 3538952 | tf_op jit(solution)/shard_map/ppermute | solution.py:343
  35.5 9.0 %copy-start = (f32[15]{0:T(128)}, f32[15]{0:T(128)S(1)}, u32[]{:S(2)}) copy-start(f32[15]{0:T(128)S(1)} %reshape.520.speeds) | copy-start | bytes 184
  35.5 8.9 %copy-start.1 = (f32[5]{0:T(128)S(1)}, f32[5]{0:T(128)}, u32[]{:S(2)}) copy-start(f32[5]{0:T(128)} %weights.1) | copy-start | bytes 64
  65.7 16.6 %collective-permute-start.13 = (bf16[2,2,9,64,128]{4,3,2,1,0:T(8,128)(2,1)S(1)}, bf16[2,2,9,64,128]{4,3,2,1,0:T(8,128)(2,1)S(1)}, u32[]{:S(2)}, u32[]{:S(2)}) collective-permute-start(bf16[2,2,9,64,128]{4,3,2,1,0:T(8,128)(2,1)S(1)} %slice.36), channel_id=1, source_target_pairs={{0,3},{1,0},{2,1},{3,2},{4,7},{5,4},{6,5},{7,6},{8,11},{9,8},{10,9... | collective-permute-start | bytes 1769480 | tf_op jit(solution)/shard_map/ppermute | solution.py:343
  70.2 12.0 %collective-permute-start.12 = (bf16[2,2,9,64,128]{4,3,2,1,0:T(8,128)(2,1)S(1)}, bf16[2,2,9,64,128]{4,3,2,1,0:T(8,128)(2,1)S(1)}, u32[]{:S(2)}, u32[]{:S(2)}) collective-permute-start(bf16[2,2,9,64,128]{4,3,2,1,0:T(8,128)(2,1)S(1)} %slice.35), channel_id=1, source_target_pairs={{0,1},{1,2},{2,3},{3,0},{4,5},{5,6},{6,7},{7,4},{8,9},{9,10},{10,1... | collective-permute-start | bytes 1769480 | tf_op jit(solution)/shard_map/ppermute | solution.py:343
  70.2 2.7 %collective-permute-start.16 = (f32[36]{0:T(128)S(1)}, f32[36]{0:T(128)S(1)}, u32[]{:S(2)}, u32[]{:S(2)}) collective-permute-start(f32[36]{0:T(128)S(1)} %broadcast_multiply_fusion), channel_id=1, source_target_pairs={{0,3},{1,0},{2,1},{3,2},{4,7},{5,4},{6,5},{7,6},{8,11},{9,8},{10,9... | collective-permute-start | bytes 440 | tf_op jit(solution)/shard_map/ppermute | solution.py:475
  71.4 3.9 %collective-permute-start.15 = (f32[36]{0:T(128)S(1)}, f32[36]{0:T(128)S(1)}, u32[]{:S(2)}, u32[]{:S(2)}) collective-permute-start(f32[36]{0:T(128)S(1)} %broadcast_multiply_fusion), channel_id=1, source_target_pairs={{0,1},{1,2},{2,3},{3,0},{4,5},{5,6},{6,7},{7,4},{8,9},{9,10},{10,1... | collective-permute-start | bytes 440 | tf_op jit(solution)/shard_map/ppermute | solution.py:475
  71.7 3.9 %collective-permute-start.14 = (f32[36]{0:T(128)S(1)}, f32[36]{0:T(128)S(1)}, u32[]{:S(2)}, u32[]{:S(2)}) collective-permute-start(f32[36]{0:T(128)S(1)} %broadcast_multiply_fusion), channel_id=1, source_target_pairs={{0,2},{1,3},{2,0},{3,1},{4,6},{5,7},{6,4},{7,5},{8,10},{9,11},{10,... | collective-permute-start | bytes 440 | tf_op jit(solution)/shard_map/ppermute | solution.py:475
  75.6 3.9 %collective-permute-start.19 = (f32[36]{0:T(128)S(1)}, f32[36]{0:T(128)S(1)}, u32[]{:S(2)}, u32[]{:S(2)}) collective-permute-start(f32[36]{0:T(128)S(1)} %add_add_fusion.2), channel_id=1, source_target_pairs={{0,12},{4,0},{8,4},{12,8},{1,13},{5,1},{9,5},{13,9},{2,14},{6,2},{... | collective-permute-start | bytes 440 | tf_op jit(solution)/shard_map/ppermute | solution.py:475
  78.3 3.6 %collective-permute-start.18 = (f32[36]{0:T(128)S(1)}, f32[36]{0:T(128)S(1)}, u32[]{:S(2)}, u32[]{:S(2)}) collective-permute-start(f32[36]{0:T(128)S(1)} %add_add_fusion.2), channel_id=1, source_target_pairs={{0,4},{4,8},{8,12},{12,0},{1,5},{5,9},{9,13},{13,1},{2,6},{6,10},{... | collective-permute-start | bytes 440 | tf_op jit(solution)/shard_map/ppermute | solution.py:475
  78.3 3.9 %collective-permute-start.17 = (f32[36]{0:T(128)S(1)}, f32[36]{0:T(128)S(1)}, u32[]{:S(2)}, u32[]{:S(2)}) collective-permute-start(f32[36]{0:T(128)S(1)} %add_add_fusion.2), channel_id=1, source_target_pairs={{0,8},{4,12},{8,0},{12,4},{1,9},{5,13},{9,1},{13,5},{2,10},{6,14},... | collective-permute-start | bytes 440 | tf_op jit(solution)/shard_map/ppermute | solution.py:475
  82.4 10.6 %copy-start.2 = (s32[2,6]{1,0:T(2,128)S(1)}, s32[2,6]{1,0:T(2,128)}, u32[]{:S(2)}) copy-start(s32[2,6]{1,0:T(2,128)} %param.12) | copy-start | bytes 148
  82.4 10.6 %copy-start.4 = (s32[2]{0:T(128)S(1)}, s32[2]{0:T(128)}, u32[]{:S(2)}) copy-start(s32[2]{0:T(128)} %param.13) | copy-start | bytes 28
  82.4 11.4 %copy-start.5 = (s32[64]{0:T(128)S(1)}, s32[64]{0:T(128)}, u32[]{:S(2)}) copy-start(s32[64]{0:T(128)} %constant.127) | copy-start | bytes 772
  85.9 20.4 %collective-permute-start.24 = (bf16[32,9,64,128]{3,2,1,0:T(8,128)(2,1)}, bf16[32,9,64,128]{3,2,1,0:T(8,128)(2,1)}, u32[]{:S(2)}, u32[]{:S(2)}) collective-permute-start(bf16[32,9,64,128]{3,2,1,0:T(8,128)(2,1)} %bitcast.35.nu_own.nu_third.q_own.q_ta), channel_id=1, source_target_pairs={{0,32},{32,0},{1,33},{33,1},{2,34},{34,2},{3,35},{35,3},{4,36},{36... | collective-permute-start | bytes 14155784 | tf_op jit(solution)/shard_map/ppermute | solution.py:347
  93.8 5.2 %collective-permute-start.22 = (f32[36]{0:T(128)S(1)}, f32[36]{0:T(128)S(1)}, u32[]{:S(2)}, u32[]{:S(2)}) collective-permute-start(f32[36]{0:T(128)S(1)} %add_add_fusion.1), channel_id=1, source_target_pairs={{0,80},{16,0},{64,16},{80,64},{1,81},{17,1},{65,17},{81,65},{2,82}... | collective-permute-start | bytes 440 | tf_op jit(solution)/shard_map/ppermute | solution.py:475
  96.5 3.6 %collective-permute-start.21 = (f32[36]{0:T(128)S(1)}, f32[36]{0:T(128)S(1)}, u32[]{:S(2)}, u32[]{:S(2)}) collective-permute-start(f32[36]{0:T(128)S(1)} %add_add_fusion.1), channel_id=1, source_target_pairs={{0,16},{16,64},{64,80},{80,0},{1,17},{17,65},{65,81},{81,1},{2,18}... | collective-permute-start | bytes 440 | tf_op jit(solution)/shard_map/ppermute | solution.py:475
  97.3 3.9 %collective-permute-start.20 = (f32[36]{0:T(128)S(1)}, f32[36]{0:T(128)S(1)}, u32[]{:S(2)}, u32[]{:S(2)}) collective-permute-start(f32[36]{0:T(128)S(1)} %add_add_fusion.1), channel_id=1, source_target_pairs={{0,64},{16,80},{64,0},{80,16},{1,65},{17,81},{65,1},{81,17},{2,66}... | collective-permute-start | bytes 440 | tf_op jit(solution)/shard_map/ppermute | solution.py:475
  101.2 2.3 %collective-permute-start.23 = (f32[36]{0:T(128)S(1)}, f32[36]{0:T(128)S(1)}, u32[]{:S(2)}, u32[]{:S(2)}) collective-permute-start(f32[36]{0:T(128)S(1)} %add_add_fusion), channel_id=1, source_target_pairs={{0,32},{32,0},{1,33},{33,1},{2,34},{34,2},{3,35},{35,3},{4,36},{36... | collective-permute-start | bytes 440 | tf_op jit(solution)/shard_map/ppermute | solution.py:347

commit v5 on v4

--- a/solution.py
+++ b/solution.py
@@ -508,12 +508,12 @@
     sums = jnp.sum(corr, axis=(1, 2)) / CELLS
     before, after, sums = lax.optimization_barrier((before, after, sums))
     half_before, half_after = forward(before[:2]), back(after[2:])
-    sums = ring_sum(ring_sum(sums, "dev_2"), "dev_1")
+    sums = ring_sum(sums, "dev_2")
     half_before, half_after, sums = lax.optimization_barrier((half_before, half_after, sums))
     across = jnp.concatenate([half_before, half_after])
     own = jnp.stack([first, after, across, before]).reshape(32, 9, 64, 128)
     partner = swap_cores(own)
-    sums = ring_sum(sums, ("grp_0", "dev_0"))
+    sums = ring_sum(ring_sum(sums, "dev_1"), ("grp_0", "dev_0"))
     sums = sums + swap_cores(sums)
     return own, partner, final, sums
 

time: 175 us -> 175 us (level)
  starting transfers between devices: 50.8 us -> 46.2 us
  waiting for transfers between devices: 25.6 us -> 30.1 us
    ppermute x3, starting transfers between devices: 8.5 us -> 3.23 us  [swap_cores(): return lax.ppermute(value, 'grp_1', [(0, 1), (1, 0)])]
    ppermute x7, waiting for transfers between devices: 6.65 us -> 11.2 us  [ring_shift(): return lambda value: lax.ppermute(value, ('grp_1', 'dev_1', 'dev_2'), pairs)]
  transfers between devices with their start and end apart: 25 -> 25, of which waited for: 12 -> 14; matrix products, arithmetic and copies ran while one was open for 6% -> 6% of each run, Pallas kernels for 8% -> 8%
where the time goes in v5:
time: 175 us; the launch traced here: 174 us
  Pallas kernels  81 us (46%)
  starting transfers between devices  46.2 us (26%)
  waiting for transfers between devices  30.1 us (17%)
  other arithmetic  11.8 us (7%)
  local copies, waits for them, and re-layouts  4.16 us (2%)
    pallas_call x1, Pallas kernels, evolve(): pl.pallas_call(evolve_kernel, name='evolve', grid=(VARS,), in_specs=[smem...  68 us
    pallas_call x1, Pallas kernels, local_steps(): pl.pallas_call(local_kernel, name='local', in_specs=[smem, smem, smem, vm...  13.1 us
    ppermute x9, starting transfers between devices, ring_sum(): lax.ppermute(value, axes, [(i, (i + by) % 4) for i in range(4)])  12.2 us
    ppermute x7, starting transfers between devices, ring_shift(): return lambda value: lax.ppermute(value, ('grp_1', 'dev_1', 'dev_2'), pairs)  11.7 us
    ppermute x7, waiting for transfers between devices, ring_shift(): return lambda value: lax.ppermute(value, ('grp_1', 'dev_1', 'dev_2'), pairs)  11.2 us
    ppermute x9, waiting for transfers between devices, ring_sum(): lax.ppermute(value, axes, [(i, (i + by) % 4) for i in range(4)])  7.93 us
    ppermute x1, waiting for transfers between devices, communicate(): after_x = lax.ppermute(column, DEV, [(b, a) for a, b in up])  7.5 us
    ppermute x1, starting transfers between devices, communicate(): far = lax.ppermute(state[3:], GRP, [(2, 0), (1, 3)])  6.32 us
  transfers between devices with their start and end apart: 25, of which 14 were waited for; matrix products, arithmetic and copies ran while one was open for 6% of the time, Pallas kernels for 8%

profile of v5, /device:TPU:1, one launch (start us, length us, event | category | flops | bytes accessed | tf_op | source)
XLA Modules:
  0.0 174.2 jit_solution(15070632524314348537)
XLA Ops:
  1.6 6.3 %collective-permute-start.1 = (bf16[3,64,128]{2,1,0:T(8,128)(2,1)S(1)}, bf16[3,64,128]{2,1,0:T(8,128)(2,1)S(1)}, u32[]{:S(2)}, u32[]{:S(2)}) collective-permute-start(bf16[3,64,128]{2,1,0:T(8,128)(2,1)S(1)} %get-tuple-element.46), channel_id=1, source_target_pairs={{64,0},{32,96},{65,1},{33,97},{66,2},{34,98},{67,3},{35,99},{68,4}... | collective-permute-start | bytes 147464 | tf_op jit(solution)/shard_map/ppermute | solution.py:484
  7.9 2.0 %collective-permute-start = (bf16[3,64,128]{2,1,0:T(8,128)(2,1)S(1)}, bf16[3,64,128]{2,1,0:T(8,128)(2,1)S(1)}, u32[]{:S(2)}, u32[]{:S(2)}) collective-permute-start(bf16[3,64,128]{2,1,0:T(8,128)(2,1)S(1)} %get-tuple-element.47), channel_id=1, source_target_pairs={{64,32},{32,64},{65,33},{33,65},{66,34},{34,66},{67,35},{35,67},{6... | collective-permute-start | bytes 147464 | tf_op jit(solution)/shard_map/ppermute | solution.py:483
  12.6 2.3 %collective-permute-done = bf16[3,64,128]{2,1,0:T(8,128)(2,1)S(1)} collective-permute-done((bf16[3,64,128]{2,1,0:T(8,128)(2,1)S(1)}, bf16[3,64,128]{2,1,0:T(8,128)(2,1)S(1)}, u32[]{:S(2)}, u32[]{:S(2)}) %collective-permute-start) | collective-permute-done | bytes 49184 | tf_op jit(solution)/shard_map/ppermute | solution.py:483
  14.9 1.3 collective-permute-start.4
  16.2 3.4 %collective-permute-start.3 = (f32[6,8,8,128]{3,2,1,0:T(8,128)S(1)}, f32[6,8,8,128]{3,2,1,0:T(8,128)S(1)}, u32[]{:S(2)}, u32[]{:S(2)}) collective-permute-start(f32[6,8,8,128]{3,2,1,0:T(8,128)S(1)} %pad_maximum_fusion.5), channel_id=1, source_target_pairs={{32,64},{64,32},{33,65},{65,33},{34,66},{66,34},{35,67},{67,35},{3... | collective-permute-start | bytes 589832 | tf_op jit(solution)/shard_map/ppermute | solution.py:488
  19.8 2.8 %collective-permute-start.8 = (bf16[2,9,64,128]{3,2,1,0:T(8,128)(2,1)S(1)}, bf16[2,9,64,128]{3,2,1,0:T(8,128)(2,1)S(1)}, u32[]{:S(2)}, u32[]{:S(2)}) collective-permute-start(bf16[2,9,64,128]{3,2,1,0:T(8,128)(2,1)S(1)} %get-tuple-element.45), channel_id=1, source_target_pairs={{0,8},{1,9},{2,10},{3,11},{4,12},{5,13},{6,14},{7,15},{8,0},{9,1},... | collective-permute-start | bytes 884744 | tf_op jit(solution)/shard_map/ppermute | solution.py:343
  24.0 0.9 collective-permute-done.3
  25.1 1.3 collective-permute-start.6
  26.4 4.8 %collective-permute-start.5 = (f32[6,8,24,128]{3,2,1,0:T(8,128)S(1)}, f32[6,8,24,128]{3,2,1,0:T(8,128)}, u32[]{:S(2)}, u32[]{:S(2)}) collective-permute-start(f32[6,8,24,128]{3,2,1,0:T(8,128)S(1)} %pad_maximum_fusion.3), channel_id=1, source_target_pairs={{0,1},{1,2},{2,3},{3,4},{4,5},{5,6},{6,7},{7,8},{8,9},{9,10},{10,1... | collective-permute-start | bytes 1769480 | tf_op jit(solution)/shard_map/ppermute | solution.py:500
  31.2 1.2 fusion.31
  32.4 2.9 %collective-permute-start.11 = (bf16[4,2,9,64,128]{4,3,2,1,0:T(8,128)(2,1)}, bf16[4,2,9,64,128]{4,3,2,1,0:T(8,128)(2,1)S(1)}, u32[]{:S(2)}, u32[]{:S(2)}) collective-permute-start(bf16[4,2,9,64,128]{4,3,2,1,0:T(8,128)(2,1)} %get-tuple-element.41), channel_id=1, source_target_pairs={{0,3},{1,0},{2,1},{3,2},{4,7},{5,4},{6,5},{7,6},{8,11},{9,8},{10,9... | collective-permute-start | bytes 3538952 | tf_op jit(solution)/shard_map/ppermute | solution.py:343
  35.5 7.5 %collective-permute-done.6 = f32[6,8,24,128]{3,2,1,0:T(8,128)} collective-permute-done((f32[6,8,24,128]{3,2,1,0:T(8,128)S(1)}, f32[6,8,24,128]{3,2,1,0:T(8,128)}, u32[]{:S(2)}, u32[]{:S(2)}) %collective-permute-start.6) | collective-permute-done | bytes 589856 | tf_op jit(solution)/shard_map/ppermute | solution.py:501
  43.0 1.4 pad_maximum_fusion.1.fields
  44.4 13.1 %local.1 = (f32[5,8,8,128]{3,2,1,0:T(8,128)}, f32[36,8,128]{2,1,0:T(8,128)S(1)}) custom-call(s32[4]{0:T(128)S(1)} %pad_add_fusion.ints, f32[15]{0:T(128)S(1)} %reshape.520.speeds, f32[5]{0:T(128)S(1)} %copy-done.1, f32[6,24,24,128]{3,2,1,0:T(8,128)S(1)} %pad_maximum_fusion.1.fields), custom_call_target="tpu_custom_call" | custom-call | flops 4000000000 | bytes 6000000 | tf_op jit(solution)/shard_map/local/pallas_call | solution.py:440
  57.9 6.6 %collective-permute-done.10 = bf16[4,2,9,64,128]{4,3,2,1,0:T(8,128)(2,1)} collective-permute-done((bf16[4,2,9,64,128]{4,3,2,1,0:T(8,128)(2,1)}, bf16[4,2,9,64,128]{4,3,2,1,0:T(8,128)(2,1)}, u32[]{:S(2)}, u32[]{:S(2)}) %collective-permute-start.10) | collective-permute-done | bytes 1179680 | tf_op jit(solution)/shard_map/ppermute | solution.py:343
  64.5 1.1 slice.35
  65.7 4.6 %collective-permute-start.13 = (bf16[2,2,9,64,128]{4,3,2,1,0:T(8,128)(2,1)S(1)}, bf16[2,2,9,64,128]{4,3,2,1,0:T(8,128)(2,1)S(1)}, u32[]{:S(2)}, u32[]{:S(2)}) collective-permute-start(bf16[2,2,9,64,128]{4,3,2,1,0:T(8,128)(2,1)S(1)} %slice.36), channel_id=1, source_target_pairs={{0,3},{1,0},{2,1},{3,2},{4,7},{5,4},{6,5},{7,6},{8,11},{9,8},{10,9... | collective-permute-start | bytes 1769480 | tf_op jit(solution)/shard_map/ppermute | solution.py:343
  70.2 1.1 collective-permute-start.16
  72.9 2.4 %collective-permute-done.15 = f32[36]{0:T(128)S(1)} collective-permute-done((f32[36]{0:T(128)S(1)}, f32[36]{0:T(128)S(1)}, u32[]{:S(2)}, u32[]{:S(2)}) %collective-permute-start.15) | collective-permute-done | bytes 176 | tf_op jit(solution)/shard_map/ppermute | solution.py:475
  75.6 1.4 collective-permute-done.13
  77.1 3.1 %collective-permute-done.12 = bf16[2,2,9,64,128]{4,3,2,1,0:T(8,128)(2,1)S(1)} collective-permute-done((bf16[2,2,9,64,128]{4,3,2,1,0:T(8,128)(2,1)S(1)}, bf16[2,2,9,64,128]{4,3,2,1,0:T(8,128)(2,1)S(1)}, u32[]{:S(2)}, u32[]{:S(2)}) %collective-permute-start.12) | collective-permute-done | bytes 589856 | tf_op jit(solution)/shard_map/ppermute | solution.py:343
  80.3 3.5 %pad_maximum_fusion = bf16[4,4,2,9,64,128]{5,4,3,2,1,0:T(8,128)(2,1)} fusion(bf16[1,4,2,9,64,128]{5,4,3,2,1,0:T(8,128)(2,1)} %bitcast.34, bf16[1,4,2,9,64,128]{5,4,3,2,1,0:T(8,128)(2,1)S(1)} %maximum_bitcast_fusion, bf16[1,4,2,9,64,128]{5,4,3,2,1,0:T(8,128)(2,1)S(1)} %bitcast.93, bf16[1,4,2,9,64,128]{5,4,3,2,1,0:T(8,128)(2,1)S(1)} %get-tuple-element.40), kind=kLoop, calls=%fused_computation.1 | loop fusion | flops 7077888 | bytes 9437184 | tf_op jit(solution)/shard_map/stack | solution.py:514
  84.7 3.7 %collective-permute-start.19 = (f32[36]{0:T(128)S(1)}, f32[36]{0:T(128)S(1)}, u32[]{:S(2)}, u32[]{:S(2)}) collective-permute-start(f32[36]{0:T(128)S(1)} %add_add_fusion.2), channel_id=1, source_target_pairs={{0,12},{4,0},{8,4},{12,8},{1,13},{5,1},{9,5},{13,9},{2,14},{6,2},{... | collective-permute-start | bytes 440 | tf_op jit(solution)/shard_map/ppermute | solution.py:475
  88.4 1.3 collective-permute-start.17
  89.7 2.4 %collective-permute-done.18 = f32[36]{0:T(128)S(1)} collective-permute-done((f32[36]{0:T(128)S(1)}, f32[36]{0:T(128)S(1)}, u32[]{:S(2)}, u32[]{:S(2)}) %collective-permute-start.18) | collective-permute-done | bytes 176 | tf_op jit(solution)/shard_map/ppermute | solution.py:475
  92.4 2.4 %collective-permute-start.22 = (f32[36]{0:T(128)S(1)}, f32[36]{0:T(128)S(1)}, u32[]{:S(2)}, u32[]{:S(2)}) collective-permute-start(f32[36]{0:T(128)S(1)} %add_add_fusion.1), channel_id=1, source_target_pairs={{0,80},{16,0},{64,16},{80,64},{1,81},{17,1},{65,17},{81,65},{2,82}... | collective-permute-start | bytes 440 | tf_op jit(solution)/shard_map/ppermute | solution.py:475
  95.5 1.7 collective-permute-start.20
  97.2 1.2 collective-permute-done.21
  98.4 1.0 collective-permute-done.20
  99.4 3.1 %collective-permute-start.23 = (f32[36]{0:T(128)S(1)}, f32[36]{0:T(128)S(1)}, u32[]{:S(2)}, u32[]{:S(2)}) collective-permute-start(f32[36]{0:T(128)S(1)} %add_add_fusion), channel_id=1, source_target_pairs={{0,32},{32,0},{1,33},{33,1},{2,34},{34,2},{3,35},{35,3},{4,36},{36... | collective-permute-start | bytes 440 | tf_op jit(solution)/shard_map/ppermute | solution.py:347
  105.2 1.0 convert_element_type.49.matrix_ref
  106.3 68.0 %evolve.1 = bf16[8,5,16,128,128]{4,3,2,1,0:T(8,128)(2,1)} custom-call(s32[67]{0:T(128)} %concatenate.31.ints, f32[15]{0:T(128)} %copy-done, bf16[256,256]{1,0:T(8,128)(2,1)} %convert_element_type.49.matrix_ref, bf16[256,512]{1,0:T(8,128)(2,1)} %constant.120.clone.shift_ref, bf16[32,9,64,128]{3,2,1,0:T(8,128)(2,1)} %bitcast.35.nu_own.nu_third.q_own.q_ta, ...), custom_call_target="tpu_custom_call" | custom-call | flops 399999991808 | bytes 40000000 | tf_op jit(solution)/shard_map/evolve/pallas_call | solution.py:305
  (83 shorter events, 12.5 us)
Async XLA Ops:
  1.6 11.0 %collective-permute-start.1 = (bf16[3,64,128]{2,1,0:T(8,128)(2,1)S(1)}, bf16[3,64,128]{2,1,0:T(8,128)(2,1)S(1)}, u32[]{:S(2)}, u32[]{:S(2)}) collective-permute-start(bf16[3,64,128]{2,1,0:T(8,128)(2,1)S(1)} %get-tuple-element.46), channel_id=1, source_target_pairs={{64,0},{32,96},{65,1},{33,97},{66,2},{34,98},{67,3},{35,99},{68,4}... | collective-permute-start | bytes 147464 | tf_op jit(solution)/shard_map/ppermute | solution.py:484
  7.9 7.0 %collective-permute-start = (bf16[3,64,128]{2,1,0:T(8,128)(2,1)S(1)}, bf16[3,64,128]{2,1,0:T(8,128)(2,1)S(1)}, u32[]{:S(2)}, u32[]{:S(2)}) collective-permute-start(bf16[3,64,128]{2,1,0:T(8,128)(2,1)S(1)} %get-tuple-element.47), channel_id=1, source_target_pairs={{64,32},{32,64},{65,33},{33,65},{66,34},{34,66},{67,35},{35,67},{6... | collective-permute-start | bytes 147464 | tf_op jit(solution)/shard_map/ppermute | solution.py:483
  14.9 4.8 %collective-permute-start.4 = (bf16[9,64,128]{2,1,0:T(8,128)(2,1)S(1)}, bf16[9,64,128]{2,1,0:T(8,128)(2,1)S(1)}, u32[]{:S(2)}, u32[]{:S(2)}) collective-permute-start(bf16[9,64,128]{2,1,0:T(8,128)(2,1)S(1)} %pad_maximum_fusion.6), channel_id=1, source_target_pairs={{0,16},{16,0},{1,17},{17,1},{2,18},{18,2},{3,19},{19,3},{4,20},{20... | collective-permute-start | bytes 442376 | tf_op jit(solution)/shard_map/ppermute | solution.py:487
  16.2 8.8 %collective-permute-start.3 = (f32[6,8,8,128]{3,2,1,0:T(8,128)S(1)}, f32[6,8,8,128]{3,2,1,0:T(8,128)S(1)}, u32[]{:S(2)}, u32[]{:S(2)}) collective-permute-start(f32[6,8,8,128]{3,2,1,0:T(8,128)S(1)} %pad_maximum_fusion.5), channel_id=1, source_target_pairs={{32,64},{64,32},{33,65},{65,33},{34,66},{66,34},{35,67},{67,35},{3... | collective-permute-start | bytes 589832 | tf_op jit(solution)/shard_map/ppermute | solution.py:488
  19.6 5.4 %collective-permute-start.2 = (f32[6,8,8,128]{3,2,1,0:T(8,128)S(1)}, f32[6,8,8,128]{3,2,1,0:T(8,128)S(1)}, u32[]{:S(2)}, u32[]{:S(2)}) collective-permute-start(f32[6,8,8,128]{3,2,1,0:T(8,128)S(1)} %pad_maximum_fusion.5), channel_id=1, source_target_pairs={{0,32},{32,0},{1,33},{33,1},{2,34},{34,2},{3,35},{35,3},{4,36},{36... | collective-permute-start | bytes 589832 | tf_op jit(solution)/shard_map/ppermute | solution.py:347
  19.8 11.4 %collective-permute-start.8 = (bf16[2,9,64,128]{3,2,1,0:T(8,128)(2,1)S(1)}, bf16[2,9,64,128]{3,2,1,0:T(8,128)(2,1)S(1)}, u32[]{:S(2)}, u32[]{:S(2)}) collective-permute-start(bf16[2,9,64,128]{3,2,1,0:T(8,128)(2,1)S(1)} %get-tuple-element.45), channel_id=1, source_target_pairs={{0,8},{1,9},{2,10},{3,11},{4,12},{5,13},{6,14},{7,15},{8,0},{9,1},... | collective-permute-start | bytes 884744 | tf_op jit(solution)/shard_map/ppermute | solution.py:343
  22.6 8.6 %collective-permute-start.7 = (bf16[2,9,64,128]{3,2,1,0:T(8,128)(2,1)S(1)}, bf16[2,9,64,128]{3,2,1,0:T(8,128)(2,1)S(1)}, u32[]{:S(2)}, u32[]{:S(2)}) collective-permute-start(bf16[2,9,64,128]{3,2,1,0:T(8,128)(2,1)S(1)} %get-tuple-element.45), channel_id=1, source_target_pairs={{0,12},{1,13},{2,14},{3,15},{4,0},{5,1},{6,2},{7,3},{8,4},{9,5},{1... | collective-permute-start | bytes 884744 | tf_op jit(solution)/shard_map/ppermute | solution.py:343
  23.4 7.8 %collective-permute-start.9 = (bf16[2,9,64,128]{3,2,1,0:T(8,128)(2,1)S(1)}, bf16[2,9,64,128]{3,2,1,0:T(8,128)(2,1)S(1)}, u32[]{:S(2)}, u32[]{:S(2)}) collective-permute-start(bf16[2,9,64,128]{3,2,1,0:T(8,128)(2,1)S(1)} %get-tuple-element.45), channel_id=1, source_target_pairs={{0,4},{1,5},{2,6},{3,7},{4,8},{5,9},{6,10},{7,11},{8,12},{9,13},{1... | collective-permute-start | bytes 884744 | tf_op jit(solution)/shard_map/ppermute | solution.py:343
  25.1 18.0 %collective-permute-start.6 = (f32[6,8,24,128]{3,2,1,0:T(8,128)S(1)}, f32[6,8,24,128]{3,2,1,0:T(8,128)}, u32[]{:S(2)}, u32[]{:S(2)}) collective-permute-start(f32[6,8,24,128]{3,2,1,0:T(8,128)S(1)} %pad_maximum_fusion.3), channel_id=1, source_target_pairs={{1,0},{2,1},{3,2},{4,3},{5,4},{6,5},{7,6},{8,7},{9,8},{10,9},{11,1... | collective-permute-start | bytes 1769480 | tf_op jit(solution)/shard_map/ppermute | solution.py:501
  26.4 16.7 %collective-permute-start.5 = (f32[6,8,24,128]{3,2,1,0:T(8,128)S(1)}, f32[6,8,24,128]{3,2,1,0:T(8,128)}, u32[]{:S(2)}, u32[]{:S(2)}) collective-permute-start(f32[6,8,24,128]{3,2,1,0:T(8,128)S(1)} %pad_maximum_fusion.3), channel_id=1, source_target_pairs={{0,1},{1,2},{2,3},{3,4},{4,5},{5,6},{6,7},{7,8},{8,9},{9,10},{10,1... | collective-permute-start | bytes 1769480 | tf_op jit(solution)/shard_map/ppermute | solution.py:500
  31.2 4.1 %copy-start.3 = (f32[5,3]{0,1:T(4,128)S(1)}, f32[5,3]{0,1:T(4,128)}, u32[]{:S(2)}) copy-start(f32[5,3]{0,1:T(4,128)} %param.10) | copy-start | bytes 184
  32.4 25.4 %collective-permute-start.11 = (bf16[4,2,9,64,128]{4,3,2,1,0:T(8,128)(2,1)}, bf16[4,2,9,64,128]{4,3,2,1,0:T(8,128)(2,1)S(1)}, u32[]{:S(2)}, u32[]{:S(2)}) collective-permute-start(bf16[4,2,9,64,128]{4,3,2,1,0:T(8,128)(2,1)} %get-tuple-element.41), channel_id=1, source_target_pairs={{0,3},{1,0},{2,1},{3,2},{4,7},{5,4},{6,5},{7,6},{8,11},{9,8},{10,9... | collective-permute-start | bytes 3538952 | tf_op jit(solution)/shard_map/ppermute | solution.py:343
  35.3 29.2 %collective-permute-start.10 = (bf16[4,2,9,64,128]{4,3,2,1,0:T(8,128)(2,1)}, bf16[4,2,9,64,128]{4,3,2,1,0:T(8,128)(2,1)}, u32[]{:S(2)}, u32[]{:S(2)}) collective-permute-start(bf16[4,2,9,64,128]{4,3,2,1,0:T(8,128)(2,1)} %get-tuple-element.41), channel_id=1, source_target_pairs={{0,1},{1,2},{2,3},{3,0},{4,5},{5,6},{6,7},{7,4},{8,9},{9,10},{10,1... | collective-permute-start | bytes 3538952 | tf_op jit(solution)/shard_map/ppermute | solution.py:343
  35.5 9.0 %copy-start = (f32[15]{0:T(128)}, f32[15]{0:T(128)S(1)}, u32[]{:S(2)}) copy-start(f32[15]{0:T(128)S(1)} %reshape.520.speeds) | copy-start | bytes 184
  35.5 8.9 %copy-start.1 = (f32[5]{0:T(128)S(1)}, f32[5]{0:T(128)}, u32[]{:S(2)}) copy-start(f32[5]{0:T(128)} %weights.1) | copy-start | bytes 64
  65.7 11.4 %collective-permute-start.13 = (bf16[2,2,9,64,128]{4,3,2,1,0:T(8,128)(2,1)S(1)}, bf16[2,2,9,64,128]{4,3,2,1,0:T(8,128)(2,1)S(1)}, u32[]{:S(2)}, u32[]{:S(2)}) collective-permute-start(bf16[2,2,9,64,128]{4,3,2,1,0:T(8,128)(2,1)S(1)} %slice.36), channel_id=1, source_target_pairs={{0,3},{1,0},{2,1},{3,2},{4,7},{5,4},{6,5},{7,6},{8,11},{9,8},{10,9... | collective-permute-start | bytes 1769480 | tf_op jit(solution)/shard_map/ppermute | solution.py:343
  70.2 9.9 %collective-permute-start.12 = (bf16[2,2,9,64,128]{4,3,2,1,0:T(8,128)(2,1)S(1)}, bf16[2,2,9,64,128]{4,3,2,1,0:T(8,128)(2,1)S(1)}, u32[]{:S(2)}, u32[]{:S(2)}) collective-permute-start(bf16[2,2,9,64,128]{4,3,2,1,0:T(8,128)(2,1)S(1)} %slice.35), channel_id=1, source_target_pairs={{0,1},{1,2},{2,3},{3,0},{4,5},{5,6},{6,7},{7,4},{8,9},{9,10},{10,1... | collective-permute-start | bytes 1769480 | tf_op jit(solution)/shard_map/ppermute | solution.py:343
  70.2 2.7 %collective-permute-start.16 = (f32[36]{0:T(128)S(1)}, f32[36]{0:T(128)S(1)}, u32[]{:S(2)}, u32[]{:S(2)}) collective-permute-start(f32[36]{0:T(128)S(1)} %broadcast_multiply_fusion), channel_id=1, source_target_pairs={{0,3},{1,0},{2,1},{3,2},{4,7},{5,4},{6,5},{7,6},{8,11},{9,8},{10,9... | collective-permute-start | bytes 440 | tf_op jit(solution)/shard_map/ppermute | solution.py:475
  71.4 3.9 %collective-permute-start.15 = (f32[36]{0:T(128)S(1)}, f32[36]{0:T(128)S(1)}, u32[]{:S(2)}, u32[]{:S(2)}) collective-permute-start(f32[36]{0:T(128)S(1)} %broadcast_multiply_fusion), channel_id=1, source_target_pairs={{0,1},{1,2},{2,3},{3,0},{4,5},{5,6},{6,7},{7,4},{8,9},{9,10},{10,1... | collective-permute-start | bytes 440 | tf_op jit(solution)/shard_map/ppermute | solution.py:475
  71.7 3.9 %collective-permute-start.14 = (f32[36]{0:T(128)S(1)}, f32[36]{0:T(128)S(1)}, u32[]{:S(2)}, u32[]{:S(2)}) collective-permute-start(f32[36]{0:T(128)S(1)} %broadcast_multiply_fusion), channel_id=1, source_target_pairs={{0,2},{1,3},{2,0},{3,1},{4,6},{5,7},{6,4},{7,5},{8,10},{9,11},{10,... | collective-permute-start | bytes 440 | tf_op jit(solution)/shard_map/ppermute | solution.py:475
  80.3 3.6 %copy-start.2 = (s32[2,6]{1,0:T(2,128)S(1)}, s32[2,6]{1,0:T(2,128)}, u32[]{:S(2)}) copy-start(s32[2,6]{1,0:T(2,128)} %param.12) | copy-start | bytes 148
  80.3 3.6 %copy-start.4 = (s32[2]{0:T(128)S(1)}, s32[2]{0:T(128)}, u32[]{:S(2)}) copy-start(s32[2]{0:T(128)} %param.13) | copy-start | bytes 28
  80.3 4.4 %copy-start.5 = (s32[64]{0:T(128)S(1)}, s32[64]{0:T(128)}, u32[]{:S(2)}) copy-start(s32[64]{0:T(128)} %constant.127) | copy-start | bytes 772
  83.8 22.4 %collective-permute-start.24 = (bf16[32,9,64,128]{3,2,1,0:T(8,128)(2,1)}, bf16[32,9,64,128]{3,2,1,0:T(8,128)(2,1)}, u32[]{:S(2)}, u32[]{:S(2)}) collective-permute-start(bf16[32,9,64,128]{3,2,1,0:T(8,128)(2,1)} %bitcast.35.nu_own.nu_third.q_own.q_ta), channel_id=1, source_target_pairs={{0,32},{32,0},{1,33},{33,1},{2,34},{34,2},{3,35},{35,3},{4,36},{36... | collective-permute-start | bytes 14155784 | tf_op jit(solution)/shard_map/ppermute | solution.py:347
  84.7 5.0 %collective-permute-start.19 = (f32[36]{0:T(128)S(1)}, f32[36]{0:T(128)S(1)}, u32[]{:S(2)}, u32[]{:S(2)}) collective-permute-start(f32[36]{0:T(128)S(1)} %add_add_fusion.2), channel_id=1, source_target_pairs={{0,12},{4,0},{8,4},{12,8},{1,13},{5,1},{9,5},{13,9},{2,14},{6,2},{... | collective-permute-start | bytes 440 | tf_op jit(solution)/shard_map/ppermute | solution.py:475
  88.4 3.6 %collective-permute-start.18 = (f32[36]{0:T(128)S(1)}, f32[36]{0:T(128)S(1)}, u32[]{:S(2)}, u32[]{:S(2)}) collective-permute-start(f32[36]{0:T(128)S(1)} %add_add_fusion.2), channel_id=1, source_target_pairs={{0,4},{4,8},{8,12},{12,0},{1,5},{5,9},{9,13},{13,1},{2,6},{6,10},{... | collective-permute-start | bytes 440 | tf_op jit(solution)/shard_map/ppermute | solution.py:475
  88.4 3.9 %collective-permute-start.17 = (f32[36]{0:T(128)S(1)}, f32[36]{0:T(128)S(1)}, u32[]{:S(2)}, u32[]{:S(2)}) collective-permute-start(f32[36]{0:T(128)S(1)} %add_add_fusion.2), channel_id=1, source_target_pairs={{0,8},{4,12},{8,0},{12,4},{1,9},{5,13},{9,1},{13,5},{2,10},{6,14},... | collective-permute-start | bytes 440 | tf_op jit(solution)/shard_map/ppermute | solution.py:475
  92.4 4.9 %collective-permute-start.22 = (f32[36]{0:T(128)S(1)}, f32[36]{0:T(128)S(1)}, u32[]{:S(2)}, u32[]{:S(2)}) collective-permute-start(f32[36]{0:T(128)S(1)} %add_add_fusion.1), channel_id=1, source_target_pairs={{0,80},{16,0},{64,16},{80,64},{1,81},{17,1},{65,17},{81,65},{2,82}... | collective-permute-start | bytes 440 | tf_op jit(solution)/shard_map/ppermute | solution.py:475
  94.8 3.6 %collective-permute-start.21 = (f32[36]{0:T(128)S(1)}, f32[36]{0:T(128)S(1)}, u32[]{:S(2)}, u32[]{:S(2)}) collective-permute-start(f32[36]{0:T(128)S(1)} %add_add_fusion.1), channel_id=1, source_target_pairs={{0,16},{16,64},{64,80},{80,0},{1,17},{17,65},{65,81},{81,1},{2,18}... | collective-permute-start | bytes 440 | tf_op jit(solution)/shard_map/ppermute | solution.py:475
  95.5 3.9 %collective-permute-start.20 = (f32[36]{0:T(128)S(1)}, f32[36]{0:T(128)S(1)}, u32[]{:S(2)}, u32[]{:S(2)}) collective-permute-start(f32[36]{0:T(128)S(1)} %add_add_fusion.1), channel_id=1, source_target_pairs={{0,64},{16,80},{64,0},{80,16},{1,65},{17,81},{65,1},{81,17},{2,66}... | collective-permute-start | bytes 440 | tf_op jit(solution)/shard_map/ppermute | solution.py:475
  99.4 4.0 %collective-permute-start.23 = (f32[36]{0:T(128)S(1)}, f32[36]{0:T(128)S(1)}, u32[]{:S(2)}, u32[]{:S(2)}) collective-permute-start(f32[36]{0:T(128)S(1)} %add_add_fusion), channel_id=1, source_target_pairs={{0,32},{32,0},{1,33},{33,1},{2,34},{34,2},{3,35},{35,3},{4,36},{36... | collective-permute-start | bytes 440 | tf_op jit(solution)/shard_map/ppermute | solution.py:347
